TPU v7x, 256 devices: a whole 4x4x8 slice. The times are simulated.
256 devices in a mesh: dp: 32 (over x, z), seq: 8 (over y, core).
Axes of the slice: x: 4, y: 4, z: 8, core: 2. Of those that a mesh axis runs over, the one named last changes fastest.
Arguments:
- span_store: bfloat16 [32, 512, 8192], P('dp', 'seq'), may hold values from -6 to 6
- target: int32 [32, 512], P('dp', 'seq'), may hold values from 0 to 31, as said below
- segment_ids: int32 [32, 512], P('dp'), may hold values from 0 to 7, never falling along the last dimension, each value on 1 to 128 neighbouring positions
- norm_gain: float32 [8192], replicated, may hold values from 0.25 to 1.75
- w_query: bfloat16 [8192, 4096], P('dp', 'seq'), may hold values from -0.0625 to 0.0625
- key_weight: bfloat16 [8192, 1024], P('dp', 'seq'), may hold values from -0.0625 to 0.0625
- value_weight: bfloat16 [8192, 1024], P('dp', 'seq'), may hold values from -0.0625 to 0.0625
Outputs:
- context: bfloat16 [32, 512, 4096], P('dp', 'seq')
Inputs may be any that keep to these rules, and one draw needn't show every extreme that they name: `target`: within one lane, the stored tokens of all shards that name one packed row number exactly 64; one shard's tokens of one lane name one row at most 3 times, and exactly 3 times for some shard and row in every lane. `segment_ids`: along a row, document ids never fall.
All inputs are finite; a program needn't handle non-finite values.
Results may differ from a plain program's by a relative error of at most 0.0079.
Values may be sent and summed in bfloat16 or wider, within the bound.
No kernel may reach another device: no remote copies, remote signals or barrier semaphores. Data moves between devices by JAX's collectives and lax.ppermute only.
A program may use at most 128 MiB of HBM per device.

v0:
```python
import jax
import jax.numpy as jnp
from jax import lax
from jax.experimental import pallas as pl
from jax.experimental.pallas import tpu as pltpu
from jax.sharding import PartitionSpec as P

HEAD = 128
EPS = 1e-05
ROPE_BASE = 500000.0
NX, NZ = 4, 8
ND = NX * NZ
LANES = 8
LANE = 64
CAP = 3
SLOTS = LANES * CAP
KB = 256
BLOCK = 128
EMPTY = 2.0**100
SELF = 128
DZ = (0, 1, 7, 2, 6, 3, 5, 4)

VMEM = pl.BlockSpec(memory_space=pltpu.VMEM)
SMEM = pl.BlockSpec(memory_space=pltpu.SMEM)
ANYWHERE = pl.BlockSpec(memory_space=pl.ANY)


def from_z(value, k):
    pairs = [(x * NZ + (z + k) % NZ, x * NZ + z) for x in range(NX) for z in range(NZ)]
    return lax.ppermute(value, "dp", pairs)


def from_x(value, k):
    pairs = [(((x + k) % NX) * NZ + z, x * NZ + z) for x in range(NX) for z in range(NZ)]
    return lax.ppermute(value, "dp", pairs)


def after(values, *done):
    return lax.optimization_barrier((values, done))[0]


def normalize_kernel(x_ref, gain_ref, target_ref, out_ref):
    dp = lax.axis_index("dp")
    x_at, z_at = dp // NZ, dp % NZ
    rows = x_ref.shape[0]
    values = x_ref[...].astype(jnp.float32)
    inverse = lax.rsqrt(jnp.mean(values * values, axis=-1, keepdims=True) + EPS)
    for b in range(ND):
        dx, dz = b // NZ, DZ[b % NZ]
        start = pl.multiple_of((((x_at + dx) % NX) * NZ + (z_at + dz) % NZ) * KB, KB)
        piece = x_ref[:, pl.ds(start, KB)].astype(jnp.float32)
        gain = gain_ref[:, pl.ds(start, KB)]
        out_ref[:, b * KB : (b + 1) * KB] = (piece * inverse * gain).astype(jnp.bfloat16)
    own = lax.broadcasted_iota(jnp.int32, (rows, rows), 0) == lax.broadcasted_iota(jnp.int32, (rows, rows), 1)
    goal = jnp.sum(jnp.where(own, target_ref[...].astype(jnp.float32), 0.0), axis=1, keepdims=True)
    tail = out_ref.shape[1] - ND * KB
    out_ref[:, ND * KB :] = jnp.broadcast_to(goal, (rows, tail)).astype(jnp.bfloat16)


def normalize(stored, norm_gain, target):
    rows, width = stored.shape
    return pl.pallas_call(
        normalize_kernel,
        out_shape=jax.ShapeDtypeStruct((rows, width + HEAD), jnp.bfloat16),
        in_specs=[VMEM, VMEM, VMEM],
        out_specs=VMEM,
    )(stored, norm_gain[None, :], target)


def join_kernel(columns, *refs):
    out_ref, at = refs[-1], 0
    for ref in refs[:-1]:
        out_ref[at : at + ref.shape[0], :] = ref[:, columns:]
        at += ref.shape[0]


def join(*parts, columns=0):
    rows = sum(p.shape[0] for p in parts)
    return pl.pallas_call(
        lambda *refs: join_kernel(columns, *refs),
        out_shape=jax.ShapeDtypeStruct((rows, parts[0].shape[1] - columns), parts[0].dtype),
        in_specs=[VMEM] * len(parts),
        out_specs=VMEM,
    )(*parts)


def part_dots(tokens, pieces):
    return sum(
        jnp.dot(tokens[:, at * KB : at * KB + w.shape[0]], w, preferred_element_type=jnp.float32)
        for w, at in pieces
    )


def project(tokens, query, key_value):
    cols = query.shape[1]
    zp1, zm1 = from_z(query, 1), from_z(query, -1)
    own = jnp.concatenate([query, key_value], axis=1)
    op, om = from_x(own, 1), from_x(own, -1)
    o2 = from_x(op, 1)
    near = after(join(zp1, zm1), op, om)
    n1, n3 = from_x(near, 1), from_x(near, -1)
    zp2, zm2 = from_z(zp1, 1), from_z(zm1, -1)
    a, b = after((zp2, zm2), zp2, zm2)
    zp3, zm3 = from_z(a, 1), from_z(b, -1)
    z4 = from_z(after(zp3, zm3), 1)
    row = after(join(own, op, o2, om, columns=cols), z4)
    rp1, rm1 = from_z(row, 1), from_z(row, -1)
    n2 = from_x(after(n3, n1), -1)
    far = after(join(zp2, zm2, zp3, zm3, z4), n1, n3, row, tokens)
    f1, f3 = from_x(far, 1), from_x(far, -1)
    early = [(query, 0), (near, 1), (op[:, :cols], 8), (n1, 9), (o2[:, :cols], 16), (om[:, :cols], 24), (n3, 25)]
    q_sum = part_dots(tokens, early)
    a, b = after((rp1, rm1), rp1, rm1, n1, n3, tokens)
    rp2, rm2 = from_z(a, 1), from_z(b, -1)
    q_sum = q_sum + part_dots(tokens, [(far, 3)])
    a, b = after((rp2, rm2), rp2, rm2)
    rp3, rm3 = from_z(a, 1), from_z(b, -1)
    f1, f3 = after((f1, f3), q_sum)
    g = far.shape[0] // 2
    f2 = [from_x(f1[:g], 1), from_x(f3[g:], -1)]
    kv_sum = kv_early(tokens, [row, rp1, rm1, rp2, rm2])
    q_sum = q_sum + part_dots(tokens, [(f1, 11), (f3, 27)])
    h = row.shape[0] // 2
    a, b = after((rp3[:h], rm3[h:]), kv_sum, q_sum)
    ends = [from_z(a, 1), from_z(b, -1)]
    q_sum = q_sum + part_dots(tokens, [(n2, 17)])
    return q_sum, kv_sum, f2, [rp3, rm3, *ends]


def kv_early_kernel(tok_ref, *refs):
    out_ref = refs[-1]
    out_ref[...] = jnp.zeros_like(out_ref)

    def step(dx, carry):
        total = jnp.zeros(out_ref.shape, jnp.float32)
        rows = pl.ds(pl.multiple_of(dx * KB, KB), KB)
        for dz, ref in enumerate(refs[:-1]):
            at = pl.multiple_of((dx * NZ + dz) * KB, KB)
            total += jnp.dot(tok_ref[:, pl.ds(at, KB)], ref[rows, :], preferred_element_type=jnp.float32)
        out_ref[...] += total
        return carry

    lax.fori_loop(0, NX, step, 0)


def kv_early(tokens, blocks):
    return pl.pallas_call(
        kv_early_kernel,
        out_shape=jax.ShapeDtypeStruct((tokens.shape[0], blocks[0].shape[1]), jnp.float32),
        in_specs=[VMEM] * (1 + len(blocks)),
        out_specs=VMEM,
        compiler_params=pltpu.CompilerParams(vmem_limit_bytes=10 << 20),
    )(tokens, *blocks)


def finish_kernel(tok_ref, slot_ref, q_ref, kv_ref, f2a, f2b, rp3, rm3, ends0, ends1, out_ref, all_ref):
    tokens = tok_ref.shape[0]
    q_cols, kv_cols = q_ref.shape[1], kv_ref.shape[1]

    def dot(at, ref, low):
        return jnp.dot(
            tok_ref[:, at * KB : (at + 1) * KB], ref[low * KB : (low + 1) * KB, :], preferred_element_type=jnp.float32
        )

    kv = kv_ref[...]
    for dx in range(NX):
        end = ends0 if dx < 2 else ends1
        kv += dot(dx * NZ + 5, rp3, dx) + dot(dx * NZ + 6, rm3, dx) + dot(dx * NZ + 7, end, dx % 2)
    all_ref[:, q_cols:] = kv.astype(jnp.bfloat16)
    q, at = q_ref[...], 19 * KB
    for ref in (f2a, f2b):
        q += jnp.dot(tok_ref[:, at : at + ref.shape[0]], ref[...], preferred_element_type=jnp.float32)
        at += ref.shape[0]
    all_ref[:, :q_cols] = q.astype(jnp.bfloat16)

    def step(i, carry):
        low = pl.multiple_of(i * BLOCK, BLOCK)
        rows = low + lax.broadcasted_iota(jnp.int32, (BLOCK, tokens), 0)
        send = (rows == slot_ref[...]).astype(jnp.bfloat16)
        used = jnp.dot(send, jnp.ones((tokens, HEAD), jnp.bfloat16), preferred_element_type=jnp.float32) > 0.5
        moved = jnp.dot(send, all_ref[...], preferred_element_type=jnp.float32)
        for c in range(0, q_cols + kv_cols, HEAD):
            part = jnp.where(used, moved[:, c : c + HEAD], EMPTY)
            out_ref[pl.ds(low, BLOCK), c : c + HEAD] = part.astype(jnp.bfloat16)
        return carry

    lax.fori_loop(0, out_ref.shape[0] // BLOCK, step, 0)


def finish(tokens, slot, q_sum, kv_sum, q_late, kv_late):
    rows = tokens.shape[0]
    columns = q_sum.shape[1] + kv_sum.shape[1]
    return pl.pallas_call(
        finish_kernel,
        out_shape=jax.ShapeDtypeStruct((ND * SLOTS, columns), jnp.bfloat16),
        in_specs=[VMEM] * (4 + len(q_late) + len(kv_late)),
        out_specs=VMEM,
        scratch_shapes=[pltpu.VMEM((rows, columns), jnp.bfloat16)],
        compiler_params=pltpu.CompilerParams(vmem_limit_bytes=10 << 20),
    )(tokens, slot[None, :], q_sum, kv_sum, *q_late, *kv_late)


def attention_kernel(arr_ref, ahead_ref, segq_ref, segk_ref, cos_ref, sin_ref, out_ref, key_ref, value_ref):
    length = out_ref.shape[0]
    arrived = arr_ref.shape[0]
    valid = (arr_ref[:, :HEAD].astype(jnp.float32) < EMPTY / 2).astype(jnp.bfloat16)
    found = lax.dot_general(
        valid, ahead_ref[...], (((0,), (0,)), ((), ())), preferred_element_type=jnp.float32
    )[:1].astype(jnp.int32)
    lane = (lax.broadcasted_iota(jnp.int32, (1, arrived), 1) % SLOTS) // CAP
    place = jnp.where(found >= SELF, lane * LANE + found - SELF, -1)
    key_ref[:BLOCK, :] = jnp.zeros((BLOCK, HEAD), jnp.bfloat16)
    value_ref[:BLOCK, :] = jnp.zeros((BLOCK, HEAD), jnp.bfloat16)

    def step(b, carry):
        at = pl.multiple_of(b * BLOCK, BLOCK)
        block, window = pl.ds(at, BLOCK), pl.ds(at, 2 * BLOCK)
        new = pl.ds(pl.multiple_of(at + BLOCK, BLOCK), BLOCK)
        rows = at + lax.broadcasted_iota(jnp.int32, (BLOCK, arrived), 0)
        pick = (rows == place).astype(jnp.bfloat16)
        packed = jnp.dot(pick, arr_ref[...], preferred_element_type=jnp.float32)
        cosine, sine = cos_ref[block, :], sin_ref[block, :]

        def turn(u):
            return (u * cosine + pltpu.roll(u, HEAD // 2, 1) * sine).astype(jnp.bfloat16)

        key_ref[new, :] = turn(packed[:, 4 * HEAD : 5 * HEAD])
        value_ref[new, :] = packed[:, 5 * HEAD : 6 * HEAD].astype(jnp.bfloat16)
        keys, values = key_ref[window, :], value_ref[window, :]
        tpos = BLOCK + lax.broadcasted_iota(jnp.int32, (BLOCK, 2 * BLOCK), 0)
        upos = lax.broadcasted_iota(jnp.int32, (BLOCK, 2 * BLOCK), 1)
        allowed = (segq_ref[block, :] == segk_ref[:, window]) & (upos <= tpos)
        for h in range(4):
            q = turn(packed[:, h * HEAD : (h + 1) * HEAD])
            score = lax.dot_general(q, keys, (((1,), (1,)), ((), ())), preferred_element_type=jnp.float32)
            terms = jnp.where(allowed, jnp.exp(score * (HEAD ** -0.5)), 0.0)
            total = jnp.sum(terms, axis=-1, keepdims=True)
            weights = (terms / total).astype(jnp.bfloat16)
            context = jnp.dot(weights, values, preferred_element_type=jnp.float32)
            out_ref[block, h * HEAD : (h + 1) * HEAD] = context.astype(jnp.bfloat16)
        return carry

    lax.fori_loop(0, length // BLOCK, step, 0)


def attention(arrived, seg, cosine, sine):
    length = seg.shape[0]
    count = arrived.shape[0]
    col = jnp.arange(count, dtype=jnp.int32)
    lane = (col % SLOTS) // CAP
    ahead = ((lane[:, None] == lane[None, :]) & (col[:, None] < col[None, :])).astype(jnp.bfloat16)
    ahead = jnp.where(col[:, None] == col[None, :], float(SELF), ahead).astype(jnp.bfloat16)
    padded = jnp.concatenate([jnp.full((BLOCK,), -1, jnp.int32), seg])
    return pl.pallas_call(
        attention_kernel,
        out_shape=jax.ShapeDtypeStruct((length, 4 * HEAD), jnp.bfloat16),
        in_specs=[VMEM] * 6,
        out_specs=VMEM,
        scratch_shapes=[
            pltpu.VMEM((BLOCK + length, HEAD), jnp.bfloat16),
            pltpu.VMEM((BLOCK + length, HEAD), jnp.bfloat16),
        ],
        compiler_params=pltpu.CompilerParams(vmem_limit_bytes=10 << 20),
    )(arrived, ahead, seg[:, None], padded[None, :], cosine, sine)


def rotary_tables(length):
    half = HEAD // 2
    frequency = ROPE_BASE ** (-(jnp.arange(half, dtype=jnp.float32) * (2.0 / HEAD)))
    angles = jnp.arange(length, dtype=jnp.float32)[:, None] * frequency[None, :]
    c, s = jnp.cos(angles), jnp.sin(angles)
    return jnp.concatenate([c, c], axis=-1), jnp.concatenate([-s, s], axis=-1)


def slots_of(target):
    lanes = target.reshape(LANES, LANE)
    same = lanes[:, :, None] == lanes[:, None, :]
    before = jnp.arange(LANE)[None, :] < jnp.arange(LANE)[:, None]
    rank = jnp.sum((same & before[None]).astype(jnp.int32), axis=2)
    return (lanes * SLOTS + jnp.arange(LANES, dtype=jnp.int32)[:, None] * CAP + rank).reshape(-1)


def shards(span_store, target, segment_ids, norm_gain, w_query, key_weight, value_weight):
    normed = normalize(span_store[0], norm_gain, target)
    tokens = lax.all_gather(normed, "seq", axis=0, tiled=True)
    slot = slots_of(tokens[:, ND * KB].astype(jnp.int32))

    key_value = jnp.concatenate([key_weight, value_weight], axis=1)
    outgoing = finish(tokens, slot, *project(tokens, w_query, key_value))
    arrived = lax.all_to_all(
        outgoing.reshape(ND, SLOTS, -1), "dp", split_axis=0, concat_axis=0, tiled=True
    ).reshape(ND * SLOTS, -1)

    seg = segment_ids[0]
    cosine, sine = rotary_tables(seg.shape[0])
    context = attention(arrived, seg, cosine, sine)
    returned = lax.all_to_all(context, "seq", split_axis=0, concat_axis=1, tiled=True)
    return returned[None]


def solution(mesh):
    placed = (
        P("dp", "seq", None),
        P("dp", "seq"),
        P("dp", None),
        P(),
        P("dp", "seq"),
        P("dp", "seq"),
        P("dp", "seq"),
    )
    return jax.shard_map(
        shards, mesh=mesh, in_specs=placed, out_specs=P("dp", "seq", None), check_vma=False
    )
```

profile of v0, /device:TPU:1, one launch (start us, length us, event | category | flops | bytes accessed | tf_op | source)
XLA Modules:
  0.0 192.8 jit_solution(1626963307945326979)
XLA Ops:
  6.5 2.8 %shard_map.73 = bf16[64,8320]{1,0:T(8,128)(2,1)} custom-call(bf16[64,8192]{1,0:T(8,128)(2,1)} %bitcast.20, f32[1,8192]{1,0:T(1,128)} %bitcast.21, s32[1,64]{1,0:T(1,128)} %target_ref.1), custom_call_target="tpu_custom_call" | custom-call | tf_op jit(solution)/shard_map/pallas_call | solution.py:62
  9.4 6.5 %collective-permute-start = (bf16[256,512]{1,0:T(8,128)(2,1)S(1)}, bf16[256,512]{1,0:T(8,128)(2,1)S(1)}, u32[]{:S(2)}, u32[]{:S(2)}) collective-permute-start(bf16[256,512]{1,0:T(8,128)(2,1)S(1)} %copy-done.10), channel_id=1, source_target_pairs={{8,0},{16,8},{24,16},{32,24},{40,32},{48,40},{56,48},{0,56},{72,64... | collective-permute-start | bytes 786440 | tf_op jit(solution)/shard_map/ppermute | solution.py:30
  15.9 4.9 %collective-permute-done.refs_0_ = bf16[256,512]{1,0:T(8,128)(2,1)S(1)} collective-permute-done((bf16[256,512]{1,0:T(8,128)(2,1)S(1)}, bf16[256,512]{1,0:T(8,128)(2,1)S(1)}, u32[]{:S(2)}, u32[]{:S(2)}) %collective-permute-start) | collective-permute-done | bytes 262176 | tf_op jit(solution)/shard_map/ppermute | solution.py:30
  20.8 3.4 %collective-permute-start.7 = (bf16[256,512]{1,0:T(8,128)(2,1)S(1)}, bf16[256,512]{1,0:T(8,128)(2,1)S(1)}, u32[]{:S(2)}, u32[]{:S(2)}) collective-permute-start(bf16[256,512]{1,0:T(8,128)(2,1)S(1)} %collective-permute-done.refs_0_), channel_id=1, source_target_pairs={{8,0},{16,8},{24,16},{32,24},{40,32},{48,40},{56,48},{0,56},{72,64... | collective-permute-start | bytes 786440 | tf_op jit(solution)/shard_map/ppermute | solution.py:30
  24.3 2.6 %collective-permute-start.2 = (bf16[256,768]{1,0:T(8,128)(2,1)S(1)}, bf16[256,768]{1,0:T(8,128)(2,1)S(1)}, u32[]{:S(2)}, u32[]{:S(2)}) collective-permute-start(bf16[256,768]{1,0:T(8,128)(2,1)S(1)} %constant_dynamic-update-slice_fusion.refs_0_), channel_id=1, source_target_pairs={{64,0},{72,8},{80,16},{88,24},{96,32},{104,40},{112,48},{120,56},{... | collective-permute-start | bytes 1179656 | tf_op jit(solution)/shard_map/ppermute | solution.py:35
  26.8 1.4 collective-permute-done.7.refs_0_
  28.3 3.2 %collective-permute-done.8.refs_1_ = bf16[256,512]{1,0:T(8,128)(2,1)S(1)} collective-permute-done((bf16[256,512]{1,0:T(8,128)(2,1)S(1)}, bf16[256,512]{1,0:T(8,128)(2,1)S(1)}, u32[]{:S(2)}, u32[]{:S(2)}) %collective-permute-start.8) | collective-permute-done | bytes 262176 | tf_op jit(solution)/shard_map/ppermute | solution.py:30
  31.5 2.7 %collective-permute-start.9 = (bf16[256,512]{1,0:T(8,128)(2,1)S(1)}, bf16[256,512]{1,0:T(8,128)(2,1)S(1)}, u32[]{:S(2)}, u32[]{:S(2)}) collective-permute-start(bf16[256,512]{1,0:T(8,128)(2,1)S(1)} %collective-permute-done.7.refs_0_), channel_id=1, source_target_pairs={{8,0},{16,8},{24,16},{32,24},{40,32},{48,40},{56,48},{0,56},{72,64... | collective-permute-start | bytes 786440 | tf_op jit(solution)/shard_map/ppermute | solution.py:30
  34.2 1.2 collective-permute-start.3
  35.4 1.5 collective-permute-start.5
  36.9 1.4 collective-permute-done.10.refs_3_
  38.4 2.7 %collective-permute-start.11 = (bf16[256,512]{1,0:T(8,128)(2,1)S(1)}, bf16[256,512]{1,0:T(8,128)(2,1)S(1)}, u32[]{:S(2)}, u32[]{:S(2)}) collective-permute-start(bf16[256,512]{1,0:T(8,128)(2,1)S(1)} %collective-permute-done.9.refs_2_), channel_id=1, source_target_pairs={{8,0},{16,8},{24,16},{32,24},{40,32},{48,40},{56,48},{0,56},{72,64... | collective-permute-start | bytes 786440 | tf_op jit(solution)/shard_map/ppermute | solution.py:30
  41.0 1.9 shard_map.74
  42.9 2.5 %collective-permute-start.4 = (bf16[512,512]{1,0:T(8,128)(2,1)}, bf16[512,512]{1,0:T(8,128)(2,1)S(1)}, u32[]{:S(2)}, u32[]{:S(2)}) collective-permute-start(bf16[512,512]{1,0:T(8,128)(2,1)} %shard_map.74), channel_id=1, source_target_pairs={{64,0},{72,8},{80,16},{88,24},{96,32},{104,40},{112,48},{120,56},{... | collective-permute-start | bytes 1572872 | tf_op jit(solution)/shard_map/ppermute | solution.py:35
  45.4 0.7 copy-done.3
  46.2 2.2 %shard_map.76.refs_0_ = bf16[1024,256]{1,0:T(8,128)(2,1)} custom-call(bf16[256,768]{1,0:T(8,128)(2,1)} %copy-done.5, bf16[256,768]{1,0:T(8,128)(2,1)} %copy-done.6, bf16[256,768]{1,0:T(8,128)(2,1)} %copy-done.3, bf16[256,768]{1,0:T(8,128)(2,1)} %copy-done.8), custom_call_target="tpu_custom_call" | custom-call | tf_op jit(solution)/shard_map/pallas_call | solution.py:79
  48.3 0.1 collective-permute-start.15
  48.5 1.4 collective-permute-start.16
  49.9 0.6 add.83
  50.5 3.5 %collective-permute-done.4 = bf16[512,512]{1,0:T(8,128)(2,1)S(1)} collective-permute-done((bf16[512,512]{1,0:T(8,128)(2,1)}, bf16[512,512]{1,0:T(8,128)(2,1)S(1)}, u32[]{:S(2)}, u32[]{:S(2)}) %collective-permute-start.4) | collective-permute-done | bytes 524320 | tf_op jit(solution)/shard_map/ppermute | solution.py:35
  54.1 2.0 %collective-permute-done.6 = bf16[512,512]{1,0:T(8,128)(2,1)} collective-permute-done((bf16[512,512]{1,0:T(8,128)(2,1)}, bf16[512,512]{1,0:T(8,128)(2,1)}, u32[]{:S(2)}, u32[]{:S(2)}) %collective-permute-start.6) | collective-permute-done | bytes 524320 | tf_op jit(solution)/shard_map/ppermute | solution.py:35
  56.1 2.5 %shard_map.75 = bf16[1280,512]{1,0:T(8,128)(2,1)} custom-call(bf16[256,512]{1,0:T(8,128)(2,1)} %copy-done.15, bf16[256,512]{1,0:T(8,128)(2,1)} %copy-done.16, bf16[256,512]{1,0:T(8,128)(2,1)} %copy-done.18, bf16[256,512]{1,0:T(8,128)(2,1)} %copy-done.17, bf16[256,512]{1,0:T(8,128)(2,1)} %copy-done.19), custom_call_target="tpu_custom_call" | custom-call | tf_op jit(solution)/shard_map/pallas_call | solution.py:79
  58.6 8.0 %all-gather.2.cloned.1.call-done.tok_ref = bf16[512,8320]{1,0:T(8,128)(2,1)} async-done(((bf16[64,8320]{1,0:T(8,128)(2,1)}), bf16[512,8320]{1,0:T(8,128)(2,1)}) %all-gather.2.cloned.1.call-update) | async-done | bytes 8519696 | tf_op jit(solution)/shard_map/all_gather | solution.py:285
  66.6 2.4 %collective-permute-start.12 = (bf16[1280,512]{1,0:T(8,128)(2,1)}, bf16[1280,512]{1,0:T(8,128)(2,1)}, u32[]{:S(2)}, u32[]{:S(2)}) collective-permute-start(bf16[1280,512]{1,0:T(8,128)(2,1)} %shard_map.75), channel_id=1, source_target_pairs={{64,0},{72,8},{80,16},{88,24},{96,32},{104,40},{112,48},{120,56},{... | collective-permute-start | bytes 3932168 | tf_op jit(solution)/shard_map/ppermute | solution.py:35
  69.0 3.1 %collective-permute-start.17 = (bf16[1024,256]{1,0:T(8,128)(2,1)S(1)}, bf16[1024,256]{1,0:T(8,128)(2,1)S(1)}, u32[]{:S(2)}, u32[]{:S(2)}) collective-permute-start(bf16[1024,256]{1,0:T(8,128)(2,1)S(1)} %collective-permute-done.15.refs_1_), channel_id=1, source_target_pairs={{8,0},{16,8},{24,16},{32,24},{40,32},{48,40},{56,48},{0,56},{72,64... | collective-permute-start | bytes 1572872 | tf_op jit(solution)/shard_map/ppermute | solution.py:30
  72.1 1.7 fusion.20
  73.8 0.1 reshape.121
  73.9 3.6 %fusion.12 = f32[512,512]{1,0:T(8,128)} fusion(bf16[1280,512]{1,0:T(8,128)(2,1)} %shard_map.75, bf16[512,8320]{1,0:T(8,128)(2,1)} %all-gather.2.cloned.1.call-done.tok_ref), kind=kOutput, calls=%fused_computation.18 | convolution fusion | flops 671088640 | bytes 3670016 | tf_op jit(solution)/shard_map/dot_general | solution.py:89
  77.5 1.5 fusion.17
  79.0 2.3 %fusion.26 = f32[512,512]{1,0:T(8,128)} fusion(bf16[256,768]{1,0:T(8,128)(2,1)S(1)} %copy-done.7, bf16[512,8320]{1,0:T(8,128)(2,1)} %all-gather.2.cloned.1.call-done.tok_ref), kind=kOutput, calls=%fused_computation.34 | convolution fusion | flops 134217728 | bytes 1572864 | tf_op jit(solution)/shard_map/dot_general | solution.py:89
  81.3 2.2 %fusion.29 = f32[512,512]{1,0:T(8,128)} fusion(bf16[256,512]{1,0:T(8,128)(2,1)S(1)} %copy-done.11, bf16[512,8320]{1,0:T(8,128)(2,1)} %all-gather.2.cloned.1.call-done.tok_ref), kind=kOutput, calls=%fused_computation.37 | convolution fusion | flops 134217728 | bytes 1572864 | tf_op jit(solution)/shard_map/dot_general | solution.py:89
  83.6 2.6 %fusion.15 = f32[512,512]{1,0:T(8,128)} fusion(bf16[512,512]{1,0:T(8,128)(2,1)} %collective-permute-done.6, bf16[512,8320]{1,0:T(8,128)(2,1)} %all-gather.2.cloned.1.call-done.tok_ref), kind=kOutput, calls=%fused_computation.21 | convolution fusion | flops 268435456 | bytes 2097152 | tf_op jit(solution)/shard_map/dot_general | solution.py:89
  86.2 0.3 convert_reduce_fusion.1
  86.5 0.1 reduce_sum.12
  86.6 1.4 fusion.21
  88.0 2.5 %fusion.4 = f32[512,512]{1,0:T(8,128)S(1)} fusion(f32[512,512]{1,0:T(8,128)S(1)} %fusion.17, f32[512,512]{1,0:T(8,128)} %fusion.26, f32[512,512]{1,0:T(8,128)} %fusion.29, bf16[512,512]{1,0:T(8,128)(2,1)} %shard_map.74, bf16[512,8320]{1,0:T(8,128)(2,1)} %all-gather.2.cloned.1.call-done.tok_ref), kind=kOutput, calls=%fused_computation.8 | convolution fusion | flops 269221888 | bytes 5242880 | tf_op jit(solution)/shard_map/dot_general | solution.py:89
  90.5 2.8 %collective-permute-start.21 = (bf16[1024,256]{1,0:T(8,128)(2,1)S(1)}, bf16[1024,256]{1,0:T(8,128)(2,1)S(1)}, u32[]{:S(2)}, u32[]{:S(2)}) collective-permute-start(bf16[1024,256]{1,0:T(8,128)(2,1)S(1)} %collective-permute-done.17.refs_3_), channel_id=1, source_target_pairs={{8,0},{16,8},{24,16},{32,24},{40,32},{48,40},{56,48},{0,56},{72,64... | collective-permute-start | bytes 1572872 | tf_op jit(solution)/shard_map/ppermute | solution.py:30
  93.3 1.3 fusion.7
  94.7 2.1 %shard_map.77.kv_ref = f32[512,256]{1,0:T(8,128)S(1)} custom-call(bf16[512,8320]{1,0:T(8,128)(2,1)S(1)} %copy-done, bf16[1024,256]{1,0:T(8,128)(2,1)S(1)} %copy-done.1, bf16[1024,256]{1,0:T(8,128)(2,1)S(1)} %collective-permute-done.15.refs_1_, bf16[1024,256]{1,0:T(8,128)(2,1)S(1)} %collective-permute-done.16.refs_2_, ...), custom_call_target="tpu_custom_call" | custom-call | tf_op jit(solution)/shard_map/pallas_call | solution.py:147
  96.8 6.6 %collective-permute-done.21.rp3 = bf16[1024,256]{1,0:T(8,128)(2,1)S(1)} collective-permute-done((bf16[1024,256]{1,0:T(8,128)(2,1)S(1)}, bf16[1024,256]{1,0:T(8,128)(2,1)S(1)}, u32[]{:S(2)}, u32[]{:S(2)}) %collective-permute-start.21) | collective-permute-done | bytes 524320 | tf_op jit(solution)/shard_map/ppermute | solution.py:30
  103.4 3.1 %collective-permute-done.22.rm3 = bf16[1024,256]{1,0:T(8,128)(2,1)S(1)} collective-permute-done((bf16[1024,256]{1,0:T(8,128)(2,1)S(1)}, bf16[1024,256]{1,0:T(8,128)(2,1)S(1)}, u32[]{:S(2)}, u32[]{:S(2)}) %collective-permute-start.22) | collective-permute-done | bytes 524320 | tf_op jit(solution)/shard_map/ppermute | solution.py:30
  106.6 1.1 slice.72
  107.7 2.5 %collective-permute-start.19 = (bf16[640,512]{1,0:T(8,128)(2,1)S(1)}, bf16[640,512]{1,0:T(8,128)(2,1)S(1)}, u32[]{:S(2)}, u32[]{:S(2)}) collective-permute-start(bf16[640,512]{1,0:T(8,128)(2,1)S(1)} %slice.72), channel_id=1, source_target_pairs={{64,0},{72,8},{80,16},{88,24},{96,32},{104,40},{112,48},{120,56},{... | collective-permute-start | bytes 1966088 | tf_op jit(solution)/shard_map/ppermute | solution.py:35
  110.1 1.1 slice.73
  111.3 0.1 collective-permute-start.20
  111.4 2.2 %fusion.9 = f32[512,512]{1,0:T(8,128)S(1)} fusion(bf16[1280,512]{1,0:T(8,128)(2,1)} %collective-permute-done.13, bf16[512,8320]{1,0:T(8,128)(2,1)S(1)} %copy-done), kind=kOutput, calls=%fused_computation.15 | convolution fusion | flops 671088640 | bytes 3670016 | tf_op jit(solution)/shard_map/dot_general | solution.py:89
  113.5 2.2 %fusion.8 = f32[512,512]{1,0:T(8,128)S(1)} fusion(f32[512,512]{1,0:T(8,128)S(1)} %fusion.7, f32[512,512]{1,0:T(8,128)S(1)} %fusion.9, bf16[1280,512]{1,0:T(8,128)(2,1)} %collective-permute-done.12, bf16[512,8320]{1,0:T(8,128)(2,1)S(1)} %copy-done), kind=kOutput, calls=%fused_computation.14 | convolution fusion | flops 671612928 | bytes 5767168 | tf_op jit(solution)/shard_map/dot_general | solution.py:89
  115.7 0.4 collective-permute-start.23
  116.1 1.2 collective-permute-start.24
  117.3 1.5 convolution_add_fusion.q_ref
  118.7 2.6 %collective-permute-done.23.ends0 = bf16[512,256]{1,0:T(8,128)(2,1)S(1)} collective-permute-done((bf16[512,256]{1,0:T(8,128)(2,1)S(1)}, bf16[512,256]{1,0:T(8,128)(2,1)S(1)}, u32[]{:S(2)}, u32[]{:S(2)}) %collective-permute-start.23) | collective-permute-done | bytes 262176 | tf_op jit(solution)/shard_map/ppermute | solution.py:30
  121.3 1.5 collective-permute-done.24.ends1
  122.8 3.1 %collective-permute-done.20.f2b = bf16[640,512]{1,0:T(8,128)(2,1)S(1)} collective-permute-done((bf16[640,512]{1,0:T(8,128)(2,1)S(1)}, bf16[640,512]{1,0:T(8,128)(2,1)S(1)}, u32[]{:S(2)}, u32[]{:S(2)}) %collective-permute-start.20) | collective-permute-done | bytes 655392 | tf_op jit(solution)/shard_map/ppermute | solution.py:35
  125.9 4.7 %shard_map.78 = bf16[768,768]{1,0:T(8,128)(2,1)} custom-call(bf16[512,8320]{1,0:T(8,128)(2,1)S(1)} %copy-done, s32[1,512]{1,0:T(1,128)S(1)} %add_add_fusion.slot_ref, f32[512,512]{1,0:T(8,128)S(1)} %convolution_add_fusion.q_ref, f32[512,256]{1,0:T(8,128)S(1)} %shard_map.77.kv_ref, bf16[640,512]{1,0:T(8,128)(2,1)S(1)} %collective-permute-done.19.f2a, ...), custom_call_target="tpu_custom_call" | custom-call | tf_op jit(solution)/shard_map/pallas_call | solution.py:193
  130.6 4.4 %all-to-all-start = ((bf16[32,24,768]{2,1,0:T(8,128)(2,1)}), bf16[32,24,768]{2,1,0:T(8,128)(2,1)S(1)}, u32[]{:S(2)}, u32[]{:S(2)}) async-start(bf16[32,24,768]{2,1,0:T(8,128)(2,1)} %bitcast.2), calls=%async_computation | async-start | bytes 2359296 | tf_op jit(solution)/shard_map/all_to_all | solution.py:290
  135.0 0.1 copy.11.segq_ref
  135.2 1.0 fusion.33
  136.2 0.2 pad_maximum_fusion
  136.4 0.3 fusion.ahead_ref
  136.8 21.9 %all-to-all-done = bf16[32,24,768]{2,1,0:T(8,128)(2,1)S(1)} async-done(((bf16[32,24,768]{2,1,0:T(8,128)(2,1)}), bf16[32,24,768]{2,1,0:T(8,128)(2,1)S(1)}, u32[]{:S(2)}, u32[]{:S(2)}) %all-to-all-start) | async-done | bytes 1179680 | tf_op jit(solution)/shard_map/all_to_all | solution.py:290
  158.7 5.0 %shard_map.79 = bf16[512,512]{1,0:T(8,128)(2,1)S(1)} custom-call(bf16[768,768]{1,0:T(8,128)(2,1)S(1)} %bitcast.17, bf16[768,768]{1,0:T(8,128)(2,1)S(1)} %fusion.ahead_ref, s32[512,1]{1,0:T(8,128)S(1)} %copy.11.segq_ref, s32[1,640]{1,0:T(1,128)S(1)} %broadcast_in_dim.11.segk_ref, f32[512,128]{1,0:T(8,128)S(1)} %get-tuple-element.40.cos_ref, ...), custom_call_target="tpu_custom_call" | custom-call | tf_op jit(solution)/shard_map/pallas_call | solution.py:254
  163.7 20.9 %all_to_all.21 = bf16[8,64,512]{2,1,0:T(8,128)(2,1)S(1)} all-to-all(bf16[8,64,512]{2,1,0:T(8,128)(2,1)S(1)} %bitcast.18), channel_id=1, replica_groups=mesh['dp'=32,'seq'=8] {'seq'}, dimensions={0} | all-to-all | bytes 1048576 | tf_op jit(solution)/shard_map/all_to_all | solution.py:297
  184.6 0.3 copy.12
  184.9 1.0 broadcast_in_dim.12
  (90 shorter events, 0.4 us)
Async XLA Ops:
  6.5 2.8 %copy-start.10 = (bf16[256,512]{1,0:T(8,128)(2,1)S(1)}, bf16[256,512]{1,0:T(8,128)(2,1)}, u32[]{:S(2)}) copy-start(bf16[256,512]{1,0:T(8,128)(2,1)} %param.11) | copy-start | bytes 786436
  6.5 9.3 %copy-start.22 = (bf16[256,128]{1,0:T(8,128)(2,1)S(1)}, bf16[256,128]{1,0:T(8,128)(2,1)}, u32[]{:S(2)}) copy-start(bf16[256,128]{1,0:T(8,128)(2,1)} %param.12) | copy-start | bytes 196612
  6.5 17.7 %copy-start.23 = (bf16[256,128]{1,0:T(8,128)(2,1)S(1)}, bf16[256,128]{1,0:T(8,128)(2,1)}, u32[]{:S(2)}) copy-start(bf16[256,128]{1,0:T(8,128)(2,1)} %param.13) | copy-start | bytes 196612
  6.5 60.0 %all-gather.2.cloned.1.call-start = ((), (), s32[]{:S(2)}) async-start(), calls=%async_computation.2 | async-start | bytes 9584640 | tf_op jit(solution)/shard_map/all_gather | solution.py:285
  9.4 11.5 %collective-permute-start = (bf16[256,512]{1,0:T(8,128)(2,1)S(1)}, bf16[256,512]{1,0:T(8,128)(2,1)S(1)}, u32[]{:S(2)}, u32[]{:S(2)}) collective-permute-start(bf16[256,512]{1,0:T(8,128)(2,1)S(1)} %copy-done.10), channel_id=1, source_target_pairs={{8,0},{16,8},{24,16},{32,24},{40,32},{48,40},{56,48},{0,56},{72,64... | collective-permute-start | bytes 786440 | tf_op jit(solution)/shard_map/ppermute | solution.py:30
  15.8 8.4 %collective-permute-start.1 = (bf16[256,512]{1,0:T(8,128)(2,1)S(1)}, bf16[256,512]{1,0:T(8,128)(2,1)S(1)}, u32[]{:S(2)}, u32[]{:S(2)}) collective-permute-start(bf16[256,512]{1,0:T(8,128)(2,1)S(1)} %copy-done.10), channel_id=1, source_target_pairs={{56,0},{0,8},{8,16},{16,24},{24,32},{32,40},{40,48},{48,56},{120,6... | collective-permute-start | bytes 786440 | tf_op jit(solution)/shard_map/ppermute | solution.py:30
  20.8 20.2 %copy-start.20 = (bf16[256,512]{1,0:T(8,128)(2,1)}, bf16[256,512]{1,0:T(8,128)(2,1)S(1)}, u32[]{:S(2)}) copy-start(bf16[256,512]{1,0:T(8,128)(2,1)S(1)} %collective-permute-done.refs_0_) | copy-start | bytes 786436
  20.8 7.5 %collective-permute-start.7 = (bf16[256,512]{1,0:T(8,128)(2,1)S(1)}, bf16[256,512]{1,0:T(8,128)(2,1)S(1)}, u32[]{:S(2)}, u32[]{:S(2)}) collective-permute-start(bf16[256,512]{1,0:T(8,128)(2,1)S(1)} %collective-permute-done.refs_0_), channel_id=1, source_target_pairs={{8,0},{16,8},{24,16},{32,24},{40,32},{48,40},{56,48},{0,56},{72,64... | collective-permute-start | bytes 786440 | tf_op jit(solution)/shard_map/ppermute | solution.py:30
  24.2 16.8 %copy-start.21 = (bf16[256,512]{1,0:T(8,128)(2,1)}, bf16[256,512]{1,0:T(8,128)(2,1)S(1)}, u32[]{:S(2)}) copy-start(bf16[256,512]{1,0:T(8,128)(2,1)S(1)} %collective-permute-done.1.refs_1_) | copy-start | bytes 786436
  24.2 7.3 %collective-permute-start.8 = (bf16[256,512]{1,0:T(8,128)(2,1)S(1)}, bf16[256,512]{1,0:T(8,128)(2,1)S(1)}, u32[]{:S(2)}, u32[]{:S(2)}) collective-permute-start(bf16[256,512]{1,0:T(8,128)(2,1)S(1)} %collective-permute-done.1.refs_1_), channel_id=1, source_target_pairs={{56,0},{0,8},{8,16},{16,24},{24,32},{32,40},{40,48},{48,56},{120,6... | collective-permute-start | bytes 786440 | tf_op jit(solution)/shard_map/ppermute | solution.py:30
  24.3 21.1 %copy-start.5 = (bf16[256,768]{1,0:T(8,128)(2,1)}, bf16[256,768]{1,0:T(8,128)(2,1)S(1)}, u32[]{:S(2)}) copy-start(bf16[256,768]{1,0:T(8,128)(2,1)S(1)} %constant_dynamic-update-slice_fusion.refs_0_) | copy-start | bytes 1179652
  24.3 11.1 %collective-permute-start.2 = (bf16[256,768]{1,0:T(8,128)(2,1)S(1)}, bf16[256,768]{1,0:T(8,128)(2,1)S(1)}, u32[]{:S(2)}, u32[]{:S(2)}) collective-permute-start(bf16[256,768]{1,0:T(8,128)(2,1)S(1)} %constant_dynamic-update-slice_fusion.refs_0_), channel_id=1, source_target_pairs={{64,0},{72,8},{80,16},{88,24},{96,32},{104,40},{112,48},{120,56},{... | collective-permute-start | bytes 1179656 | tf_op jit(solution)/shard_map/ppermute | solution.py:35
  28.3 27.8 %copy-start.15 = (bf16[256,512]{1,0:T(8,128)(2,1)}, bf16[256,512]{1,0:T(8,128)(2,1)S(1)}, u32[]{:S(2)}) copy-start(bf16[256,512]{1,0:T(8,128)(2,1)S(1)} %collective-permute-done.7.refs_0_) | copy-start | bytes 786436
  31.5 24.6 %copy-start.16 = (bf16[256,512]{1,0:T(8,128)(2,1)}, bf16[256,512]{1,0:T(8,128)(2,1)S(1)}, u32[]{:S(2)}) copy-start(bf16[256,512]{1,0:T(8,128)(2,1)S(1)} %collective-permute-done.8.refs_1_) | copy-start | bytes 786436
  31.5 6.8 %collective-permute-start.10 = (bf16[256,512]{1,0:T(8,128)(2,1)S(1)}, bf16[256,512]{1,0:T(8,128)(2,1)S(1)}, u32[]{:S(2)}, u32[]{:S(2)}) collective-permute-start(bf16[256,512]{1,0:T(8,128)(2,1)S(1)} %collective-permute-done.8.refs_1_), channel_id=1, source_target_pairs={{56,0},{0,8},{8,16},{16,24},{24,32},{32,40},{40,48},{48,56},{120,6... | collective-permute-start | bytes 786440 | tf_op jit(solution)/shard_map/ppermute | solution.py:30
  31.5 6.8 %collective-permute-start.9 = (bf16[256,512]{1,0:T(8,128)(2,1)S(1)}, bf16[256,512]{1,0:T(8,128)(2,1)S(1)}, u32[]{:S(2)}, u32[]{:S(2)}) collective-permute-start(bf16[256,512]{1,0:T(8,128)(2,1)S(1)} %collective-permute-done.7.refs_0_), channel_id=1, source_target_pairs={{8,0},{16,8},{24,16},{32,24},{40,32},{48,40},{56,48},{0,56},{72,64... | collective-permute-start | bytes 786440 | tf_op jit(solution)/shard_map/ppermute | solution.py:30
  34.2 8.7 %collective-permute-start.3 = (bf16[256,768]{1,0:T(8,128)(2,1)S(1)}, bf16[256,768]{1,0:T(8,128)(2,1)S(1)}, u32[]{:S(2)}, u32[]{:S(2)}) collective-permute-start(bf16[256,768]{1,0:T(8,128)(2,1)S(1)} %constant_dynamic-update-slice_fusion.refs_0_), channel_id=1, source_target_pairs={{192,0},{200,8},{208,16},{216,24},{224,32},{232,40},{240,48},{248,... | collective-permute-start | bytes 1179656 | tf_op jit(solution)/shard_map/ppermute | solution.py:35
  35.4 10.0 %copy-start.6 = (bf16[256,768]{1,0:T(8,128)(2,1)}, bf16[256,768]{1,0:T(8,128)(2,1)S(1)}, u32[]{:S(2)}) copy-start(bf16[256,768]{1,0:T(8,128)(2,1)S(1)} %collective-permute-done.2.refs_1_) | copy-start | bytes 1179652
  35.4 10.0 %collective-permute-start.5 = (bf16[256,768]{1,0:T(8,128)(2,1)S(1)}, bf16[256,768]{1,0:T(8,128)(2,1)S(1)}, u32[]{:S(2)}, u32[]{:S(2)}) collective-permute-start(bf16[256,768]{1,0:T(8,128)(2,1)S(1)} %collective-permute-done.2.refs_1_), channel_id=1, source_target_pairs={{64,0},{72,8},{80,16},{88,24},{96,32},{104,40},{112,48},{120,56},{... | collective-permute-start | bytes 1179656 | tf_op jit(solution)/shard_map/ppermute | solution.py:35
  38.4 17.7 %copy-start.17 = (bf16[256,512]{1,0:T(8,128)(2,1)}, bf16[256,512]{1,0:T(8,128)(2,1)S(1)}, u32[]{:S(2)}) copy-start(bf16[256,512]{1,0:T(8,128)(2,1)S(1)} %collective-permute-done.10.refs_3_) | copy-start | bytes 786436
  38.4 17.8 %copy-start.18 = (bf16[256,512]{1,0:T(8,128)(2,1)}, bf16[256,512]{1,0:T(8,128)(2,1)S(1)}, u32[]{:S(2)}) copy-start(bf16[256,512]{1,0:T(8,128)(2,1)S(1)} %collective-permute-done.9.refs_2_) | copy-start | bytes 786436
  38.4 10.0 %collective-permute-start.11 = (bf16[256,512]{1,0:T(8,128)(2,1)S(1)}, bf16[256,512]{1,0:T(8,128)(2,1)S(1)}, u32[]{:S(2)}, u32[]{:S(2)}) collective-permute-start(bf16[256,512]{1,0:T(8,128)(2,1)S(1)} %collective-permute-done.9.refs_2_), channel_id=1, source_target_pairs={{8,0},{16,8},{24,16},{32,24},{40,32},{48,40},{56,48},{0,56},{72,64... | collective-permute-start | bytes 786440 | tf_op jit(solution)/shard_map/ppermute | solution.py:30
  42.9 2.5 %copy-start.8 = (bf16[256,768]{1,0:T(8,128)(2,1)}, bf16[256,768]{1,0:T(8,128)(2,1)S(1)}, u32[]{:S(2)}) copy-start(bf16[256,768]{1,0:T(8,128)(2,1)S(1)} %collective-permute-done.3.refs_3_) | copy-start | bytes 1179652
  42.9 11.1 %collective-permute-start.4 = (bf16[512,512]{1,0:T(8,128)(2,1)}, bf16[512,512]{1,0:T(8,128)(2,1)S(1)}, u32[]{:S(2)}, u32[]{:S(2)}) collective-permute-start(bf16[512,512]{1,0:T(8,128)(2,1)} %shard_map.74), channel_id=1, source_target_pairs={{64,0},{72,8},{80,16},{88,24},{96,32},{104,40},{112,48},{120,56},{... | collective-permute-start | bytes 1572872 | tf_op jit(solution)/shard_map/ppermute | solution.py:35
  45.4 10.7 %collective-permute-start.6 = (bf16[512,512]{1,0:T(8,128)(2,1)}, bf16[512,512]{1,0:T(8,128)(2,1)}, u32[]{:S(2)}, u32[]{:S(2)}) collective-permute-start(bf16[512,512]{1,0:T(8,128)(2,1)} %shard_map.74), channel_id=1, source_target_pairs={{192,0},{200,8},{208,16},{216,24},{224,32},{232,40},{240,48},{248,... | collective-permute-start | bytes 1572872 | tf_op jit(solution)/shard_map/ppermute | solution.py:35
  45.4 0.7 copy-start.3
  48.3 7.8 %copy-start.19 = (bf16[256,512]{1,0:T(8,128)(2,1)}, bf16[256,512]{1,0:T(8,128)(2,1)S(1)}, u32[]{:S(2)}) copy-start(bf16[256,512]{1,0:T(8,128)(2,1)S(1)} %collective-permute-done.11.refs_4_) | copy-start | bytes 786436
  48.3 20.7 %collective-permute-start.15 = (bf16[1024,256]{1,0:T(8,128)(2,1)}, bf16[1024,256]{1,0:T(8,128)(2,1)S(1)}, u32[]{:S(2)}, u32[]{:S(2)}) collective-permute-start(bf16[1024,256]{1,0:T(8,128)(2,1)} %shard_map.76.refs_0_), channel_id=1, source_target_pairs={{8,0},{16,8},{24,16},{32,24},{40,32},{48,40},{56,48},{0,56},{72,64... | collective-permute-start | bytes 1572872 | tf_op jit(solution)/shard_map/ppermute | solution.py:30
  48.5 20.5 %collective-permute-start.16 = (bf16[1024,256]{1,0:T(8,128)(2,1)}, bf16[1024,256]{1,0:T(8,128)(2,1)S(1)}, u32[]{:S(2)}, u32[]{:S(2)}) collective-permute-start(bf16[1024,256]{1,0:T(8,128)(2,1)} %shard_map.76.refs_0_), channel_id=1, source_target_pairs={{56,0},{0,8},{8,16},{16,24},{24,32},{32,40},{40,48},{48,56},{120,6... | collective-permute-start | bytes 1572872 | tf_op jit(solution)/shard_map/ppermute | solution.py:30
  54.1 14.9 %copy-start.13 = (bf16[512,512]{1,0:T(8,128)(2,1)}, bf16[512,512]{1,0:T(8,128)(2,1)S(1)}, u32[]{:S(2)}) copy-start(bf16[512,512]{1,0:T(8,128)(2,1)S(1)} %collective-permute-done.4) | copy-start | bytes 1572868
  56.1 61.2 %collective-permute-start.14 = (bf16[512,512]{1,0:T(8,128)(2,1)}, bf16[512,512]{1,0:T(8,128)(2,1)}, u32[]{:S(2)}, u32[]{:S(2)}) collective-permute-start(bf16[512,512]{1,0:T(8,128)(2,1)} %collective-permute-done.6), channel_id=1, source_target_pairs={{192,0},{200,8},{208,16},{216,24},{224,32},{232,40},{240,48},{248,... | collective-permute-start | bytes 1572872 | tf_op jit(solution)/shard_map/ppermute | solution.py:35
  66.6 40.0 %collective-permute-start.12 = (bf16[1280,512]{1,0:T(8,128)(2,1)}, bf16[1280,512]{1,0:T(8,128)(2,1)}, u32[]{:S(2)}, u32[]{:S(2)}) collective-permute-start(bf16[1280,512]{1,0:T(8,128)(2,1)} %shard_map.75), channel_id=1, source_target_pairs={{64,0},{72,8},{80,16},{88,24},{96,32},{104,40},{112,48},{120,56},{... | collective-permute-start | bytes 3932168 | tf_op jit(solution)/shard_map/ppermute | solution.py:35
  69.0 37.6 %collective-permute-start.13 = (bf16[1280,512]{1,0:T(8,128)(2,1)}, bf16[1280,512]{1,0:T(8,128)(2,1)}, u32[]{:S(2)}, u32[]{:S(2)}) collective-permute-start(bf16[1280,512]{1,0:T(8,128)(2,1)} %shard_map.75), channel_id=1, source_target_pairs={{192,0},{200,8},{208,16},{216,24},{224,32},{232,40},{240,48},{248,... | collective-permute-start | bytes 3932168 | tf_op jit(solution)/shard_map/ppermute | solution.py:35
  69.0 21.5 %collective-permute-start.17 = (bf16[1024,256]{1,0:T(8,128)(2,1)S(1)}, bf16[1024,256]{1,0:T(8,128)(2,1)S(1)}, u32[]{:S(2)}, u32[]{:S(2)}) collective-permute-start(bf16[1024,256]{1,0:T(8,128)(2,1)S(1)} %collective-permute-done.15.refs_1_), channel_id=1, source_target_pairs={{8,0},{16,8},{24,16},{32,24},{40,32},{48,40},{56,48},{0,56},{72,64... | collective-permute-start | bytes 1572872 | tf_op jit(solution)/shard_map/ppermute | solution.py:30
  72.1 18.4 %collective-permute-start.18 = (bf16[1024,256]{1,0:T(8,128)(2,1)S(1)}, bf16[1024,256]{1,0:T(8,128)(2,1)S(1)}, u32[]{:S(2)}, u32[]{:S(2)}) collective-permute-start(bf16[1024,256]{1,0:T(8,128)(2,1)S(1)} %collective-permute-done.16.refs_2_), channel_id=1, source_target_pairs={{56,0},{0,8},{8,16},{16,24},{24,32},{32,40},{40,48},{48,56},{120,6... | collective-permute-start | bytes 1572872 | tf_op jit(solution)/shard_map/ppermute | solution.py:30
  73.9 3.6 %copy-start.14 = (bf16[512,512]{1,0:T(8,128)(2,1)S(1)}, bf16[512,512]{1,0:T(8,128)(2,1)}, u32[]{:S(2)}) copy-start(bf16[512,512]{1,0:T(8,128)(2,1)} %copy-done.13) | copy-start | bytes 1572868
  73.9 5.1 %copy-start.7 = (bf16[256,768]{1,0:T(8,128)(2,1)S(1)}, bf16[256,768]{1,0:T(8,128)(2,1)}, u32[]{:S(2)}) copy-start(bf16[256,768]{1,0:T(8,128)(2,1)} %copy-done.6) | copy-start | bytes 1179652
  77.5 3.8 %copy-start.11 = (bf16[256,512]{1,0:T(8,128)(2,1)S(1)}, bf16[256,512]{1,0:T(8,128)(2,1)}, u32[]{:S(2)}) copy-start(bf16[256,512]{1,0:T(8,128)(2,1)} %param.11) | copy-start | bytes 786436
  79.0 7.5 %copy-start.9 = (bf16[256,768]{1,0:T(8,128)(2,1)S(1)}, bf16[256,768]{1,0:T(8,128)(2,1)}, u32[]{:S(2)}) copy-start(bf16[256,768]{1,0:T(8,128)(2,1)} %copy-done.8) | copy-start | bytes 1179652
  86.6 6.7 %copy-start.25 = (s32[512]{0:T(512)S(1)}, s32[512]{0:T(512)}, u32[]{:S(2)}) copy-start(s32[512]{0:T(512)} %get-tuple-element.35) | copy-start | bytes 6148
  86.6 6.7 %copy-start.26 = (s32[1,512]{1,0:T(1,128)S(1)}, s32[1,512]{1,0:T(1,128)}, u32[]{:S(2)}) copy-start(s32[1,512]{1,0:T(1,128)} %add.83) | copy-start | bytes 6148
  86.6 6.7 %copy-start.2 = (f32[512,512]{1,0:T(8,128)S(1)}, f32[512,512]{1,0:T(8,128)}, u32[]{:S(2)}) copy-start(f32[512,512]{1,0:T(8,128)} %fusion.15) | copy-start | bytes 3145732
  86.6 6.7 %copy-start.4 = (bf16[256,768]{1,0:T(8,128)(2,1)S(1)}, bf16[256,768]{1,0:T(8,128)(2,1)}, u32[]{:S(2)}) copy-start(bf16[256,768]{1,0:T(8,128)(2,1)} %copy-done.3) | copy-start | bytes 1179652
  86.6 6.7 %copy-start.12 = (f32[512,512]{1,0:T(8,128)S(1)}, f32[512,512]{1,0:T(8,128)}, u32[]{:S(2)}) copy-start(f32[512,512]{1,0:T(8,128)} %fusion.12) | copy-start | bytes 3145732
  88.0 6.7 %copy-start = (bf16[512,8320]{1,0:T(8,128)(2,1)S(1)}, bf16[512,8320]{1,0:T(8,128)(2,1)}, u32[]{:S(2)}) copy-start(bf16[512,8320]{1,0:T(8,128)(2,1)} %all-gather.2.cloned.1.call-done.tok_ref) | copy-start | bytes 25559044
  90.5 12.9 %collective-permute-start.21 = (bf16[1024,256]{1,0:T(8,128)(2,1)S(1)}, bf16[1024,256]{1,0:T(8,128)(2,1)S(1)}, u32[]{:S(2)}, u32[]{:S(2)}) collective-permute-start(bf16[1024,256]{1,0:T(8,128)(2,1)S(1)} %collective-permute-done.17.refs_3_), channel_id=1, source_target_pairs={{8,0},{16,8},{24,16},{32,24},{40,32},{48,40},{56,48},{0,56},{72,64... | collective-permute-start | bytes 1572872 | tf_op jit(solution)/shard_map/ppermute | solution.py:30
  93.2 13.3 %collective-permute-start.22 = (bf16[1024,256]{1,0:T(8,128)(2,1)S(1)}, bf16[1024,256]{1,0:T(8,128)(2,1)S(1)}, u32[]{:S(2)}, u32[]{:S(2)}) collective-permute-start(bf16[1024,256]{1,0:T(8,128)(2,1)S(1)} %collective-permute-done.18.refs_4_), channel_id=1, source_target_pairs={{56,0},{0,8},{8,16},{16,24},{24,32},{32,40},{40,48},{48,56},{120,6... | collective-permute-start | bytes 1572872 | tf_op jit(solution)/shard_map/ppermute | solution.py:30
  93.3 1.4 copy-start.1
  107.7 15.1 %collective-permute-start.19 = (bf16[640,512]{1,0:T(8,128)(2,1)S(1)}, bf16[640,512]{1,0:T(8,128)(2,1)S(1)}, u32[]{:S(2)}, u32[]{:S(2)}) collective-permute-start(bf16[640,512]{1,0:T(8,128)(2,1)S(1)} %slice.72), channel_id=1, source_target_pairs={{64,0},{72,8},{80,16},{88,24},{96,32},{104,40},{112,48},{120,56},{... | collective-permute-start | bytes 1966088 | tf_op jit(solution)/shard_map/ppermute | solution.py:35
  111.3 14.7 %collective-permute-start.20 = (bf16[640,512]{1,0:T(8,128)(2,1)S(1)}, bf16[640,512]{1,0:T(8,128)(2,1)S(1)}, u32[]{:S(2)}, u32[]{:S(2)}) collective-permute-start(bf16[640,512]{1,0:T(8,128)(2,1)S(1)} %slice.73), channel_id=1, source_target_pairs={{192,0},{200,8},{208,16},{216,24},{224,32},{232,40},{240,48},{248,... | collective-permute-start | bytes 1966088 | tf_op jit(solution)/shard_map/ppermute | solution.py:35
  115.7 5.6 %collective-permute-start.23 = (bf16[512,256]{1,0:T(8,128)(2,1)S(1)}, bf16[512,256]{1,0:T(8,128)(2,1)S(1)}, u32[]{:S(2)}, u32[]{:S(2)}) collective-permute-start(bf16[512,256]{1,0:T(8,128)(2,1)S(1)} %slice.91), channel_id=1, source_target_pairs={{8,0},{16,8},{24,16},{32,24},{40,32},{48,40},{56,48},{0,56},{72,64... | collective-permute-start | bytes 786440 | tf_op jit(solution)/shard_map/ppermute | solution.py:30
  116.1 6.7 %collective-permute-start.24 = (bf16[512,256]{1,0:T(8,128)(2,1)S(1)}, bf16[512,256]{1,0:T(8,128)(2,1)S(1)}, u32[]{:S(2)}, u32[]{:S(2)}) collective-permute-start(bf16[512,256]{1,0:T(8,128)(2,1)S(1)} %slice.92), channel_id=1, source_target_pairs={{56,0},{0,8},{8,16},{16,24},{24,32},{32,40},{40,48},{48,56},{120,6... | collective-permute-start | bytes 786440 | tf_op jit(solution)/shard_map/ppermute | solution.py:30
  130.6 4.4 %copy-start.24 = (s32[1,512]{1,0:T(1,128)S(1)}, s32[1,512]{1,0:T(1,128)}, u32[]{:S(2)}) copy-start(s32[1,512]{1,0:T(1,128)} %param.9) | copy-start | bytes 6148
  130.6 28.1 %all-to-all-start = ((bf16[32,24,768]{2,1,0:T(8,128)(2,1)}), bf16[32,24,768]{2,1,0:T(8,128)(2,1)S(1)}, u32[]{:S(2)}, u32[]{:S(2)}) async-start(bf16[32,24,768]{2,1,0:T(8,128)(2,1)} %bitcast.2), calls=%async_computation | async-start | bytes 2359296 | tf_op jit(solution)/shard_map/all_to_all | solution.py:290
Sparse Core Ops, SparseCore 0:
  9.5 57.0 all-gather.1
where the time goes:
time: 193 us
  waiting for transfers between devices  63.4 us (33%)
  starting transfers between devices  41.2 us (21%)
  matrix products  23.3 us (12%)
  Pallas kernels  21.1 us (11%)
  blocking collectives  20.9 us (11%)
  between operations  13.8 us (7%)
  local copies, waits for them, and re-layouts  5.52 us (3%)
  other arithmetic  3.55 us (2%)
    ppermute x15, waiting for transfers between devices, from_z(): return lax.ppermute(value, 'dp', pairs)  24.8 us
    ppermute x15, starting transfers between devices, from_z(): return lax.ppermute(value, 'dp', pairs)  24.1 us
    dot_general x11, matrix products, part_dots(): jnp.dot(tokens[:, at * KB:at * KB + w.shape[0]], w, preferred_element_typ...  23.3 us
    all_to_all x1, waiting for transfers between devices, shards(): lax.all_to_all(outgoing.reshape(ND, SLOTS, -1), 'dp', split_axis=0, conca...  21.9 us
    all_to_all x1, blocking collectives, shards(): lax.all_to_all(context, 'seq', split_axis=0, concat_axis=1, tiled=True)  20.9 us
    ppermute x10, starting transfers between devices, from_x(): return lax.ppermute(value, 'dp', pairs)  12.7 us
    ppermute x10, waiting for transfers between devices, from_x(): return lax.ppermute(value, 'dp', pairs)  8.73 us
    all_gather x1, waiting for transfers between devices, shards(): tokens = lax.all_gather(normed, 'seq', axis=0, tiled=True)  7.96 us
  transfers between devices with their start and end apart: 27, of which 13 were waited for; matrix products, arithmetic and copies ran while one was open for 16% of the time, Pallas kernels for 4%

commit v1 on v0

--- a/solution.py
+++ b/solution.py
@@ -99,29 +99,29 @@
     o2 = from_x(op, 1)
     near = after(join(zp1, zm1), op, om)
     n1, n3 = from_x(near, 1), from_x(near, -1)
-    zp2, zm2 = from_z(zp1, 1), from_z(zm1, -1)
-    a, b = after((zp2, zm2), zp2, zm2)
+    a, b = after((zp1, zm1), op, om)
+    zp2, zm2 = from_z(a, 1), from_z(b, -1)
+    a, b = after((zp2, zm2), o2)
     zp3, zm3 = from_z(a, 1), from_z(b, -1)
-    z4 = from_z(after(zp3, zm3), 1)
-    row = after(join(own, op, o2, om, columns=cols), z4)
+    z4 = from_z(after(zp3, zm3, n3), 1)
+    row = after(join(own, op, o2, om, columns=cols), z4, n1)
     rp1, rm1 = from_z(row, 1), from_z(row, -1)
-    n2 = from_x(after(n3, n1), -1)
-    far = after(join(zp2, zm2, zp3, zm3, z4), n1, n3, row, tokens)
+    n2 = from_x(n3, -1)
+    far = after(join(zp2, zm2, zp3, zm3, z4), n1, n3, row)
     f1, f3 = from_x(far, 1), from_x(far, -1)
     early = [(query, 0), (near, 1), (op[:, :cols], 8), (n1, 9), (o2[:, :cols], 16), (om[:, :cols], 24), (n3, 25)]
     q_sum = part_dots(tokens, early)
-    a, b = after((rp1, rm1), rp1, rm1, n1, n3, tokens)
+    a, b = after((rp1, rm1), n1, n2, tokens)
     rp2, rm2 = from_z(a, 1), from_z(b, -1)
-    q_sum = q_sum + part_dots(tokens, [(far, 3)])
     a, b = after((rp2, rm2), rp2, rm2)
     rp3, rm3 = from_z(a, 1), from_z(b, -1)
-    f1, f3 = after((f1, f3), q_sum)
+    f1, f3 = after((f1, f3), q_sum, rp2, rm2)
     g = far.shape[0] // 2
     f2 = [from_x(f1[:g], 1), from_x(f3[g:], -1)]
     kv_sum = kv_early(tokens, [row, rp1, rm1, rp2, rm2])
-    q_sum = q_sum + part_dots(tokens, [(f1, 11), (f3, 27)])
+    q_sum = q_sum + part_dots(tokens, [(far, 3), (f1, 11), (f3, 27)])
     h = row.shape[0] // 2
-    a, b = after((rp3[:h], rm3[h:]), kv_sum, q_sum)
+    a, b = after((rp3[:h], rm3[h:]), kv_sum)
     ends = [from_z(a, 1), from_z(b, -1)]
     q_sum = q_sum + part_dots(tokens, [(n2, 17)])
     return q_sum, kv_sum, f2, [rp3, rm3, *ends]

time: 193 us -> 180 us (0.933)
  waiting for transfers between devices: 63.4 us -> 54.1 us
  matrix products: 23.3 us -> 19.2 us
    ppermute x15, waiting for transfers between devices: 24.8 us -> 14.7 us  [from_z(): return lax.ppermute(value, 'dp', pairs)]
    dot_general x11, matrix products: 23.3 us -> 19.2 us  [part_dots(): jnp.dot(tokens[:, at * KB:at * KB + w.shape[0]], w, preferred_element_typ...]
    ppermute x10, waiting for transfers between devices: 8.73 us -> 11.7 us  [from_x(): return lax.ppermute(value, 'dp', pairs)]
    all_to_all x1, starting transfers between devices: 4.39 us -> 6.85 us  [shards(): lax.all_to_all(outgoing.reshape(ND, SLOTS, -1), 'dp', split_axis=0, conca...]
    all_to_all x1, waiting for transfers between devices: 21.9 us -> 19.8 us  [shards(): lax.all_to_all(outgoing.reshape(ND, SLOTS, -1), 'dp', split_axis=0, conca...]
  transfers between devices with their start and end apart: 27 -> 27, of which waited for: 13 -> 13; matrix products, arithmetic and copies ran while one was open for 16% -> 14% of each run, Pallas kernels for 4% -> 5%
where the time goes in v1:
time: 180 us
  waiting for transfers between devices  54.1 us (30%)
  starting transfers between devices  41.1 us (23%)
  blocking collectives  22.5 us (12%)
  Pallas kernels  21.1 us (12%)
  matrix products  19.2 us (11%)
  between operations  13.8 us (8%)
  local copies, waits for them, and re-layouts  4.84 us (3%)
  other arithmetic  3.01 us (2%)
    ppermute x15, starting transfers between devices, from_z(): return lax.ppermute(value, 'dp', pairs)  22.7 us
    all_to_all x1, blocking collectives, shards(): lax.all_to_all(context, 'seq', split_axis=0, concat_axis=1, tiled=True)  22.5 us
    all_to_all x1, waiting for transfers between devices, shards(): lax.all_to_all(outgoing.reshape(ND, SLOTS, -1), 'dp', split_axis=0, conca...  19.8 us
    dot_general x11, matrix products, part_dots(): jnp.dot(tokens[:, at * KB:at * KB + w.shape[0]], w, preferred_element_typ...  19.2 us
    ppermute x15, waiting for transfers between devices, from_z(): return lax.ppermute(value, 'dp', pairs)  14.7 us
    ppermute x10, waiting for transfers between devices, from_x(): return lax.ppermute(value, 'dp', pairs)  11.7 us
    ppermute x10, starting transfers between devices, from_x(): return lax.ppermute(value, 'dp', pairs)  11.6 us
    all_gather x1, waiting for transfers between devices, shards(): tokens = lax.all_gather(normed, 'seq', axis=0, tiled=True)  7.89 us
  transfers between devices with their start and end apart: 27, of which 13 were waited for; matrix products, arithmetic and copies ran while one was open for 14% of the time, Pallas kernels for 5%

profile of v1, /device:TPU:1, one launch (start us, length us, event | category | flops | bytes accessed | tf_op | source)
XLA Modules:
  0.0 179.7 jit_solution(16431973895869861438)
XLA Ops:
  6.5 2.8 %shard_map.73 = bf16[64,8320]{1,0:T(8,128)(2,1)} custom-call(bf16[64,8192]{1,0:T(8,128)(2,1)} %bitcast.20, f32[1,8192]{1,0:T(1,128)} %bitcast.21, s32[1,64]{1,0:T(1,128)} %target_ref.1), custom_call_target="tpu_custom_call" | custom-call | tf_op jit(solution)/shard_map/pallas_call | solution.py:62
  9.5 3.4 %collective-permute-start.2 = (bf16[256,768]{1,0:T(8,128)(2,1)S(1)}, bf16[256,768]{1,0:T(8,128)(2,1)S(1)}, u32[]{:S(2)}, u32[]{:S(2)}) collective-permute-start(bf16[256,768]{1,0:T(8,128)(2,1)S(1)} %constant_dynamic-update-slice_fusion.refs_0_), channel_id=1, source_target_pairs={{64,0},{72,8},{80,16},{88,24},{96,32},{104,40},{112,48},{120,56},{... | collective-permute-start | bytes 1179656 | tf_op jit(solution)/shard_map/ppermute | solution.py:35
  12.8 5.6 %collective-permute-start = (bf16[256,512]{1,0:T(8,128)(2,1)S(1)}, bf16[256,512]{1,0:T(8,128)(2,1)S(1)}, u32[]{:S(2)}, u32[]{:S(2)}) collective-permute-start(bf16[256,512]{1,0:T(8,128)(2,1)S(1)} %copy-done.13), channel_id=1, source_target_pairs={{8,0},{16,8},{24,16},{32,24},{40,32},{48,40},{56,48},{0,56},{72,64... | collective-permute-start | bytes 786440 | tf_op jit(solution)/shard_map/ppermute | solution.py:30
  18.4 2.2 %collective-permute-done.2.refs_1_ = bf16[256,768]{1,0:T(8,128)(2,1)S(1)} collective-permute-done((bf16[256,768]{1,0:T(8,128)(2,1)S(1)}, bf16[256,768]{1,0:T(8,128)(2,1)S(1)}, u32[]{:S(2)}, u32[]{:S(2)}) %collective-permute-start.2) | collective-permute-done | bytes 393248 | tf_op jit(solution)/shard_map/ppermute | solution.py:35
  20.6 3.4 %collective-permute-start.5 = (bf16[256,768]{1,0:T(8,128)(2,1)S(1)}, bf16[256,768]{1,0:T(8,128)(2,1)S(1)}, u32[]{:S(2)}, u32[]{:S(2)}) collective-permute-start(bf16[256,768]{1,0:T(8,128)(2,1)S(1)} %collective-permute-done.2.refs_1_), channel_id=1, source_target_pairs={{64,0},{72,8},{80,16},{88,24},{96,32},{104,40},{112,48},{120,56},{... | collective-permute-start | bytes 1179656 | tf_op jit(solution)/shard_map/ppermute | solution.py:35
  24.0 2.2 %collective-permute-done.1.refs_1_ = bf16[256,512]{1,0:T(8,128)(2,1)S(1)} collective-permute-done((bf16[256,512]{1,0:T(8,128)(2,1)S(1)}, bf16[256,512]{1,0:T(8,128)(2,1)S(1)}, u32[]{:S(2)}, u32[]{:S(2)}) %collective-permute-start.1) | collective-permute-done | bytes 262176 | tf_op jit(solution)/shard_map/ppermute | solution.py:30
  26.2 3.5 %collective-permute-start.7 = (bf16[256,512]{1,0:T(8,128)(2,1)S(1)}, bf16[256,512]{1,0:T(8,128)(2,1)S(1)}, u32[]{:S(2)}, u32[]{:S(2)}) collective-permute-start(bf16[256,512]{1,0:T(8,128)(2,1)S(1)} %collective-permute-done.refs_0_), channel_id=1, source_target_pairs={{8,0},{16,8},{24,16},{32,24},{40,32},{48,40},{56,48},{0,56},{72,64... | collective-permute-start | bytes 786440 | tf_op jit(solution)/shard_map/ppermute | solution.py:30
  29.7 1.9 %shard_map.74 = bf16[512,512]{1,0:T(8,128)(2,1)} custom-call(bf16[256,512]{1,0:T(8,128)(2,1)} %copy-done.22, bf16[256,512]{1,0:T(8,128)(2,1)} %copy-done.23), custom_call_target="tpu_custom_call" | custom-call | tf_op jit(solution)/shard_map/pallas_call | solution.py:79
  31.6 1.9 %collective-permute-done.7.refs_0_ = bf16[256,512]{1,0:T(8,128)(2,1)S(1)} collective-permute-done((bf16[256,512]{1,0:T(8,128)(2,1)S(1)}, bf16[256,512]{1,0:T(8,128)(2,1)S(1)}, u32[]{:S(2)}, u32[]{:S(2)}) %collective-permute-start.7) | collective-permute-done | bytes 262176 | tf_op jit(solution)/shard_map/ppermute | solution.py:30
  33.5 3.2 %collective-permute-done.8.refs_1_ = bf16[256,512]{1,0:T(8,128)(2,1)S(1)} collective-permute-done((bf16[256,512]{1,0:T(8,128)(2,1)S(1)}, bf16[256,512]{1,0:T(8,128)(2,1)S(1)}, u32[]{:S(2)}, u32[]{:S(2)}) %collective-permute-start.8) | collective-permute-done | bytes 262176 | tf_op jit(solution)/shard_map/ppermute | solution.py:30
  36.8 0.4 collective-permute-start.9
  37.1 1.2 collective-permute-start.10
  38.3 1.7 collective-permute-start.4
  40.0 4.4 %collective-permute-done.6 = bf16[512,512]{1,0:T(8,128)(2,1)S(1)} collective-permute-done((bf16[512,512]{1,0:T(8,128)(2,1)}, bf16[512,512]{1,0:T(8,128)(2,1)S(1)}, u32[]{:S(2)}, u32[]{:S(2)}) %collective-permute-start.6) | collective-permute-done | bytes 524320 | tf_op jit(solution)/shard_map/ppermute | solution.py:35
  44.5 2.5 %collective-permute-start.11 = (bf16[256,512]{1,0:T(8,128)(2,1)}, bf16[256,512]{1,0:T(8,128)(2,1)}, u32[]{:S(2)}, u32[]{:S(2)}) collective-permute-start(bf16[256,512]{1,0:T(8,128)(2,1)} %collective-permute-done.9.refs_2_), channel_id=1, source_target_pairs={{8,0},{16,8},{24,16},{32,24},{40,32},{48,40},{56,48},{0,56},{72,64... | collective-permute-start | bytes 786440 | tf_op jit(solution)/shard_map/ppermute | solution.py:30
  47.0 2.2 %shard_map.76.refs_0_ = bf16[1024,256]{1,0:T(8,128)(2,1)} custom-call(bf16[256,768]{1,0:T(8,128)(2,1)} %copy-done.8, bf16[256,768]{1,0:T(8,128)(2,1)} %copy-done.9, bf16[256,768]{1,0:T(8,128)(2,1)} %copy-done.6, bf16[256,768]{1,0:T(8,128)(2,1)} %copy-done.11), custom_call_target="tpu_custom_call" | custom-call | tf_op jit(solution)/shard_map/pallas_call | solution.py:79
  49.2 1.4 collective-permute-done.11.refs_4_
  50.6 3.4 %collective-permute-start.14 = (bf16[1024,256]{1,0:T(8,128)(2,1)}, bf16[1024,256]{1,0:T(8,128)(2,1)S(1)}, u32[]{:S(2)}, u32[]{:S(2)}) collective-permute-start(bf16[1024,256]{1,0:T(8,128)(2,1)} %shard_map.76.refs_0_), channel_id=1, source_target_pairs={{8,0},{16,8},{24,16},{32,24},{40,32},{48,40},{56,48},{0,56},{72,64... | collective-permute-start | bytes 1572872 | tf_op jit(solution)/shard_map/ppermute | solution.py:30
  54.0 0.1 add.82
  54.1 0.7 add.83
  54.7 2.5 %shard_map.75 = bf16[1280,512]{1,0:T(8,128)(2,1)} custom-call(bf16[256,512]{1,0:T(8,128)(2,1)} %copy-done.19, bf16[256,512]{1,0:T(8,128)(2,1)} %copy-done.20, bf16[256,512]{1,0:T(8,128)(2,1)} %collective-permute-done.9.refs_2_, bf16[256,512]{1,0:T(8,128)(2,1)} %copy-done.21, bf16[256,512]{1,0:T(8,128)(2,1)} %collective-permute-done.11.refs_4_), custom_call_target="tpu_custom_call" | custom-call | tf_op jit(solution)/shard_map/pallas_call | solution.py:79
  57.2 0.9 collective-permute-start.12
  58.1 0.5 collective-permute-start.13
  58.7 7.9 %all-gather.2.cloned.1.call-done.tok_ref = bf16[512,8320]{1,0:T(8,128)(2,1)} async-done(((bf16[64,8320]{1,0:T(8,128)(2,1)}), bf16[512,8320]{1,0:T(8,128)(2,1)}) %all-gather.2.cloned.1.call-update) | async-done | bytes 8519696 | tf_op jit(solution)/shard_map/all_gather | solution.py:285
  66.6 1.1 fusion.22
  67.7 0.1 reshape.121
  67.8 3.1 %collective-permute-start.17 = (bf16[1024,256]{1,0:T(8,128)(2,1)S(1)}, bf16[1024,256]{1,0:T(8,128)(2,1)S(1)}, u32[]{:S(2)}, u32[]{:S(2)}) collective-permute-start(bf16[1024,256]{1,0:T(8,128)(2,1)S(1)} %collective-permute-done.14.refs_1_), channel_id=1, source_target_pairs={{8,0},{16,8},{24,16},{32,24},{40,32},{48,40},{56,48},{0,56},{72,64... | collective-permute-start | bytes 1572872 | tf_op jit(solution)/shard_map/ppermute | solution.py:30
  70.9 2.6 %fusion.17 = f32[512,512]{1,0:T(8,128)} fusion(bf16[512,512]{1,0:T(8,128)(2,1)} %copy-done.17, bf16[512,8320]{1,0:T(8,128)(2,1)} %all-gather.2.cloned.1.call-done.tok_ref), kind=kOutput, calls=%fused_computation.21 | convolution fusion | flops 268435456 | bytes 2097152 | tf_op jit(solution)/shard_map/dot_general | solution.py:89
  73.5 2.2 %fusion.23 = f32[512,512]{1,0:T(8,128)} fusion(bf16[256,768]{1,0:T(8,128)(2,1)S(1)} %copy-done.12, bf16[512,8320]{1,0:T(8,128)(2,1)} %all-gather.2.cloned.1.call-done.tok_ref), kind=kOutput, calls=%fused_computation.29 | convolution fusion | flops 134217728 | bytes 1572864 | tf_op jit(solution)/shard_map/dot_general | solution.py:89
  75.8 1.2 fusion.28
  77.0 2.3 %fusion.31 = f32[512,512]{1,0:T(8,128)} fusion(bf16[256,512]{1,0:T(8,128)(2,1)S(1)} %copy-done.14, bf16[512,8320]{1,0:T(8,128)(2,1)} %all-gather.2.cloned.1.call-done.tok_ref), kind=kOutput, calls=%fused_computation.37 | convolution fusion | flops 134217728 | bytes 1572864 | tf_op jit(solution)/shard_map/dot_general | solution.py:89
  79.3 0.3 convert_reduce_fusion.1
  79.6 0.1 reduce_sum.12
  79.7 1.8 fusion.19
  81.5 1.8 %fusion.4 = f32[512,512]{1,0:T(8,128)S(1)} fusion(f32[512,512]{1,0:T(8,128)S(1)} %fusion.19, f32[512,512]{1,0:T(8,128)S(1)} %fusion.28, f32[512,512]{1,0:T(8,128)S(1)} %copy-done.3, bf16[512,512]{1,0:T(8,128)(2,1)} %shard_map.74, bf16[512,8320]{1,0:T(8,128)(2,1)} %all-gather.2.cloned.1.call-done.tok_ref), kind=kOutput, calls=%fused_computation.8 | convolution fusion | flops 269221888 | bytes 5242880 | tf_op jit(solution)/shard_map/dot_general | solution.py:89
  83.4 1.7 fusion.6
  85.1 3.9 %collective-permute-done.13 = bf16[1280,512]{1,0:T(8,128)(2,1)} collective-permute-done((bf16[1280,512]{1,0:T(8,128)(2,1)}, bf16[1280,512]{1,0:T(8,128)(2,1)}, u32[]{:S(2)}, u32[]{:S(2)}) %collective-permute-start.13) | collective-permute-done | bytes 1310752 | tf_op jit(solution)/shard_map/ppermute | solution.py:35
  89.0 1.1 slice.72
  90.1 0.4 collective-permute-start.19
  90.5 1.1 slice.73
  91.7 1.2 collective-permute-start.20
  92.9 1.5 collective-permute-start.22
  94.3 2.2 %fusion.8 = f32[512,512]{1,0:T(8,128)S(1)} fusion(bf16[1280,512]{1,0:T(8,128)(2,1)} %collective-permute-done.13, bf16[512,8320]{1,0:T(8,128)(2,1)S(1)} %copy-done), kind=kOutput, calls=%fused_computation.14 | convolution fusion | flops 671088640 | bytes 3670016 | tf_op jit(solution)/shard_map/dot_general | solution.py:89
  96.5 2.2 %fusion.10 = f32[512,512]{1,0:T(8,128)S(1)} fusion(bf16[1280,512]{1,0:T(8,128)(2,1)} %collective-permute-done.12, bf16[512,8320]{1,0:T(8,128)(2,1)S(1)} %copy-done), kind=kOutput, calls=%fused_computation.16 | convolution fusion | flops 671088640 | bytes 3670016 | tf_op jit(solution)/shard_map/dot_general | solution.py:89
  98.8 2.1 %shard_map.77.kv_ref = f32[512,256]{1,0:T(8,128)S(1)} custom-call(bf16[512,8320]{1,0:T(8,128)(2,1)S(1)} %copy-done, bf16[1024,256]{1,0:T(8,128)(2,1)S(1)} %copy-done.1, bf16[1024,256]{1,0:T(8,128)(2,1)S(1)} %collective-permute-done.14.refs_1_, bf16[1024,256]{1,0:T(8,128)(2,1)S(1)} %collective-permute-done.15.refs_2_, ...), custom_call_target="tpu_custom_call" | custom-call | tf_op jit(solution)/shard_map/pallas_call | solution.py:147
  100.9 0.9 fusion.13
  101.8 0.6 collective-permute-done.22.rm3
  102.4 0.7 collective-permute-start.23
  103.1 0.8 collective-permute-start.24
  104.0 0.4 convolution_add_fusion.q_ref
  104.4 1.1 collective-permute-done.20.f2b
  105.5 4.1 %collective-permute-done.23.ends0 = bf16[512,256]{1,0:T(8,128)(2,1)S(1)} collective-permute-done((bf16[512,256]{1,0:T(8,128)(2,1)S(1)}, bf16[512,256]{1,0:T(8,128)(2,1)S(1)}, u32[]{:S(2)}, u32[]{:S(2)}) %collective-permute-start.23) | collective-permute-done | bytes 262176 | tf_op jit(solution)/shard_map/ppermute | solution.py:30
  109.6 1.3 collective-permute-done.24.ends1
  110.9 4.7 %shard_map.78 = bf16[768,768]{1,0:T(8,128)(2,1)} custom-call(bf16[512,8320]{1,0:T(8,128)(2,1)S(1)} %copy-done, s32[1,512]{1,0:T(1,128)S(1)} %add_add_fusion.slot_ref, f32[512,512]{1,0:T(8,128)S(1)} %convolution_add_fusion.q_ref, f32[512,256]{1,0:T(8,128)S(1)} %shard_map.77.kv_ref, bf16[640,512]{1,0:T(8,128)(2,1)S(1)} %collective-permute-done.19.f2a, ...), custom_call_target="tpu_custom_call" | custom-call | tf_op jit(solution)/shard_map/pallas_call | solution.py:193
  115.6 6.8 %all-to-all-start = ((bf16[32,24,768]{2,1,0:T(8,128)(2,1)}), bf16[32,24,768]{2,1,0:T(8,128)(2,1)S(1)}, u32[]{:S(2)}, u32[]{:S(2)}) async-start(bf16[32,24,768]{2,1,0:T(8,128)(2,1)} %bitcast.2), calls=%async_computation | async-start | bytes 2359296 | tf_op jit(solution)/shard_map/all_to_all | solution.py:290
  122.4 0.1 copy.11.segq_ref
  122.7 1.0 fusion.35
  123.6 0.2 pad_maximum_fusion
  123.9 0.3 fusion.ahead_ref
  124.2 19.8 %all-to-all-done = bf16[32,24,768]{2,1,0:T(8,128)(2,1)S(1)} async-done(((bf16[32,24,768]{2,1,0:T(8,128)(2,1)}), bf16[32,24,768]{2,1,0:T(8,128)(2,1)S(1)}, u32[]{:S(2)}, u32[]{:S(2)}) %all-to-all-start) | async-done | bytes 1179680 | tf_op jit(solution)/shard_map/all_to_all | solution.py:290
  144.0 5.0 %shard_map.79 = bf16[512,512]{1,0:T(8,128)(2,1)S(1)} custom-call(bf16[768,768]{1,0:T(8,128)(2,1)S(1)} %bitcast.17, bf16[768,768]{1,0:T(8,128)(2,1)S(1)} %fusion.ahead_ref, s32[512,1]{1,0:T(8,128)S(1)} %copy.11.segq_ref, s32[1,640]{1,0:T(1,128)S(1)} %broadcast_in_dim.11.segk_ref, f32[512,128]{1,0:T(8,128)S(1)} %get-tuple-element.42.cos_ref, ...), custom_call_target="tpu_custom_call" | custom-call | tf_op jit(solution)/shard_map/pallas_call | solution.py:254
  149.0 22.5 %all_to_all.21 = bf16[8,64,512]{2,1,0:T(8,128)(2,1)S(1)} all-to-all(bf16[8,64,512]{2,1,0:T(8,128)(2,1)S(1)} %bitcast.18), channel_id=1, replica_groups=mesh['dp'=32,'seq'=8] {'seq'}, dimensions={0} | all-to-all | bytes 1048576 | tf_op jit(solution)/shard_map/all_to_all | solution.py:297
  171.5 0.3 copy.12
  171.8 1.0 broadcast_in_dim.12
  (92 shorter events, 0.4 us)
Async XLA Ops:
  6.5 2.8 %copy-start.13 = (bf16[256,512]{1,0:T(8,128)(2,1)S(1)}, bf16[256,512]{1,0:T(8,128)(2,1)}, u32[]{:S(2)}) copy-start(bf16[256,512]{1,0:T(8,128)(2,1)} %param.11) | copy-start | bytes 786436
  6.5 2.8 %copy-start.24 = (bf16[256,128]{1,0:T(8,128)(2,1)S(1)}, bf16[256,128]{1,0:T(8,128)(2,1)}, u32[]{:S(2)}) copy-start(bf16[256,128]{1,0:T(8,128)(2,1)} %param.12) | copy-start | bytes 196612
  6.5 2.9 %copy-start.25 = (bf16[256,128]{1,0:T(8,128)(2,1)S(1)}, bf16[256,128]{1,0:T(8,128)(2,1)}, u32[]{:S(2)}) copy-start(bf16[256,128]{1,0:T(8,128)(2,1)} %param.13) | copy-start | bytes 196612
  6.5 60.0 %all-gather.2.cloned.1.call-start = ((), (), s32[]{:S(2)}) async-start(), calls=%async_computation.2 | async-start | bytes 9584640 | tf_op jit(solution)/shard_map/all_gather | solution.py:285
  9.4 37.5 %copy-start.8 = (bf16[256,768]{1,0:T(8,128)(2,1)}, bf16[256,768]{1,0:T(8,128)(2,1)S(1)}, u32[]{:S(2)}) copy-start(bf16[256,768]{1,0:T(8,128)(2,1)S(1)} %constant_dynamic-update-slice_fusion.refs_0_) | copy-start | bytes 1179652
  9.5 11.2 %collective-permute-start.2 = (bf16[256,768]{1,0:T(8,128)(2,1)S(1)}, bf16[256,768]{1,0:T(8,128)(2,1)S(1)}, u32[]{:S(2)}, u32[]{:S(2)}) collective-permute-start(bf16[256,768]{1,0:T(8,128)(2,1)S(1)} %constant_dynamic-update-slice_fusion.refs_0_), channel_id=1, source_target_pairs={{64,0},{72,8},{80,16},{88,24},{96,32},{104,40},{112,48},{120,56},{... | collective-permute-start | bytes 1179656 | tf_op jit(solution)/shard_map/ppermute | solution.py:35
  12.8 13.4 %collective-permute-start.3 = (bf16[256,768]{1,0:T(8,128)(2,1)S(1)}, bf16[256,768]{1,0:T(8,128)(2,1)S(1)}, u32[]{:S(2)}, u32[]{:S(2)}) collective-permute-start(bf16[256,768]{1,0:T(8,128)(2,1)S(1)} %constant_dynamic-update-slice_fusion.refs_0_), channel_id=1, source_target_pairs={{192,0},{200,8},{208,16},{216,24},{224,32},{232,40},{240,48},{248,... | collective-permute-start | bytes 1179656 | tf_op jit(solution)/shard_map/ppermute | solution.py:35
  12.8 11.2 %collective-permute-start = (bf16[256,512]{1,0:T(8,128)(2,1)S(1)}, bf16[256,512]{1,0:T(8,128)(2,1)S(1)}, u32[]{:S(2)}, u32[]{:S(2)}) collective-permute-start(bf16[256,512]{1,0:T(8,128)(2,1)S(1)} %copy-done.13), channel_id=1, source_target_pairs={{8,0},{16,8},{24,16},{32,24},{40,32},{48,40},{56,48},{0,56},{72,64... | collective-permute-start | bytes 786440 | tf_op jit(solution)/shard_map/ppermute | solution.py:30
  18.4 7.8 %collective-permute-start.1 = (bf16[256,512]{1,0:T(8,128)(2,1)S(1)}, bf16[256,512]{1,0:T(8,128)(2,1)S(1)}, u32[]{:S(2)}, u32[]{:S(2)}) collective-permute-start(bf16[256,512]{1,0:T(8,128)(2,1)S(1)} %copy-done.13), channel_id=1, source_target_pairs={{56,0},{0,8},{8,16},{16,24},{24,32},{32,40},{40,48},{48,56},{120,6... | collective-permute-start | bytes 786440 | tf_op jit(solution)/shard_map/ppermute | solution.py:30
  20.6 26.3 %copy-start.9 = (bf16[256,768]{1,0:T(8,128)(2,1)}, bf16[256,768]{1,0:T(8,128)(2,1)S(1)}, u32[]{:S(2)}) copy-start(bf16[256,768]{1,0:T(8,128)(2,1)S(1)} %collective-permute-done.2.refs_1_) | copy-start | bytes 1179652
  20.6 16.1 %collective-permute-start.5 = (bf16[256,768]{1,0:T(8,128)(2,1)S(1)}, bf16[256,768]{1,0:T(8,128)(2,1)S(1)}, u32[]{:S(2)}, u32[]{:S(2)}) collective-permute-start(bf16[256,768]{1,0:T(8,128)(2,1)S(1)} %collective-permute-done.2.refs_1_), channel_id=1, source_target_pairs={{64,0},{72,8},{80,16},{88,24},{96,32},{104,40},{112,48},{120,56},{... | collective-permute-start | bytes 1179656 | tf_op jit(solution)/shard_map/ppermute | solution.py:35
  24.0 5.7 %copy-start.22 = (bf16[256,512]{1,0:T(8,128)(2,1)}, bf16[256,512]{1,0:T(8,128)(2,1)S(1)}, u32[]{:S(2)}) copy-start(bf16[256,512]{1,0:T(8,128)(2,1)S(1)} %collective-permute-done.refs_0_) | copy-start | bytes 786436
  26.2 3.5 %copy-start.23 = (bf16[256,512]{1,0:T(8,128)(2,1)}, bf16[256,512]{1,0:T(8,128)(2,1)S(1)}, u32[]{:S(2)}) copy-start(bf16[256,512]{1,0:T(8,128)(2,1)S(1)} %collective-permute-done.1.refs_1_) | copy-start | bytes 786436
  26.2 20.7 %copy-start.11 = (bf16[256,768]{1,0:T(8,128)(2,1)}, bf16[256,768]{1,0:T(8,128)(2,1)S(1)}, u32[]{:S(2)}) copy-start(bf16[256,768]{1,0:T(8,128)(2,1)S(1)} %collective-permute-done.3.refs_3_) | copy-start | bytes 1179652
  26.2 7.3 %collective-permute-start.7 = (bf16[256,512]{1,0:T(8,128)(2,1)S(1)}, bf16[256,512]{1,0:T(8,128)(2,1)S(1)}, u32[]{:S(2)}, u32[]{:S(2)}) collective-permute-start(bf16[256,512]{1,0:T(8,128)(2,1)S(1)} %collective-permute-done.refs_0_), channel_id=1, source_target_pairs={{8,0},{16,8},{24,16},{32,24},{40,32},{48,40},{56,48},{0,56},{72,64... | collective-permute-start | bytes 786440 | tf_op jit(solution)/shard_map/ppermute | solution.py:30
  29.7 7.0 %collective-permute-start.8 = (bf16[256,512]{1,0:T(8,128)(2,1)S(1)}, bf16[256,512]{1,0:T(8,128)(2,1)S(1)}, u32[]{:S(2)}, u32[]{:S(2)}) collective-permute-start(bf16[256,512]{1,0:T(8,128)(2,1)S(1)} %collective-permute-done.1.refs_1_), channel_id=1, source_target_pairs={{56,0},{0,8},{8,16},{16,24},{24,32},{32,40},{40,48},{48,56},{120,6... | collective-permute-start | bytes 786440 | tf_op jit(solution)/shard_map/ppermute | solution.py:30
  31.6 12.8 %collective-permute-start.6 = (bf16[512,512]{1,0:T(8,128)(2,1)}, bf16[512,512]{1,0:T(8,128)(2,1)S(1)}, u32[]{:S(2)}, u32[]{:S(2)}) collective-permute-start(bf16[512,512]{1,0:T(8,128)(2,1)} %shard_map.74), channel_id=1, source_target_pairs={{192,0},{200,8},{208,16},{216,24},{224,32},{232,40},{240,48},{248,... | collective-permute-start | bytes 1572872 | tf_op jit(solution)/shard_map/ppermute | solution.py:35
  33.5 17.1 %copy-start.19 = (bf16[256,512]{1,0:T(8,128)(2,1)}, bf16[256,512]{1,0:T(8,128)(2,1)S(1)}, u32[]{:S(2)}) copy-start(bf16[256,512]{1,0:T(8,128)(2,1)S(1)} %collective-permute-done.7.refs_0_) | copy-start | bytes 786436
  36.7 10.2 %copy-start.20 = (bf16[256,512]{1,0:T(8,128)(2,1)}, bf16[256,512]{1,0:T(8,128)(2,1)S(1)}, u32[]{:S(2)}) copy-start(bf16[256,512]{1,0:T(8,128)(2,1)S(1)} %collective-permute-done.8.refs_1_) | copy-start | bytes 786436
  36.7 10.2 %copy-start.6 = (bf16[256,768]{1,0:T(8,128)(2,1)}, bf16[256,768]{1,0:T(8,128)(2,1)S(1)}, u32[]{:S(2)}) copy-start(bf16[256,768]{1,0:T(8,128)(2,1)S(1)} %collective-permute-done.5.refs_2_) | copy-start | bytes 1179652
  36.8 7.7 %collective-permute-start.9 = (bf16[256,512]{1,0:T(8,128)(2,1)S(1)}, bf16[256,512]{1,0:T(8,128)(2,1)}, u32[]{:S(2)}, u32[]{:S(2)}) collective-permute-start(bf16[256,512]{1,0:T(8,128)(2,1)S(1)} %collective-permute-done.7.refs_0_), channel_id=1, source_target_pairs={{8,0},{16,8},{24,16},{32,24},{40,32},{48,40},{56,48},{0,56},{72,64... | collective-permute-start | bytes 786440 | tf_op jit(solution)/shard_map/ppermute | solution.py:30
  37.1 7.3 %collective-permute-start.10 = (bf16[256,512]{1,0:T(8,128)(2,1)S(1)}, bf16[256,512]{1,0:T(8,128)(2,1)S(1)}, u32[]{:S(2)}, u32[]{:S(2)}) collective-permute-start(bf16[256,512]{1,0:T(8,128)(2,1)S(1)} %collective-permute-done.8.refs_1_), channel_id=1, source_target_pairs={{56,0},{0,8},{8,16},{16,24},{24,32},{32,40},{40,48},{48,56},{120,6... | collective-permute-start | bytes 786440 | tf_op jit(solution)/shard_map/ppermute | solution.py:30
  38.3 10.9 %collective-permute-start.4 = (bf16[512,512]{1,0:T(8,128)(2,1)}, bf16[512,512]{1,0:T(8,128)(2,1)S(1)}, u32[]{:S(2)}, u32[]{:S(2)}) collective-permute-start(bf16[512,512]{1,0:T(8,128)(2,1)} %shard_map.74), channel_id=1, source_target_pairs={{64,0},{72,8},{80,16},{88,24},{96,32},{104,40},{112,48},{120,56},{... | collective-permute-start | bytes 1572872 | tf_op jit(solution)/shard_map/ppermute | solution.py:35
  44.4 23.4 %copy-start.17 = (bf16[512,512]{1,0:T(8,128)(2,1)}, bf16[512,512]{1,0:T(8,128)(2,1)S(1)}, u32[]{:S(2)}) copy-start(bf16[512,512]{1,0:T(8,128)(2,1)S(1)} %collective-permute-done.6) | copy-start | bytes 1572868
  44.5 2.5 %copy-start.21 = (bf16[256,512]{1,0:T(8,128)(2,1)}, bf16[256,512]{1,0:T(8,128)(2,1)S(1)}, u32[]{:S(2)}) copy-start(bf16[256,512]{1,0:T(8,128)(2,1)S(1)} %collective-permute-done.10.refs_3_) | copy-start | bytes 786436
  44.5 6.1 %collective-permute-start.11 = (bf16[256,512]{1,0:T(8,128)(2,1)}, bf16[256,512]{1,0:T(8,128)(2,1)}, u32[]{:S(2)}, u32[]{:S(2)}) collective-permute-start(bf16[256,512]{1,0:T(8,128)(2,1)} %collective-permute-done.9.refs_2_), channel_id=1, source_target_pairs={{8,0},{16,8},{24,16},{32,24},{40,32},{48,40},{56,48},{0,56},{72,64... | collective-permute-start | bytes 786440 | tf_op jit(solution)/shard_map/ppermute | solution.py:30
  49.2 18.6 %collective-permute-start.16 = (bf16[512,512]{1,0:T(8,128)(2,1)S(1)}, bf16[512,512]{1,0:T(8,128)(2,1)S(1)}, u32[]{:S(2)}, u32[]{:S(2)}) collective-permute-start(bf16[512,512]{1,0:T(8,128)(2,1)S(1)} %collective-permute-done.6), channel_id=1, source_target_pairs={{192,0},{200,8},{208,16},{216,24},{224,32},{232,40},{240,48},{248,... | collective-permute-start | bytes 1572872 | tf_op jit(solution)/shard_map/ppermute | solution.py:35
  49.2 18.6 %copy-start.18 = (bf16[512,512]{1,0:T(8,128)(2,1)}, bf16[512,512]{1,0:T(8,128)(2,1)S(1)}, u32[]{:S(2)}) copy-start(bf16[512,512]{1,0:T(8,128)(2,1)S(1)} %collective-permute-done.4) | copy-start | bytes 1572868
  50.6 17.2 %collective-permute-start.14 = (bf16[1024,256]{1,0:T(8,128)(2,1)}, bf16[1024,256]{1,0:T(8,128)(2,1)S(1)}, u32[]{:S(2)}, u32[]{:S(2)}) collective-permute-start(bf16[1024,256]{1,0:T(8,128)(2,1)} %shard_map.76.refs_0_), channel_id=1, source_target_pairs={{8,0},{16,8},{24,16},{32,24},{40,32},{48,40},{56,48},{0,56},{72,64... | collective-permute-start | bytes 1572872 | tf_op jit(solution)/shard_map/ppermute | solution.py:30
  54.0 13.8 %collective-permute-start.15 = (bf16[1024,256]{1,0:T(8,128)(2,1)}, bf16[1024,256]{1,0:T(8,128)(2,1)S(1)}, u32[]{:S(2)}, u32[]{:S(2)}) collective-permute-start(bf16[1024,256]{1,0:T(8,128)(2,1)} %shard_map.76.refs_0_), channel_id=1, source_target_pairs={{56,0},{0,8},{8,16},{16,24},{24,32},{32,40},{40,48},{48,56},{120,6... | collective-permute-start | bytes 1572872 | tf_op jit(solution)/shard_map/ppermute | solution.py:30
  54.7 18.8 %copy-start.12 = (bf16[256,768]{1,0:T(8,128)(2,1)S(1)}, bf16[256,768]{1,0:T(8,128)(2,1)}, u32[]{:S(2)}) copy-start(bf16[256,768]{1,0:T(8,128)(2,1)} %copy-done.11) | copy-start | bytes 1179652
  57.2 18.5 %copy-start.10 = (bf16[256,768]{1,0:T(8,128)(2,1)S(1)}, bf16[256,768]{1,0:T(8,128)(2,1)}, u32[]{:S(2)}) copy-start(bf16[256,768]{1,0:T(8,128)(2,1)} %copy-done.9) | copy-start | bytes 1179652
  57.2 27.8 %collective-permute-start.12 = (bf16[1280,512]{1,0:T(8,128)(2,1)}, bf16[1280,512]{1,0:T(8,128)(2,1)}, u32[]{:S(2)}, u32[]{:S(2)}) collective-permute-start(bf16[1280,512]{1,0:T(8,128)(2,1)} %shard_map.75), channel_id=1, source_target_pairs={{64,0},{72,8},{80,16},{88,24},{96,32},{104,40},{112,48},{120,56},{... | collective-permute-start | bytes 3932168 | tf_op jit(solution)/shard_map/ppermute | solution.py:35
  58.1 30.8 %collective-permute-start.13 = (bf16[1280,512]{1,0:T(8,128)(2,1)}, bf16[1280,512]{1,0:T(8,128)(2,1)}, u32[]{:S(2)}, u32[]{:S(2)}) collective-permute-start(bf16[1280,512]{1,0:T(8,128)(2,1)} %shard_map.75), channel_id=1, source_target_pairs={{192,0},{200,8},{208,16},{216,24},{224,32},{232,40},{240,48},{248,... | collective-permute-start | bytes 3932168 | tf_op jit(solution)/shard_map/ppermute | solution.py:35
  67.8 9.2 %copy-start.14 = (bf16[256,512]{1,0:T(8,128)(2,1)S(1)}, bf16[256,512]{1,0:T(8,128)(2,1)}, u32[]{:S(2)}) copy-start(bf16[256,512]{1,0:T(8,128)(2,1)} %param.11) | copy-start | bytes 786436
  67.8 5.8 %copy-start.15 = (bf16[512,512]{1,0:T(8,128)(2,1)}, bf16[512,512]{1,0:T(8,128)(2,1)S(1)}, u32[]{:S(2)}) copy-start(bf16[512,512]{1,0:T(8,128)(2,1)S(1)} %collective-permute-done.16) | copy-start | bytes 1572868
  67.8 21.2 %collective-permute-start.17 = (bf16[1024,256]{1,0:T(8,128)(2,1)S(1)}, bf16[1024,256]{1,0:T(8,128)(2,1)S(1)}, u32[]{:S(2)}, u32[]{:S(2)}) collective-permute-start(bf16[1024,256]{1,0:T(8,128)(2,1)S(1)} %collective-permute-done.14.refs_1_), channel_id=1, source_target_pairs={{8,0},{16,8},{24,16},{32,24},{40,32},{48,40},{56,48},{0,56},{72,64... | collective-permute-start | bytes 1572872 | tf_op jit(solution)/shard_map/ppermute | solution.py:30
  70.9 18.1 %collective-permute-start.18 = (bf16[1024,256]{1,0:T(8,128)(2,1)S(1)}, bf16[1024,256]{1,0:T(8,128)(2,1)S(1)}, u32[]{:S(2)}, u32[]{:S(2)}) collective-permute-start(bf16[1024,256]{1,0:T(8,128)(2,1)S(1)} %collective-permute-done.15.refs_2_), channel_id=1, source_target_pairs={{56,0},{0,8},{8,16},{16,24},{24,32},{32,40},{40,48},{48,56},{120,6... | collective-permute-start | bytes 1572872 | tf_op jit(solution)/shard_map/ppermute | solution.py:30
  79.7 1.8 %copy-start.3 = (f32[512,512]{1,0:T(8,128)S(1)}, f32[512,512]{1,0:T(8,128)}, u32[]{:S(2)}) copy-start(f32[512,512]{1,0:T(8,128)} %fusion.31) | copy-start | bytes 3145732
  79.7 3.6 %copy-start.27 = (s32[1,512]{1,0:T(1,128)S(1)}, s32[1,512]{1,0:T(1,128)}, u32[]{:S(2)}) copy-start(s32[1,512]{1,0:T(1,128)} %add.83) | copy-start | bytes 6148
  79.7 3.7 %copy-start.4 = (f32[512,512]{1,0:T(8,128)S(1)}, f32[512,512]{1,0:T(8,128)}, u32[]{:S(2)}) copy-start(f32[512,512]{1,0:T(8,128)} %fusion.17) | copy-start | bytes 3145732
  79.7 3.7 %copy-start.5 = (f32[512,512]{1,0:T(8,128)S(1)}, f32[512,512]{1,0:T(8,128)}, u32[]{:S(2)}) copy-start(f32[512,512]{1,0:T(8,128)} %fusion.23) | copy-start | bytes 3145732
  79.7 3.7 %copy-start.7 = (bf16[256,768]{1,0:T(8,128)(2,1)S(1)}, bf16[256,768]{1,0:T(8,128)(2,1)}, u32[]{:S(2)}) copy-start(bf16[256,768]{1,0:T(8,128)(2,1)} %copy-done.6) | copy-start | bytes 1179652
  81.5 12.8 %copy-start = (bf16[512,8320]{1,0:T(8,128)(2,1)S(1)}, bf16[512,8320]{1,0:T(8,128)(2,1)}, u32[]{:S(2)}) copy-start(bf16[512,8320]{1,0:T(8,128)(2,1)} %all-gather.2.cloned.1.call-done.tok_ref) | copy-start | bytes 25559044
  90.1 14.3 %collective-permute-start.19 = (bf16[640,512]{1,0:T(8,128)(2,1)S(1)}, bf16[640,512]{1,0:T(8,128)(2,1)S(1)}, u32[]{:S(2)}, u32[]{:S(2)}) collective-permute-start(bf16[640,512]{1,0:T(8,128)(2,1)S(1)} %slice.72), channel_id=1, source_target_pairs={{64,0},{72,8},{80,16},{88,24},{96,32},{104,40},{112,48},{120,56},{... | collective-permute-start | bytes 1966088 | tf_op jit(solution)/shard_map/ppermute | solution.py:35
  91.7 13.9 %collective-permute-start.20 = (bf16[640,512]{1,0:T(8,128)(2,1)S(1)}, bf16[640,512]{1,0:T(8,128)(2,1)S(1)}, u32[]{:S(2)}, u32[]{:S(2)}) collective-permute-start(bf16[640,512]{1,0:T(8,128)(2,1)S(1)} %slice.73), channel_id=1, source_target_pairs={{192,0},{200,8},{208,16},{216,24},{224,32},{232,40},{240,48},{248,... | collective-permute-start | bytes 1966088 | tf_op jit(solution)/shard_map/ppermute | solution.py:35
  92.9 8.9 %collective-permute-start.21 = (bf16[1024,256]{1,0:T(8,128)(2,1)S(1)}, bf16[1024,256]{1,0:T(8,128)(2,1)S(1)}, u32[]{:S(2)}, u32[]{:S(2)}) collective-permute-start(bf16[1024,256]{1,0:T(8,128)(2,1)S(1)} %collective-permute-done.17.refs_3_), channel_id=1, source_target_pairs={{8,0},{16,8},{24,16},{32,24},{40,32},{48,40},{56,48},{0,56},{72,64... | collective-permute-start | bytes 1572872 | tf_op jit(solution)/shard_map/ppermute | solution.py:30
  92.9 9.5 %collective-permute-start.22 = (bf16[1024,256]{1,0:T(8,128)(2,1)S(1)}, bf16[1024,256]{1,0:T(8,128)(2,1)S(1)}, u32[]{:S(2)}, u32[]{:S(2)}) collective-permute-start(bf16[1024,256]{1,0:T(8,128)(2,1)S(1)} %collective-permute-done.18.refs_4_), channel_id=1, source_target_pairs={{56,0},{0,8},{8,16},{16,24},{24,32},{32,40},{40,48},{48,56},{120,6... | collective-permute-start | bytes 1572872 | tf_op jit(solution)/shard_map/ppermute | solution.py:30
  96.5 2.2 %copy-start.1 = (bf16[1024,256]{1,0:T(8,128)(2,1)S(1)}, bf16[1024,256]{1,0:T(8,128)(2,1)}, u32[]{:S(2)}) copy-start(bf16[1024,256]{1,0:T(8,128)(2,1)} %shard_map.76.refs_0_) | copy-start | bytes 1572868
  98.7 2.1 %copy-start.2 = (bf16[1280,512]{1,0:T(8,128)(2,1)S(1)}, bf16[1280,512]{1,0:T(8,128)(2,1)}, u32[]{:S(2)}) copy-start(bf16[1280,512]{1,0:T(8,128)(2,1)} %shard_map.75) | copy-start | bytes 3932164
  100.9 3.1 %copy-start.16 = (bf16[512,512]{1,0:T(8,128)(2,1)S(1)}, bf16[512,512]{1,0:T(8,128)(2,1)}, u32[]{:S(2)}) copy-start(bf16[512,512]{1,0:T(8,128)(2,1)} %copy-done.15) | copy-start | bytes 1572868
  102.4 7.2 %collective-permute-start.23 = (bf16[512,256]{1,0:T(8,128)(2,1)S(1)}, bf16[512,256]{1,0:T(8,128)(2,1)S(1)}, u32[]{:S(2)}, u32[]{:S(2)}) collective-permute-start(bf16[512,256]{1,0:T(8,128)(2,1)S(1)} %slice.91), channel_id=1, source_target_pairs={{8,0},{16,8},{24,16},{32,24},{40,32},{48,40},{56,48},{0,56},{72,64... | collective-permute-start | bytes 786440 | tf_op jit(solution)/shard_map/ppermute | solution.py:30
  103.1 7.8 %collective-permute-start.24 = (bf16[512,256]{1,0:T(8,128)(2,1)S(1)}, bf16[512,256]{1,0:T(8,128)(2,1)S(1)}, u32[]{:S(2)}, u32[]{:S(2)}) collective-permute-start(bf16[512,256]{1,0:T(8,128)(2,1)S(1)} %slice.92), channel_id=1, source_target_pairs={{56,0},{0,8},{8,16},{16,24},{24,32},{32,40},{40,48},{48,56},{120,6... | collective-permute-start | bytes 786440 | tf_op jit(solution)/shard_map/ppermute | solution.py:30
  115.6 6.9 %copy-start.26 = (s32[1,512]{1,0:T(1,128)S(1)}, s32[1,512]{1,0:T(1,128)}, u32[]{:S(2)}) copy-start(s32[1,512]{1,0:T(1,128)} %param.9) | copy-start | bytes 6148
  115.6 28.4 %all-to-all-start = ((bf16[32,24,768]{2,1,0:T(8,128)(2,1)}), bf16[32,24,768]{2,1,0:T(8,128)(2,1)S(1)}, u32[]{:S(2)}, u32[]{:S(2)}) async-start(bf16[32,24,768]{2,1,0:T(8,128)(2,1)} %bitcast.2), calls=%async_computation | async-start | bytes 2359296 | tf_op jit(solution)/shard_map/all_to_all | solution.py:290
Sparse Core Ops, SparseCore 0:
  9.5 57.0 all-gather.1

commit v2 on v1

--- a/solution.py
+++ b/solution.py
@@ -104,26 +104,27 @@
     a, b = after((zp2, zm2), o2)
     zp3, zm3 = from_z(a, 1), from_z(b, -1)
     z4 = from_z(after(zp3, zm3, n3), 1)
-    row = after(join(own, op, o2, om, columns=cols), z4, n1)
+    far = join(zp2, zm2, zp3, zm3, z4)
+    row = after(join(own, op, o2, om, columns=cols), n1, far)
     rp1, rm1 = from_z(row, 1), from_z(row, -1)
     n2 = from_x(n3, -1)
-    far = after(join(zp2, zm2, zp3, zm3, z4), n1, n3, row)
+    far = after(far, n1, n3)
     f1, f3 = from_x(far, 1), from_x(far, -1)
-    early = [(query, 0), (near, 1), (op[:, :cols], 8), (n1, 9), (o2[:, :cols], 16), (om[:, :cols], 24), (n3, 25)]
-    q_sum = part_dots(tokens, early)
-    a, b = after((rp1, rm1), n1, n2, tokens)
+    q_sum = part_dots(tokens, [(query, 0), (near, 1), (op[:, :cols], 8), (n1, 9)])
+    a, b = after((rp1, rm1), n1, n2)
     rp2, rm2 = from_z(a, 1), from_z(b, -1)
-    a, b = after((rp2, rm2), rp2, rm2)
+    a, b = after((rp2, rm2), q_sum)
     rp3, rm3 = from_z(a, 1), from_z(b, -1)
-    f1, f3 = after((f1, f3), q_sum, rp2, rm2)
+    q_sum = q_sum + part_dots(tokens, [(o2[:, :cols], 16), (om[:, :cols], 24), (n3, 25)])
+    f1, f3 = after((f1, f3), q_sum)
     g = far.shape[0] // 2
     f2 = [from_x(f1[:g], 1), from_x(f3[g:], -1)]
+    late = after(tokens, rp3, rm3)
     kv_sum = kv_early(tokens, [row, rp1, rm1, rp2, rm2])
-    q_sum = q_sum + part_dots(tokens, [(far, 3), (f1, 11), (f3, 27)])
     h = row.shape[0] // 2
-    a, b = after((rp3[:h], rm3[h:]), kv_sum)
-    ends = [from_z(a, 1), from_z(b, -1)]
-    q_sum = q_sum + part_dots(tokens, [(n2, 17)])
+    ends = [from_z(rp3[:h], 1), from_z(rm3[h:], -1)]
+    q_sum = q_sum + part_dots(late, [(far, 3), (f3, 27)])
+    q_sum = q_sum + part_dots(after(tokens, *ends), [(f1, 11), (n2, 17)])
     return q_sum, kv_sum, f2, [rp3, rm3, *ends]
 
 

time: 180 us -> 178 us (0.989)
  starting transfers between devices: 41.1 us -> 37.7 us
    all_gather x1, waiting for transfers between devices: 7.89 us -> 0.01 us  [shards(): tokens = lax.all_gather(normed, 'seq', axis=0, tiled=True)]
    ppermute x15, waiting for transfers between devices: 14.7 us -> 18.9 us  [from_z(): return lax.ppermute(value, 'dp', pairs)]
    all_to_all x1, starting transfers between devices: 6.85 us -> 4.51 us  [shards(): lax.all_to_all(outgoing.reshape(ND, SLOTS, -1), 'dp', split_axis=0, conca...]
    ppermute x10, waiting for transfers between devices: 11.7 us -> 13.8 us  [from_x(): return lax.ppermute(value, 'dp', pairs)]
  transfers between devices with their start and end apart: 27 -> 27, of which waited for: 13 -> 13; matrix products, arithmetic and copies ran while one was open for 14% -> 15% of each run, Pallas kernels for 5% -> 5%
where the time goes in v2:
time: 178 us; the launch traced here: 177 us
  waiting for transfers between devices  52.8 us (30%)
  starting transfers between devices  37.7 us (21%)
  blocking collectives  23.7 us (13%)
  Pallas kernels  21.1 us (12%)
  matrix products  19.8 us (11%)
  between operations  13.8 us (8%)
  local copies, waits for them, and re-layouts  5.51 us (3%)
  other arithmetic  3.01 us (2%)
    all_to_all x1, blocking collectives, shards(): lax.all_to_all(context, 'seq', split_axis=0, concat_axis=1, tiled=True)  23.7 us
    ppermute x15, starting transfers between devices, from_z(): return lax.ppermute(value, 'dp', pairs)  21.5 us
    all_to_all x1, waiting for transfers between devices, shards(): lax.all_to_all(outgoing.reshape(ND, SLOTS, -1), 'dp', split_axis=0, conca...  20.1 us
    dot_general x11, matrix products, part_dots(): jnp.dot(tokens[:, at * KB:at * KB + w.shape[0]], w, preferred_element_typ...  19.8 us
    ppermute x15, waiting for transfers between devices, from_z(): return lax.ppermute(value, 'dp', pairs)  18.9 us
    ppermute x10, waiting for transfers between devices, from_x(): return lax.ppermute(value, 'dp', pairs)  13.8 us
    ppermute x10, starting transfers between devices, from_x(): return lax.ppermute(value, 'dp', pairs)  11.7 us
    pallas_call x3, Pallas kernels, join(): pl.pallas_call(lambda *refs: join_kernel(columns, *refs), out_shape=jax.S...  6.57 us
  transfers between devices with their start and end apart: 27, of which 13 were waited for; matrix products, arithmetic and copies ran while one was open for 15% of the time, Pallas kernels for 5%

profile of v2, /device:TPU:1, one launch (start us, length us, event | category | flops | bytes accessed | tf_op | source)
XLA Modules:
  0.0 177.4 jit_solution(1882728694198275001)
XLA Ops:
  6.5 2.8 %shard_map.73 = bf16[64,8320]{1,0:T(8,128)(2,1)} custom-call(bf16[64,8192]{1,0:T(8,128)(2,1)} %bitcast.20, f32[1,8192]{1,0:T(1,128)} %bitcast.21, s32[1,64]{1,0:T(1,128)} %target_ref.1), custom_call_target="tpu_custom_call" | custom-call | tf_op jit(solution)/shard_map/pallas_call | solution.py:62
  9.4 3.4 %collective-permute-start.2 = (bf16[256,768]{1,0:T(8,128)(2,1)S(1)}, bf16[256,768]{1,0:T(8,128)(2,1)S(1)}, u32[]{:S(2)}, u32[]{:S(2)}) collective-permute-start(bf16[256,768]{1,0:T(8,128)(2,1)S(1)} %constant_dynamic-update-slice_fusion.refs_0_), channel_id=1, source_target_pairs={{64,0},{72,8},{80,16},{88,24},{96,32},{104,40},{112,48},{120,56},{... | collective-permute-start | bytes 1179656 | tf_op jit(solution)/shard_map/ppermute | solution.py:35
  12.8 5.6 %collective-permute-start = (bf16[256,512]{1,0:T(8,128)(2,1)S(1)}, bf16[256,512]{1,0:T(8,128)(2,1)S(1)}, u32[]{:S(2)}, u32[]{:S(2)}) collective-permute-start(bf16[256,512]{1,0:T(8,128)(2,1)S(1)} %copy-done.10), channel_id=1, source_target_pairs={{8,0},{16,8},{24,16},{32,24},{40,32},{48,40},{56,48},{0,56},{72,64... | collective-permute-start | bytes 786440 | tf_op jit(solution)/shard_map/ppermute | solution.py:30
  18.4 2.2 %collective-permute-done.2.refs_1_ = bf16[256,768]{1,0:T(8,128)(2,1)S(1)} collective-permute-done((bf16[256,768]{1,0:T(8,128)(2,1)S(1)}, bf16[256,768]{1,0:T(8,128)(2,1)S(1)}, u32[]{:S(2)}, u32[]{:S(2)}) %collective-permute-start.2) | collective-permute-done | bytes 393248 | tf_op jit(solution)/shard_map/ppermute | solution.py:35
  20.6 3.4 %collective-permute-start.5 = (bf16[256,768]{1,0:T(8,128)(2,1)S(1)}, bf16[256,768]{1,0:T(8,128)(2,1)S(1)}, u32[]{:S(2)}, u32[]{:S(2)}) collective-permute-start(bf16[256,768]{1,0:T(8,128)(2,1)S(1)} %collective-permute-done.2.refs_1_), channel_id=1, source_target_pairs={{64,0},{72,8},{80,16},{88,24},{96,32},{104,40},{112,48},{120,56},{... | collective-permute-start | bytes 1179656 | tf_op jit(solution)/shard_map/ppermute | solution.py:35
  24.0 2.2 %collective-permute-done.1.refs_1_ = bf16[256,512]{1,0:T(8,128)(2,1)S(1)} collective-permute-done((bf16[256,512]{1,0:T(8,128)(2,1)S(1)}, bf16[256,512]{1,0:T(8,128)(2,1)S(1)}, u32[]{:S(2)}, u32[]{:S(2)}) %collective-permute-start.1) | collective-permute-done | bytes 262176 | tf_op jit(solution)/shard_map/ppermute | solution.py:30
  26.2 3.5 %collective-permute-start.7 = (bf16[256,512]{1,0:T(8,128)(2,1)S(1)}, bf16[256,512]{1,0:T(8,128)(2,1)S(1)}, u32[]{:S(2)}, u32[]{:S(2)}) collective-permute-start(bf16[256,512]{1,0:T(8,128)(2,1)S(1)} %collective-permute-done.refs_0_), channel_id=1, source_target_pairs={{8,0},{16,8},{24,16},{32,24},{40,32},{48,40},{56,48},{0,56},{72,64... | collective-permute-start | bytes 786440 | tf_op jit(solution)/shard_map/ppermute | solution.py:30
  29.7 1.9 %shard_map.74 = bf16[512,512]{1,0:T(8,128)(2,1)} custom-call(bf16[256,512]{1,0:T(8,128)(2,1)} %copy-done.18, bf16[256,512]{1,0:T(8,128)(2,1)} %copy-done.19), custom_call_target="tpu_custom_call" | custom-call | tf_op jit(solution)/shard_map/pallas_call | solution.py:79
  31.6 1.9 %collective-permute-done.7.refs_0_ = bf16[256,512]{1,0:T(8,128)(2,1)S(1)} collective-permute-done((bf16[256,512]{1,0:T(8,128)(2,1)S(1)}, bf16[256,512]{1,0:T(8,128)(2,1)S(1)}, u32[]{:S(2)}, u32[]{:S(2)}) %collective-permute-start.7) | collective-permute-done | bytes 262176 | tf_op jit(solution)/shard_map/ppermute | solution.py:30
  33.5 3.2 %collective-permute-done.8.refs_1_ = bf16[256,512]{1,0:T(8,128)(2,1)S(1)} collective-permute-done((bf16[256,512]{1,0:T(8,128)(2,1)S(1)}, bf16[256,512]{1,0:T(8,128)(2,1)S(1)}, u32[]{:S(2)}, u32[]{:S(2)}) %collective-permute-start.8) | collective-permute-done | bytes 262176 | tf_op jit(solution)/shard_map/ppermute | solution.py:30
  36.7 0.4 collective-permute-start.9
  37.1 1.2 collective-permute-start.10
  38.3 1.7 collective-permute-start.4
  40.0 4.4 %collective-permute-done.6 = bf16[512,512]{1,0:T(8,128)(2,1)S(1)} collective-permute-done((bf16[512,512]{1,0:T(8,128)(2,1)}, bf16[512,512]{1,0:T(8,128)(2,1)S(1)}, u32[]{:S(2)}, u32[]{:S(2)}) %collective-permute-start.6) | collective-permute-done | bytes 524320 | tf_op jit(solution)/shard_map/ppermute | solution.py:35
  44.4 0.7 copy-done.17
  45.2 2.4 %collective-permute-start.11 = (bf16[256,512]{1,0:T(8,128)(2,1)S(1)}, bf16[256,512]{1,0:T(8,128)(2,1)}, u32[]{:S(2)}, u32[]{:S(2)}) collective-permute-start(bf16[256,512]{1,0:T(8,128)(2,1)S(1)} %collective-permute-done.9.refs_2_), channel_id=1, source_target_pairs={{8,0},{16,8},{24,16},{32,24},{40,32},{48,40},{56,48},{0,56},{72,64... | collective-permute-start | bytes 786440 | tf_op jit(solution)/shard_map/ppermute | solution.py:30
  47.6 2.3 %shard_map.75.refs_0_ = bf16[1024,256]{1,0:T(8,128)(2,1)} custom-call(bf16[256,768]{1,0:T(8,128)(2,1)} %copy-done.6, bf16[256,768]{1,0:T(8,128)(2,1)} %copy-done.8, bf16[256,768]{1,0:T(8,128)(2,1)} %copy-done.4, bf16[256,768]{1,0:T(8,128)(2,1)} %copy-done.7), custom_call_target="tpu_custom_call" | custom-call | tf_op jit(solution)/shard_map/pallas_call | solution.py:79
  49.9 1.0 collective-permute-done.11.refs_4_
  50.9 2.4 %shard_map.76 = bf16[1280,512]{1,0:T(8,128)(2,1)} custom-call(bf16[256,512]{1,0:T(8,128)(2,1)} %copy-done.14, bf16[256,512]{1,0:T(8,128)(2,1)} %copy-done.15, bf16[256,512]{1,0:T(8,128)(2,1)} %copy-done.16, bf16[256,512]{1,0:T(8,128)(2,1)} %copy-done.17, bf16[256,512]{1,0:T(8,128)(2,1)} %collective-permute-done.11.refs_4_), custom_call_target="tpu_custom_call" | custom-call | tf_op jit(solution)/shard_map/pallas_call | solution.py:79
  53.3 3.6 %collective-permute-start.12 = (bf16[1024,256]{1,0:T(8,128)(2,1)S(1)}, bf16[1024,256]{1,0:T(8,128)(2,1)S(1)}, u32[]{:S(2)}, u32[]{:S(2)}) collective-permute-start(bf16[1024,256]{1,0:T(8,128)(2,1)S(1)} %copy-done.1), channel_id=1, source_target_pairs={{8,0},{16,8},{24,16},{32,24},{40,32},{48,40},{56,48},{0,56},{72,64... | collective-permute-start | bytes 1572872 | tf_op jit(solution)/shard_map/ppermute | solution.py:30
  57.0 0.6 add.83
  57.7 0.3 collective-permute-start.19
  57.9 1.3 collective-permute-start.20
  59.2 1.9 %collective-permute-done.14 = bf16[512,512]{1,0:T(8,128)(2,1)} collective-permute-done((bf16[512,512]{1,0:T(8,128)(2,1)S(1)}, bf16[512,512]{1,0:T(8,128)(2,1)}, u32[]{:S(2)}, u32[]{:S(2)}) %collective-permute-start.14) | collective-permute-done | bytes 524320 | tf_op jit(solution)/shard_map/ppermute | solution.py:35
  61.1 2.9 %collective-permute-done.12.refs_1_ = bf16[1024,256]{1,0:T(8,128)(2,1)S(1)} collective-permute-done((bf16[1024,256]{1,0:T(8,128)(2,1)S(1)}, bf16[1024,256]{1,0:T(8,128)(2,1)S(1)}, u32[]{:S(2)}, u32[]{:S(2)}) %collective-permute-start.12) | collective-permute-done | bytes 524320 | tf_op jit(solution)/shard_map/ppermute | solution.py:30
  64.1 3.2 %collective-permute-done.13.refs_2_ = bf16[1024,256]{1,0:T(8,128)(2,1)S(1)} collective-permute-done((bf16[1024,256]{1,0:T(8,128)(2,1)S(1)}, bf16[1024,256]{1,0:T(8,128)(2,1)S(1)}, u32[]{:S(2)}, u32[]{:S(2)}) %collective-permute-start.13) | collective-permute-done | bytes 524320 | tf_op jit(solution)/shard_map/ppermute | solution.py:30
  67.3 0.3 collective-permute-start.15
  67.6 1.2 collective-permute-start.16
  68.8 2.6 %fusion.16 = f32[512,512]{1,0:T(8,128)} fusion(bf16[512,512]{1,0:T(8,128)(2,1)} %copy-done.13, bf16[512,8320]{1,0:T(8,128)(2,1)} %all-gather.2.cloned.1.call-done.tok_ref), kind=kOutput, calls=%fused_computation.22 | convolution fusion | flops 268435456 | bytes 2097152 | tf_op jit(solution)/shard_map/dot_general | solution.py:89
  71.4 2.3 %fusion.26 = f32[512,512]{1,0:T(8,128)} fusion(bf16[256,768]{1,0:T(8,128)(2,1)S(1)} %copy-done.9, bf16[512,8320]{1,0:T(8,128)(2,1)} %all-gather.2.cloned.1.call-done.tok_ref), kind=kOutput, calls=%fused_computation.34 | convolution fusion | flops 134217728 | bytes 1572864 | tf_op jit(solution)/shard_map/dot_general | solution.py:89
  73.7 2.2 %fusion.29 = f32[512,512]{1,0:T(8,128)} fusion(bf16[256,512]{1,0:T(8,128)(2,1)S(1)} %copy-done.11, bf16[512,8320]{1,0:T(8,128)(2,1)} %all-gather.2.cloned.1.call-done.tok_ref), kind=kOutput, calls=%fused_computation.37 | convolution fusion | flops 134217728 | bytes 1572864 | tf_op jit(solution)/shard_map/dot_general | solution.py:89
  75.9 1.1 fusion.20
  77.1 0.3 convert_reduce_fusion.1
  77.5 0.1 reduce_sum.12
  77.5 2.6 %fusion.5 = f32[512,512]{1,0:T(8,128)S(1)} fusion(f32[512,512]{1,0:T(8,128)} %fusion.16, f32[512,512]{1,0:T(8,128)} %fusion.26, f32[512,512]{1,0:T(8,128)} %fusion.29, bf16[512,512]{1,0:T(8,128)(2,1)S(1)} %copy-done.3, bf16[512,8320]{1,0:T(8,128)(2,1)} %all-gather.2.cloned.1.call-done.tok_ref), kind=kOutput, calls=%fused_computation.9 | convolution fusion | flops 269221888 | bytes 5242880 | tf_op jit(solution)/shard_map/dot_general | solution.py:89
  80.2 1.6 collective-permute-start.17
  81.7 1.3 fusion.21
  83.1 1.6 fusion.14
  84.7 0.4 fusion.7
  85.1 5.2 %collective-permute-done.20 = bf16[1280,512]{1,0:T(8,128)(2,1)} collective-permute-done((bf16[1280,512]{1,0:T(8,128)(2,1)}, bf16[1280,512]{1,0:T(8,128)(2,1)}, u32[]{:S(2)}, u32[]{:S(2)}) %collective-permute-start.20) | collective-permute-done | bytes 1310752 | tf_op jit(solution)/shard_map/ppermute | solution.py:35
  90.3 1.1 slice.74
  91.5 0.1 collective-permute-start.23
  91.6 1.1 slice.75
  92.7 1.5 collective-permute-start.24
  94.2 2.1 %shard_map.77.kv_ref = f32[512,256]{1,0:T(8,128)S(1)} custom-call(bf16[512,8320]{1,0:T(8,128)(2,1)S(1)} %copy-done, bf16[1024,256]{1,0:T(8,128)(2,1)S(1)} %copy-done.1, bf16[1024,256]{1,0:T(8,128)(2,1)S(1)} %collective-permute-done.12.refs_1_, bf16[1024,256]{1,0:T(8,128)(2,1)S(1)} %collective-permute-done.13.refs_2_, ...), custom_call_target="tpu_custom_call" | custom-call | tf_op jit(solution)/shard_map/pallas_call | solution.py:148
  96.4 2.3 %fusion.11 = f32[512,512]{1,0:T(8,128)S(1)} fusion(bf16[1280,512]{1,0:T(8,128)(2,1)} %collective-permute-done.20, bf16[512,8320]{1,0:T(8,128)(2,1)S(1)} %copy-done), kind=kOutput, calls=%fused_computation.17 | convolution fusion | flops 671088640 | bytes 3670016 | tf_op jit(solution)/shard_map/dot_general | solution.py:89
  98.7 0.1 collective-permute-start.21
  98.8 1.7 collective-permute-start.22
  100.6 0.9 fusion.8
  101.4 2.9 %collective-permute-done.21.ends0 = bf16[512,256]{1,0:T(8,128)(2,1)S(1)} collective-permute-done((bf16[512,256]{1,0:T(8,128)(2,1)S(1)}, bf16[512,256]{1,0:T(8,128)(2,1)S(1)}, u32[]{:S(2)}, u32[]{:S(2)}) %collective-permute-start.21) | collective-permute-done | bytes 262176 | tf_op jit(solution)/shard_map/ppermute | solution.py:30
  104.3 1.5 collective-permute-done.22.ends1
  105.8 2.2 %fusion.9 = f32[512,512]{1,0:T(8,128)S(1)} fusion(bf16[1280,512]{1,0:T(8,128)(2,1)} %collective-permute-done.19, bf16[512,8320]{1,0:T(8,128)(2,1)S(1)} %copy-done), kind=kOutput, calls=%fused_computation.15 | convolution fusion | flops 671088640 | bytes 3670016 | tf_op jit(solution)/shard_map/dot_general | solution.py:89
  108.0 1.5 fusion.3.q_ref
  109.5 4.6 %shard_map.78 = bf16[768,768]{1,0:T(8,128)(2,1)} custom-call(bf16[512,8320]{1,0:T(8,128)(2,1)S(1)} %copy-done, s32[1,512]{1,0:T(1,128)S(1)} %add_add_fusion.slot_ref, f32[512,512]{1,0:T(8,128)S(1)} %fusion.3.q_ref, f32[512,256]{1,0:T(8,128)S(1)} %shard_map.77.kv_ref, bf16[640,512]{1,0:T(8,128)(2,1)S(1)} %collective-permute-done.23.f2a, ...), custom_call_target="tpu_custom_call" | custom-call | tf_op jit(solution)/shard_map/pallas_call | solution.py:194
  114.2 4.5 %all-to-all-start = ((bf16[32,24,768]{2,1,0:T(8,128)(2,1)}), bf16[32,24,768]{2,1,0:T(8,128)(2,1)S(1)}, u32[]{:S(2)}, u32[]{:S(2)}) async-start(bf16[32,24,768]{2,1,0:T(8,128)(2,1)} %bitcast.2), calls=%async_computation | async-start | bytes 2359296 | tf_op jit(solution)/shard_map/all_to_all | solution.py:291
  118.7 0.1 copy.11.segq_ref
  118.9 1.0 fusion.33
  119.9 0.2 pad_maximum_fusion
  120.1 0.3 fusion.ahead_ref
  120.4 20.1 %all-to-all-done = bf16[32,24,768]{2,1,0:T(8,128)(2,1)S(1)} async-done(((bf16[32,24,768]{2,1,0:T(8,128)(2,1)}), bf16[32,24,768]{2,1,0:T(8,128)(2,1)S(1)}, u32[]{:S(2)}, u32[]{:S(2)}) %all-to-all-start) | async-done | bytes 1179680 | tf_op jit(solution)/shard_map/all_to_all | solution.py:291
  140.5 5.0 %shard_map.79 = bf16[512,512]{1,0:T(8,128)(2,1)S(1)} custom-call(bf16[768,768]{1,0:T(8,128)(2,1)S(1)} %bitcast.17, bf16[768,768]{1,0:T(8,128)(2,1)S(1)} %fusion.ahead_ref, s32[512,1]{1,0:T(8,128)S(1)} %copy.11.segq_ref, s32[1,640]{1,0:T(1,128)S(1)} %broadcast_in_dim.11.segk_ref, f32[512,128]{1,0:T(8,128)S(1)} %get-tuple-element.42.cos_ref, ...), custom_call_target="tpu_custom_call" | custom-call | tf_op jit(solution)/shard_map/pallas_call | solution.py:255
  145.5 23.7 %all_to_all.21 = bf16[8,64,512]{2,1,0:T(8,128)(2,1)S(1)} all-to-all(bf16[8,64,512]{2,1,0:T(8,128)(2,1)S(1)} %bitcast.18), channel_id=1, replica_groups=mesh['dp'=32,'seq'=8] {'seq'}, dimensions={0} | all-to-all | bytes 1048576 | tf_op jit(solution)/shard_map/all_to_all | solution.py:298
  169.2 0.3 copy.12
  169.5 1.0 broadcast_in_dim.12
  (84 shorter events, 0.5 us)
Async XLA Ops:
  6.5 2.8 %copy-start.10 = (bf16[256,512]{1,0:T(8,128)(2,1)S(1)}, bf16[256,512]{1,0:T(8,128)(2,1)}, u32[]{:S(2)}) copy-start(bf16[256,512]{1,0:T(8,128)(2,1)} %param.11) | copy-start | bytes 786436
  6.5 2.8 %copy-start.20 = (bf16[256,128]{1,0:T(8,128)(2,1)S(1)}, bf16[256,128]{1,0:T(8,128)(2,1)}, u32[]{:S(2)}) copy-start(bf16[256,128]{1,0:T(8,128)(2,1)} %param.12) | copy-start | bytes 196612
  6.5 2.9 %copy-start.21 = (bf16[256,128]{1,0:T(8,128)(2,1)S(1)}, bf16[256,128]{1,0:T(8,128)(2,1)}, u32[]{:S(2)}) copy-start(bf16[256,128]{1,0:T(8,128)(2,1)} %param.13) | copy-start | bytes 196612
  6.5 62.2 %all-gather.2.cloned.1.call-start = ((), (), s32[]{:S(2)}) async-start(), calls=%async_computation.2 | async-start | bytes 9584640 | tf_op jit(solution)/shard_map/all_gather | solution.py:286
  9.4 38.1 %copy-start.6 = (bf16[256,768]{1,0:T(8,128)(2,1)}, bf16[256,768]{1,0:T(8,128)(2,1)S(1)}, u32[]{:S(2)}) copy-start(bf16[256,768]{1,0:T(8,128)(2,1)S(1)} %constant_dynamic-update-slice_fusion.refs_0_) | copy-start | bytes 1179652
  9.4 11.2 %collective-permute-start.2 = (bf16[256,768]{1,0:T(8,128)(2,1)S(1)}, bf16[256,768]{1,0:T(8,128)(2,1)S(1)}, u32[]{:S(2)}, u32[]{:S(2)}) collective-permute-start(bf16[256,768]{1,0:T(8,128)(2,1)S(1)} %constant_dynamic-update-slice_fusion.refs_0_), channel_id=1, source_target_pairs={{64,0},{72,8},{80,16},{88,24},{96,32},{104,40},{112,48},{120,56},{... | collective-permute-start | bytes 1179656 | tf_op jit(solution)/shard_map/ppermute | solution.py:35
  12.8 13.4 %collective-permute-start.3 = (bf16[256,768]{1,0:T(8,128)(2,1)S(1)}, bf16[256,768]{1,0:T(8,128)(2,1)S(1)}, u32[]{:S(2)}, u32[]{:S(2)}) collective-permute-start(bf16[256,768]{1,0:T(8,128)(2,1)S(1)} %constant_dynamic-update-slice_fusion.refs_0_), channel_id=1, source_target_pairs={{192,0},{200,8},{208,16},{216,24},{224,32},{232,40},{240,48},{248,... | collective-permute-start | bytes 1179656 | tf_op jit(solution)/shard_map/ppermute | solution.py:35
  12.8 11.2 %collective-permute-start = (bf16[256,512]{1,0:T(8,128)(2,1)S(1)}, bf16[256,512]{1,0:T(8,128)(2,1)S(1)}, u32[]{:S(2)}, u32[]{:S(2)}) collective-permute-start(bf16[256,512]{1,0:T(8,128)(2,1)S(1)} %copy-done.10), channel_id=1, source_target_pairs={{8,0},{16,8},{24,16},{32,24},{40,32},{48,40},{56,48},{0,56},{72,64... | collective-permute-start | bytes 786440 | tf_op jit(solution)/shard_map/ppermute | solution.py:30
  18.4 7.8 %collective-permute-start.1 = (bf16[256,512]{1,0:T(8,128)(2,1)S(1)}, bf16[256,512]{1,0:T(8,128)(2,1)S(1)}, u32[]{:S(2)}, u32[]{:S(2)}) collective-permute-start(bf16[256,512]{1,0:T(8,128)(2,1)S(1)} %copy-done.10), channel_id=1, source_target_pairs={{56,0},{0,8},{8,16},{16,24},{24,32},{32,40},{40,48},{48,56},{120,6... | collective-permute-start | bytes 786440 | tf_op jit(solution)/shard_map/ppermute | solution.py:30
  20.6 27.0 %copy-start.8 = (bf16[256,768]{1,0:T(8,128)(2,1)}, bf16[256,768]{1,0:T(8,128)(2,1)S(1)}, u32[]{:S(2)}) copy-start(bf16[256,768]{1,0:T(8,128)(2,1)S(1)} %collective-permute-done.2.refs_1_) | copy-start | bytes 1179652
  20.6 16.1 %collective-permute-start.5 = (bf16[256,768]{1,0:T(8,128)(2,1)S(1)}, bf16[256,768]{1,0:T(8,128)(2,1)S(1)}, u32[]{:S(2)}, u32[]{:S(2)}) collective-permute-start(bf16[256,768]{1,0:T(8,128)(2,1)S(1)} %collective-permute-done.2.refs_1_), channel_id=1, source_target_pairs={{64,0},{72,8},{80,16},{88,24},{96,32},{104,40},{112,48},{120,56},{... | collective-permute-start | bytes 1179656 | tf_op jit(solution)/shard_map/ppermute | solution.py:35
  24.0 5.7 %copy-start.18 = (bf16[256,512]{1,0:T(8,128)(2,1)}, bf16[256,512]{1,0:T(8,128)(2,1)S(1)}, u32[]{:S(2)}) copy-start(bf16[256,512]{1,0:T(8,128)(2,1)S(1)} %collective-permute-done.refs_0_) | copy-start | bytes 786436
  26.2 3.5 %copy-start.19 = (bf16[256,512]{1,0:T(8,128)(2,1)}, bf16[256,512]{1,0:T(8,128)(2,1)S(1)}, u32[]{:S(2)}) copy-start(bf16[256,512]{1,0:T(8,128)(2,1)S(1)} %collective-permute-done.1.refs_1_) | copy-start | bytes 786436
  26.2 21.4 %copy-start.7 = (bf16[256,768]{1,0:T(8,128)(2,1)}, bf16[256,768]{1,0:T(8,128)(2,1)S(1)}, u32[]{:S(2)}) copy-start(bf16[256,768]{1,0:T(8,128)(2,1)S(1)} %collective-permute-done.3.refs_3_) | copy-start | bytes 1179652
  26.2 7.3 %collective-permute-start.7 = (bf16[256,512]{1,0:T(8,128)(2,1)S(1)}, bf16[256,512]{1,0:T(8,128)(2,1)S(1)}, u32[]{:S(2)}, u32[]{:S(2)}) collective-permute-start(bf16[256,512]{1,0:T(8,128)(2,1)S(1)} %collective-permute-done.refs_0_), channel_id=1, source_target_pairs={{8,0},{16,8},{24,16},{32,24},{40,32},{48,40},{56,48},{0,56},{72,64... | collective-permute-start | bytes 786440 | tf_op jit(solution)/shard_map/ppermute | solution.py:30
  29.7 7.0 %collective-permute-start.8 = (bf16[256,512]{1,0:T(8,128)(2,1)S(1)}, bf16[256,512]{1,0:T(8,128)(2,1)S(1)}, u32[]{:S(2)}, u32[]{:S(2)}) collective-permute-start(bf16[256,512]{1,0:T(8,128)(2,1)S(1)} %collective-permute-done.1.refs_1_), channel_id=1, source_target_pairs={{56,0},{0,8},{8,16},{16,24},{24,32},{32,40},{40,48},{48,56},{120,6... | collective-permute-start | bytes 786440 | tf_op jit(solution)/shard_map/ppermute | solution.py:30
  31.6 12.8 %collective-permute-start.6 = (bf16[512,512]{1,0:T(8,128)(2,1)}, bf16[512,512]{1,0:T(8,128)(2,1)S(1)}, u32[]{:S(2)}, u32[]{:S(2)}) collective-permute-start(bf16[512,512]{1,0:T(8,128)(2,1)} %shard_map.74), channel_id=1, source_target_pairs={{192,0},{200,8},{208,16},{216,24},{224,32},{232,40},{240,48},{248,... | collective-permute-start | bytes 1572872 | tf_op jit(solution)/shard_map/ppermute | solution.py:35
  33.5 17.4 %copy-start.14 = (bf16[256,512]{1,0:T(8,128)(2,1)}, bf16[256,512]{1,0:T(8,128)(2,1)S(1)}, u32[]{:S(2)}) copy-start(bf16[256,512]{1,0:T(8,128)(2,1)S(1)} %collective-permute-done.7.refs_0_) | copy-start | bytes 786436
  36.7 14.1 %copy-start.15 = (bf16[256,512]{1,0:T(8,128)(2,1)}, bf16[256,512]{1,0:T(8,128)(2,1)S(1)}, u32[]{:S(2)}) copy-start(bf16[256,512]{1,0:T(8,128)(2,1)S(1)} %collective-permute-done.8.refs_1_) | copy-start | bytes 786436
  36.7 10.8 %copy-start.4 = (bf16[256,768]{1,0:T(8,128)(2,1)}, bf16[256,768]{1,0:T(8,128)(2,1)S(1)}, u32[]{:S(2)}) copy-start(bf16[256,768]{1,0:T(8,128)(2,1)S(1)} %collective-permute-done.5.refs_2_) | copy-start | bytes 1179652
  36.7 7.7 %collective-permute-start.9 = (bf16[256,512]{1,0:T(8,128)(2,1)S(1)}, bf16[256,512]{1,0:T(8,128)(2,1)S(1)}, u32[]{:S(2)}, u32[]{:S(2)}) collective-permute-start(bf16[256,512]{1,0:T(8,128)(2,1)S(1)} %collective-permute-done.7.refs_0_), channel_id=1, source_target_pairs={{8,0},{16,8},{24,16},{32,24},{40,32},{48,40},{56,48},{0,56},{72,64... | collective-permute-start | bytes 786440 | tf_op jit(solution)/shard_map/ppermute | solution.py:30
  37.1 7.3 %collective-permute-start.10 = (bf16[256,512]{1,0:T(8,128)(2,1)S(1)}, bf16[256,512]{1,0:T(8,128)(2,1)S(1)}, u32[]{:S(2)}, u32[]{:S(2)}) collective-permute-start(bf16[256,512]{1,0:T(8,128)(2,1)S(1)} %collective-permute-done.8.refs_1_), channel_id=1, source_target_pairs={{56,0},{0,8},{8,16},{16,24},{24,32},{32,40},{40,48},{48,56},{120,6... | collective-permute-start | bytes 786440 | tf_op jit(solution)/shard_map/ppermute | solution.py:30
  38.3 15.0 %collective-permute-start.4 = (bf16[512,512]{1,0:T(8,128)(2,1)}, bf16[512,512]{1,0:T(8,128)(2,1)S(1)}, u32[]{:S(2)}, u32[]{:S(2)}) collective-permute-start(bf16[512,512]{1,0:T(8,128)(2,1)} %shard_map.74), channel_id=1, source_target_pairs={{64,0},{72,8},{80,16},{88,24},{96,32},{104,40},{112,48},{120,56},{... | collective-permute-start | bytes 1572872 | tf_op jit(solution)/shard_map/ppermute | solution.py:35
  44.4 12.5 %copy-start.12 = (bf16[512,512]{1,0:T(8,128)(2,1)}, bf16[512,512]{1,0:T(8,128)(2,1)S(1)}, u32[]{:S(2)}) copy-start(bf16[512,512]{1,0:T(8,128)(2,1)S(1)} %collective-permute-done.6) | copy-start | bytes 1572868
  44.4 6.4 %copy-start.16 = (bf16[256,512]{1,0:T(8,128)(2,1)}, bf16[256,512]{1,0:T(8,128)(2,1)S(1)}, u32[]{:S(2)}) copy-start(bf16[256,512]{1,0:T(8,128)(2,1)S(1)} %collective-permute-done.9.refs_2_) | copy-start | bytes 786436
  44.4 0.7 copy-start.17
  45.2 5.7 %collective-permute-start.11 = (bf16[256,512]{1,0:T(8,128)(2,1)S(1)}, bf16[256,512]{1,0:T(8,128)(2,1)}, u32[]{:S(2)}, u32[]{:S(2)}) collective-permute-start(bf16[256,512]{1,0:T(8,128)(2,1)S(1)} %collective-permute-done.9.refs_2_), channel_id=1, source_target_pairs={{8,0},{16,8},{24,16},{32,24},{40,32},{48,40},{56,48},{0,56},{72,64... | collective-permute-start | bytes 786440 | tf_op jit(solution)/shard_map/ppermute | solution.py:30
  49.9 3.4 %copy-start.1 = (bf16[1024,256]{1,0:T(8,128)(2,1)S(1)}, bf16[1024,256]{1,0:T(8,128)(2,1)}, u32[]{:S(2)}) copy-start(bf16[1024,256]{1,0:T(8,128)(2,1)} %shard_map.75.refs_0_) | copy-start | bytes 1572868
  49.9 21.6 %copy-start.9 = (bf16[256,768]{1,0:T(8,128)(2,1)S(1)}, bf16[256,768]{1,0:T(8,128)(2,1)}, u32[]{:S(2)}) copy-start(bf16[256,768]{1,0:T(8,128)(2,1)} %copy-done.8) | copy-start | bytes 1179652
  49.9 11.3 %collective-permute-start.14 = (bf16[512,512]{1,0:T(8,128)(2,1)S(1)}, bf16[512,512]{1,0:T(8,128)(2,1)}, u32[]{:S(2)}, u32[]{:S(2)}) collective-permute-start(bf16[512,512]{1,0:T(8,128)(2,1)S(1)} %collective-permute-done.6), channel_id=1, source_target_pairs={{192,0},{200,8},{208,16},{216,24},{224,32},{232,40},{240,48},{248,... | collective-permute-start | bytes 1572872 | tf_op jit(solution)/shard_map/ppermute | solution.py:35
  53.3 14.0 %copy-start.13 = (bf16[512,512]{1,0:T(8,128)(2,1)}, bf16[512,512]{1,0:T(8,128)(2,1)S(1)}, u32[]{:S(2)}) copy-start(bf16[512,512]{1,0:T(8,128)(2,1)S(1)} %collective-permute-done.4) | copy-start | bytes 1572868
  53.3 10.8 %collective-permute-start.12 = (bf16[1024,256]{1,0:T(8,128)(2,1)S(1)}, bf16[1024,256]{1,0:T(8,128)(2,1)S(1)}, u32[]{:S(2)}, u32[]{:S(2)}) collective-permute-start(bf16[1024,256]{1,0:T(8,128)(2,1)S(1)} %copy-done.1), channel_id=1, source_target_pairs={{8,0},{16,8},{24,16},{32,24},{40,32},{48,40},{56,48},{0,56},{72,64... | collective-permute-start | bytes 1572872 | tf_op jit(solution)/shard_map/ppermute | solution.py:30
  56.9 10.4 %collective-permute-start.13 = (bf16[1024,256]{1,0:T(8,128)(2,1)S(1)}, bf16[1024,256]{1,0:T(8,128)(2,1)S(1)}, u32[]{:S(2)}, u32[]{:S(2)}) collective-permute-start(bf16[1024,256]{1,0:T(8,128)(2,1)S(1)} %copy-done.1), channel_id=1, source_target_pairs={{56,0},{0,8},{8,16},{16,24},{24,32},{32,40},{40,48},{48,56},{120,6... | collective-permute-start | bytes 1572872 | tf_op jit(solution)/shard_map/ppermute | solution.py:30
  57.6 19.9 %copy-start.3 = (bf16[512,512]{1,0:T(8,128)(2,1)S(1)}, bf16[512,512]{1,0:T(8,128)(2,1)}, u32[]{:S(2)}) copy-start(bf16[512,512]{1,0:T(8,128)(2,1)} %shard_map.74) | copy-start | bytes 1572868
  57.7 27.4 %collective-permute-start.19 = (bf16[1280,512]{1,0:T(8,128)(2,1)}, bf16[1280,512]{1,0:T(8,128)(2,1)}, u32[]{:S(2)}, u32[]{:S(2)}) collective-permute-start(bf16[1280,512]{1,0:T(8,128)(2,1)} %shard_map.76), channel_id=1, source_target_pairs={{64,0},{72,8},{80,16},{88,24},{96,32},{104,40},{112,48},{120,56},{... | collective-permute-start | bytes 3932168 | tf_op jit(solution)/shard_map/ppermute | solution.py:35
  57.9 32.4 %collective-permute-start.20 = (bf16[1280,512]{1,0:T(8,128)(2,1)}, bf16[1280,512]{1,0:T(8,128)(2,1)}, u32[]{:S(2)}, u32[]{:S(2)}) collective-permute-start(bf16[1280,512]{1,0:T(8,128)(2,1)} %shard_map.76), channel_id=1, source_target_pairs={{192,0},{200,8},{208,16},{216,24},{224,32},{232,40},{240,48},{248,... | collective-permute-start | bytes 3932168 | tf_op jit(solution)/shard_map/ppermute | solution.py:35
  67.3 12.8 %collective-permute-start.15 = (bf16[1024,256]{1,0:T(8,128)(2,1)S(1)}, bf16[1024,256]{1,0:T(8,128)(2,1)S(1)}, u32[]{:S(2)}, u32[]{:S(2)}) collective-permute-start(bf16[1024,256]{1,0:T(8,128)(2,1)S(1)} %collective-permute-done.12.refs_1_), channel_id=1, source_target_pairs={{8,0},{16,8},{24,16},{32,24},{40,32},{48,40},{56,48},{0,56},{72,64... | collective-permute-start | bytes 1572872 | tf_op jit(solution)/shard_map/ppermute | solution.py:30
  67.6 12.6 %collective-permute-start.16 = (bf16[1024,256]{1,0:T(8,128)(2,1)S(1)}, bf16[1024,256]{1,0:T(8,128)(2,1)S(1)}, u32[]{:S(2)}, u32[]{:S(2)}) collective-permute-start(bf16[1024,256]{1,0:T(8,128)(2,1)S(1)} %collective-permute-done.13.refs_2_), channel_id=1, source_target_pairs={{56,0},{0,8},{8,16},{16,24},{24,32},{32,40},{40,48},{48,56},{120,6... | collective-permute-start | bytes 1572872 | tf_op jit(solution)/shard_map/ppermute | solution.py:30
  68.8 4.9 %copy-start.11 = (bf16[256,512]{1,0:T(8,128)(2,1)S(1)}, bf16[256,512]{1,0:T(8,128)(2,1)}, u32[]{:S(2)}) copy-start(bf16[256,512]{1,0:T(8,128)(2,1)} %param.11) | copy-start | bytes 786436
  77.4 7.3 %copy-start.5 = (bf16[256,768]{1,0:T(8,128)(2,1)S(1)}, bf16[256,768]{1,0:T(8,128)(2,1)}, u32[]{:S(2)}) copy-start(bf16[256,768]{1,0:T(8,128)(2,1)} %copy-done.4) | copy-start | bytes 1179652
  77.5 7.2 %copy-start = (bf16[512,8320]{1,0:T(8,128)(2,1)S(1)}, bf16[512,8320]{1,0:T(8,128)(2,1)}, u32[]{:S(2)}) copy-start(bf16[512,8320]{1,0:T(8,128)(2,1)} %all-gather.2.cloned.1.call-done.tok_ref) | copy-start | bytes 25559044
  80.2 16.2 %collective-permute-start.17 = (bf16[1024,256]{1,0:T(8,128)(2,1)S(1)}, bf16[1024,256]{1,0:T(8,128)(2,1)S(1)}, u32[]{:S(2)}, u32[]{:S(2)}) collective-permute-start(bf16[1024,256]{1,0:T(8,128)(2,1)S(1)} %collective-permute-done.15.refs_3_), channel_id=1, source_target_pairs={{8,0},{16,8},{24,16},{32,24},{40,32},{48,40},{56,48},{0,56},{72,64... | collective-permute-start | bytes 1572872 | tf_op jit(solution)/shard_map/ppermute | solution.py:30
  81.7 14.7 %collective-permute-start.18 = (bf16[1024,256]{1,0:T(8,128)(2,1)S(1)}, bf16[1024,256]{1,0:T(8,128)(2,1)S(1)}, u32[]{:S(2)}, u32[]{:S(2)}) collective-permute-start(bf16[1024,256]{1,0:T(8,128)(2,1)S(1)} %collective-permute-done.16.refs_4_), channel_id=1, source_target_pairs={{56,0},{0,8},{8,16},{16,24},{24,32},{32,40},{40,48},{48,56},{120,6... | collective-permute-start | bytes 1572872 | tf_op jit(solution)/shard_map/ppermute | solution.py:30
  91.5 18.0 %collective-permute-start.23 = (bf16[640,512]{1,0:T(8,128)(2,1)S(1)}, bf16[640,512]{1,0:T(8,128)(2,1)S(1)}, u32[]{:S(2)}, u32[]{:S(2)}) collective-permute-start(bf16[640,512]{1,0:T(8,128)(2,1)S(1)} %slice.74), channel_id=1, source_target_pairs={{64,0},{72,8},{80,16},{88,24},{96,32},{104,40},{112,48},{120,56},{... | collective-permute-start | bytes 1966088 | tf_op jit(solution)/shard_map/ppermute | solution.py:35
  92.7 3.7 %copy-start.23 = (s32[1,512]{1,0:T(1,128)S(1)}, s32[1,512]{1,0:T(1,128)}, u32[]{:S(2)}) copy-start(s32[1,512]{1,0:T(1,128)} %add.83) | copy-start | bytes 6148
  92.7 16.8 %collective-permute-start.24 = (bf16[640,512]{1,0:T(8,128)(2,1)S(1)}, bf16[640,512]{1,0:T(8,128)(2,1)S(1)}, u32[]{:S(2)}, u32[]{:S(2)}) collective-permute-start(bf16[640,512]{1,0:T(8,128)(2,1)S(1)} %slice.75), channel_id=1, source_target_pairs={{192,0},{200,8},{208,16},{216,24},{224,32},{232,40},{240,48},{248,... | collective-permute-start | bytes 1966088 | tf_op jit(solution)/shard_map/ppermute | solution.py:35
  96.4 4.2 %copy-start.2 = (bf16[1280,512]{1,0:T(8,128)(2,1)S(1)}, bf16[1280,512]{1,0:T(8,128)(2,1)}, u32[]{:S(2)}) copy-start(bf16[1280,512]{1,0:T(8,128)(2,1)} %shard_map.76) | copy-start | bytes 3932164
  98.7 5.6 %collective-permute-start.21 = (bf16[512,256]{1,0:T(8,128)(2,1)S(1)}, bf16[512,256]{1,0:T(8,128)(2,1)S(1)}, u32[]{:S(2)}, u32[]{:S(2)}) collective-permute-start(bf16[512,256]{1,0:T(8,128)(2,1)S(1)} %slice.87), channel_id=1, source_target_pairs={{8,0},{16,8},{24,16},{32,24},{40,32},{48,40},{56,48},{0,56},{72,64... | collective-permute-start | bytes 786440 | tf_op jit(solution)/shard_map/ppermute | solution.py:30
  98.8 7.0 %collective-permute-start.22 = (bf16[512,256]{1,0:T(8,128)(2,1)S(1)}, bf16[512,256]{1,0:T(8,128)(2,1)S(1)}, u32[]{:S(2)}, u32[]{:S(2)}) collective-permute-start(bf16[512,256]{1,0:T(8,128)(2,1)S(1)} %slice.88), channel_id=1, source_target_pairs={{56,0},{0,8},{8,16},{16,24},{24,32},{32,40},{40,48},{48,56},{120,6... | collective-permute-start | bytes 786440 | tf_op jit(solution)/shard_map/ppermute | solution.py:30
  114.1 4.5 %copy-start.22 = (s32[1,512]{1,0:T(1,128)S(1)}, s32[1,512]{1,0:T(1,128)}, u32[]{:S(2)}) copy-start(s32[1,512]{1,0:T(1,128)} %param.9) | copy-start | bytes 6148
  114.2 26.4 %all-to-all-start = ((bf16[32,24,768]{2,1,0:T(8,128)(2,1)}), bf16[32,24,768]{2,1,0:T(8,128)(2,1)S(1)}, u32[]{:S(2)}, u32[]{:S(2)}) async-start(bf16[32,24,768]{2,1,0:T(8,128)(2,1)} %bitcast.2), calls=%async_computation | async-start | bytes 2359296 | tf_op jit(solution)/shard_map/all_to_all | solution.py:291
Sparse Core Ops, SparseCore 0:
  9.4 57.0 all-gather.1

commit v3 on v2

--- a/solution.py
+++ b/solution.py
@@ -185,7 +185,7 @@
             out_ref[pl.ds(low, BLOCK), c : c + HEAD] = part.astype(jnp.bfloat16)
         return carry
 
-    lax.fori_loop(0, out_ref.shape[0] // BLOCK, step, 0)
+    lax.fori_loop(0, out_ref.shape[0] // BLOCK, step, 0, unroll=2)
 
 
 def finish(tokens, slot, q_sum, kv_sum, q_late, kv_late):
@@ -241,7 +241,7 @@
             out_ref[block, h * HEAD : (h + 1) * HEAD] = context.astype(jnp.bfloat16)
         return carry
 
-    lax.fori_loop(0, length // BLOCK, step, 0)
+    lax.fori_loop(0, length // BLOCK, step, 0, unroll=2)
 
 
 def attention(arrived, seg, cosine, sine):

time: 178 us -> 177 us (level)
  no operation moved by 1% of the time
where the time goes in v3:
time: 177 us; the launch traced here: 176 us
  waiting for transfers between devices  52.8 us (30%)
  starting transfers between devices  37.7 us (21%)
  blocking collectives  23.7 us (13%)
  Pallas kernels  19.9 us (11%)
  matrix products  19.8 us (11%)
  between operations  13.8 us (8%)
  local copies, waits for them, and re-layouts  5.51 us (3%)
  other arithmetic  3.01 us (2%)
    all_to_all x1, blocking collectives, shards(): lax.all_to_all(context, 'seq', split_axis=0, concat_axis=1, tiled=True)  23.7 us
    ppermute x15, starting transfers between devices, from_z(): return lax.ppermute(value, 'dp', pairs)  21.5 us
    all_to_all x1, waiting for transfers between devices, shards(): lax.all_to_all(outgoing.reshape(ND, SLOTS, -1), 'dp', split_axis=0, conca...  20.1 us
    dot_general x11, matrix products, part_dots(): jnp.dot(tokens[:, at * KB:at * KB + w.shape[0]], w, preferred_element_typ...  19.8 us
    ppermute x15, waiting for transfers between devices, from_z(): return lax.ppermute(value, 'dp', pairs)  18.9 us
    ppermute x10, waiting for transfers between devices, from_x(): return lax.ppermute(value, 'dp', pairs)  13.8 us
    ppermute x10, starting transfers between devices, from_x(): return lax.ppermute(value, 'dp', pairs)  11.7 us
    pallas_call x3, Pallas kernels, join(): pl.pallas_call(lambda *refs: join_kernel(columns, *refs), out_shape=jax.S...  6.57 us
  transfers between devices with their start and end apart: 27, of which 13 were waited for; matrix products, arithmetic and copies ran while one was open for 15% of the time, Pallas kernels for 5%

profile of v3, /device:TPU:1, one launch (start us, length us, event | category | flops | bytes accessed | tf_op | source)
XLA Modules:
  0.0 176.3 jit_solution(10367071639523682145)
XLA Ops:
  6.5 2.8 %shard_map.73 = bf16[64,8320]{1,0:T(8,128)(2,1)} custom-call(bf16[64,8192]{1,0:T(8,128)(2,1)} %bitcast.20, f32[1,8192]{1,0:T(1,128)} %bitcast.21, s32[1,64]{1,0:T(1,128)} %target_ref.1), custom_call_target="tpu_custom_call" | custom-call | tf_op jit(solution)/shard_map/pallas_call | solution.py:62
  9.4 3.4 %collective-permute-start.2 = (bf16[256,768]{1,0:T(8,128)(2,1)S(1)}, bf16[256,768]{1,0:T(8,128)(2,1)S(1)}, u32[]{:S(2)}, u32[]{:S(2)}) collective-permute-start(bf16[256,768]{1,0:T(8,128)(2,1)S(1)} %constant_dynamic-update-slice_fusion.refs_0_), channel_id=1, source_target_pairs={{64,0},{72,8},{80,16},{88,24},{96,32},{104,40},{112,48},{120,56},{... | collective-permute-start | bytes 1179656 | tf_op jit(solution)/shard_map/ppermute | solution.py:35
  12.8 5.6 %collective-permute-start = (bf16[256,512]{1,0:T(8,128)(2,1)S(1)}, bf16[256,512]{1,0:T(8,128)(2,1)S(1)}, u32[]{:S(2)}, u32[]{:S(2)}) collective-permute-start(bf16[256,512]{1,0:T(8,128)(2,1)S(1)} %copy-done.10), channel_id=1, source_target_pairs={{8,0},{16,8},{24,16},{32,24},{40,32},{48,40},{56,48},{0,56},{72,64... | collective-permute-start | bytes 786440 | tf_op jit(solution)/shard_map/ppermute | solution.py:30
  18.4 2.2 %collective-permute-done.2.refs_1_ = bf16[256,768]{1,0:T(8,128)(2,1)S(1)} collective-permute-done((bf16[256,768]{1,0:T(8,128)(2,1)S(1)}, bf16[256,768]{1,0:T(8,128)(2,1)S(1)}, u32[]{:S(2)}, u32[]{:S(2)}) %collective-permute-start.2) | collective-permute-done | bytes 393248 | tf_op jit(solution)/shard_map/ppermute | solution.py:35
  20.6 3.4 %collective-permute-start.5 = (bf16[256,768]{1,0:T(8,128)(2,1)S(1)}, bf16[256,768]{1,0:T(8,128)(2,1)S(1)}, u32[]{:S(2)}, u32[]{:S(2)}) collective-permute-start(bf16[256,768]{1,0:T(8,128)(2,1)S(1)} %collective-permute-done.2.refs_1_), channel_id=1, source_target_pairs={{64,0},{72,8},{80,16},{88,24},{96,32},{104,40},{112,48},{120,56},{... | collective-permute-start | bytes 1179656 | tf_op jit(solution)/shard_map/ppermute | solution.py:35
  24.0 2.2 %collective-permute-done.1.refs_1_ = bf16[256,512]{1,0:T(8,128)(2,1)S(1)} collective-permute-done((bf16[256,512]{1,0:T(8,128)(2,1)S(1)}, bf16[256,512]{1,0:T(8,128)(2,1)S(1)}, u32[]{:S(2)}, u32[]{:S(2)}) %collective-permute-start.1) | collective-permute-done | bytes 262176 | tf_op jit(solution)/shard_map/ppermute | solution.py:30
  26.2 3.5 %collective-permute-start.7 = (bf16[256,512]{1,0:T(8,128)(2,1)S(1)}, bf16[256,512]{1,0:T(8,128)(2,1)S(1)}, u32[]{:S(2)}, u32[]{:S(2)}) collective-permute-start(bf16[256,512]{1,0:T(8,128)(2,1)S(1)} %collective-permute-done.refs_0_), channel_id=1, source_target_pairs={{8,0},{16,8},{24,16},{32,24},{40,32},{48,40},{56,48},{0,56},{72,64... | collective-permute-start | bytes 786440 | tf_op jit(solution)/shard_map/ppermute | solution.py:30
  29.7 1.9 %shard_map.74 = bf16[512,512]{1,0:T(8,128)(2,1)} custom-call(bf16[256,512]{1,0:T(8,128)(2,1)} %copy-done.18, bf16[256,512]{1,0:T(8,128)(2,1)} %copy-done.19), custom_call_target="tpu_custom_call" | custom-call | tf_op jit(solution)/shard_map/pallas_call | solution.py:79
  31.6 1.9 %collective-permute-done.7.refs_0_ = bf16[256,512]{1,0:T(8,128)(2,1)S(1)} collective-permute-done((bf16[256,512]{1,0:T(8,128)(2,1)S(1)}, bf16[256,512]{1,0:T(8,128)(2,1)S(1)}, u32[]{:S(2)}, u32[]{:S(2)}) %collective-permute-start.7) | collective-permute-done | bytes 262176 | tf_op jit(solution)/shard_map/ppermute | solution.py:30
  33.5 3.2 %collective-permute-done.8.refs_1_ = bf16[256,512]{1,0:T(8,128)(2,1)S(1)} collective-permute-done((bf16[256,512]{1,0:T(8,128)(2,1)S(1)}, bf16[256,512]{1,0:T(8,128)(2,1)S(1)}, u32[]{:S(2)}, u32[]{:S(2)}) %collective-permute-start.8) | collective-permute-done | bytes 262176 | tf_op jit(solution)/shard_map/ppermute | solution.py:30
  36.7 0.4 collective-permute-start.9
  37.1 1.2 collective-permute-start.10
  38.3 1.7 collective-permute-start.4
  40.0 4.4 %collective-permute-done.6 = bf16[512,512]{1,0:T(8,128)(2,1)S(1)} collective-permute-done((bf16[512,512]{1,0:T(8,128)(2,1)}, bf16[512,512]{1,0:T(8,128)(2,1)S(1)}, u32[]{:S(2)}, u32[]{:S(2)}) %collective-permute-start.6) | collective-permute-done | bytes 524320 | tf_op jit(solution)/shard_map/ppermute | solution.py:35
  44.4 0.7 copy-done.17
  45.2 2.4 %collective-permute-start.11 = (bf16[256,512]{1,0:T(8,128)(2,1)S(1)}, bf16[256,512]{1,0:T(8,128)(2,1)}, u32[]{:S(2)}, u32[]{:S(2)}) collective-permute-start(bf16[256,512]{1,0:T(8,128)(2,1)S(1)} %collective-permute-done.9.refs_2_), channel_id=1, source_target_pairs={{8,0},{16,8},{24,16},{32,24},{40,32},{48,40},{56,48},{0,56},{72,64... | collective-permute-start | bytes 786440 | tf_op jit(solution)/shard_map/ppermute | solution.py:30
  47.6 2.3 %shard_map.75.refs_0_ = bf16[1024,256]{1,0:T(8,128)(2,1)} custom-call(bf16[256,768]{1,0:T(8,128)(2,1)} %copy-done.6, bf16[256,768]{1,0:T(8,128)(2,1)} %copy-done.8, bf16[256,768]{1,0:T(8,128)(2,1)} %copy-done.4, bf16[256,768]{1,0:T(8,128)(2,1)} %copy-done.7), custom_call_target="tpu_custom_call" | custom-call | tf_op jit(solution)/shard_map/pallas_call | solution.py:79
  49.9 1.0 collective-permute-done.11.refs_4_
  50.9 2.4 %shard_map.76 = bf16[1280,512]{1,0:T(8,128)(2,1)} custom-call(bf16[256,512]{1,0:T(8,128)(2,1)} %copy-done.14, bf16[256,512]{1,0:T(8,128)(2,1)} %copy-done.15, bf16[256,512]{1,0:T(8,128)(2,1)} %copy-done.16, bf16[256,512]{1,0:T(8,128)(2,1)} %copy-done.17, bf16[256,512]{1,0:T(8,128)(2,1)} %collective-permute-done.11.refs_4_), custom_call_target="tpu_custom_call" | custom-call | tf_op jit(solution)/shard_map/pallas_call | solution.py:79
  53.3 3.6 %collective-permute-start.12 = (bf16[1024,256]{1,0:T(8,128)(2,1)S(1)}, bf16[1024,256]{1,0:T(8,128)(2,1)S(1)}, u32[]{:S(2)}, u32[]{:S(2)}) collective-permute-start(bf16[1024,256]{1,0:T(8,128)(2,1)S(1)} %copy-done.1), channel_id=1, source_target_pairs={{8,0},{16,8},{24,16},{32,24},{40,32},{48,40},{56,48},{0,56},{72,64... | collective-permute-start | bytes 1572872 | tf_op jit(solution)/shard_map/ppermute | solution.py:30
  57.0 0.6 add.83
  57.7 0.3 collective-permute-start.19
  57.9 1.3 collective-permute-start.20
  59.2 1.9 %collective-permute-done.14 = bf16[512,512]{1,0:T(8,128)(2,1)} collective-permute-done((bf16[512,512]{1,0:T(8,128)(2,1)S(1)}, bf16[512,512]{1,0:T(8,128)(2,1)}, u32[]{:S(2)}, u32[]{:S(2)}) %collective-permute-start.14) | collective-permute-done | bytes 524320 | tf_op jit(solution)/shard_map/ppermute | solution.py:35
  61.1 2.9 %collective-permute-done.12.refs_1_ = bf16[1024,256]{1,0:T(8,128)(2,1)S(1)} collective-permute-done((bf16[1024,256]{1,0:T(8,128)(2,1)S(1)}, bf16[1024,256]{1,0:T(8,128)(2,1)S(1)}, u32[]{:S(2)}, u32[]{:S(2)}) %collective-permute-start.12) | collective-permute-done | bytes 524320 | tf_op jit(solution)/shard_map/ppermute | solution.py:30
  64.1 3.2 %collective-permute-done.13.refs_2_ = bf16[1024,256]{1,0:T(8,128)(2,1)S(1)} collective-permute-done((bf16[1024,256]{1,0:T(8,128)(2,1)S(1)}, bf16[1024,256]{1,0:T(8,128)(2,1)S(1)}, u32[]{:S(2)}, u32[]{:S(2)}) %collective-permute-start.13) | collective-permute-done | bytes 524320 | tf_op jit(solution)/shard_map/ppermute | solution.py:30
  67.3 0.3 collective-permute-start.15
  67.6 1.2 collective-permute-start.16
  68.8 2.6 %fusion.16 = f32[512,512]{1,0:T(8,128)} fusion(bf16[512,512]{1,0:T(8,128)(2,1)} %copy-done.13, bf16[512,8320]{1,0:T(8,128)(2,1)} %all-gather.2.cloned.1.call-done.tok_ref), kind=kOutput, calls=%fused_computation.22 | convolution fusion | flops 268435456 | bytes 2097152 | tf_op jit(solution)/shard_map/dot_general | solution.py:89
  71.4 2.3 %fusion.26 = f32[512,512]{1,0:T(8,128)} fusion(bf16[256,768]{1,0:T(8,128)(2,1)S(1)} %copy-done.9, bf16[512,8320]{1,0:T(8,128)(2,1)} %all-gather.2.cloned.1.call-done.tok_ref), kind=kOutput, calls=%fused_computation.34 | convolution fusion | flops 134217728 | bytes 1572864 | tf_op jit(solution)/shard_map/dot_general | solution.py:89
  73.7 2.2 %fusion.29 = f32[512,512]{1,0:T(8,128)} fusion(bf16[256,512]{1,0:T(8,128)(2,1)S(1)} %copy-done.11, bf16[512,8320]{1,0:T(8,128)(2,1)} %all-gather.2.cloned.1.call-done.tok_ref), kind=kOutput, calls=%fused_computation.37 | convolution fusion | flops 134217728 | bytes 1572864 | tf_op jit(solution)/shard_map/dot_general | solution.py:89
  75.9 1.1 fusion.20
  77.1 0.3 convert_reduce_fusion.1
  77.5 0.1 reduce_sum.12
  77.5 2.6 %fusion.5 = f32[512,512]{1,0:T(8,128)S(1)} fusion(f32[512,512]{1,0:T(8,128)} %fusion.16, f32[512,512]{1,0:T(8,128)} %fusion.26, f32[512,512]{1,0:T(8,128)} %fusion.29, bf16[512,512]{1,0:T(8,128)(2,1)S(1)} %copy-done.3, bf16[512,8320]{1,0:T(8,128)(2,1)} %all-gather.2.cloned.1.call-done.tok_ref), kind=kOutput, calls=%fused_computation.9 | convolution fusion | flops 269221888 | bytes 5242880 | tf_op jit(solution)/shard_map/dot_general | solution.py:89
  80.2 1.6 collective-permute-start.17
  81.7 1.3 fusion.21
  83.1 1.6 fusion.14
  84.7 0.4 fusion.7
  85.1 5.2 %collective-permute-done.20 = bf16[1280,512]{1,0:T(8,128)(2,1)} collective-permute-done((bf16[1280,512]{1,0:T(8,128)(2,1)}, bf16[1280,512]{1,0:T(8,128)(2,1)}, u32[]{:S(2)}, u32[]{:S(2)}) %collective-permute-start.20) | collective-permute-done | bytes 1310752 | tf_op jit(solution)/shard_map/ppermute | solution.py:35
  90.3 1.1 slice.74
  91.5 0.1 collective-permute-start.23
  91.6 1.1 slice.75
  92.7 1.5 collective-permute-start.24
  94.2 2.1 %shard_map.77.kv_ref = f32[512,256]{1,0:T(8,128)S(1)} custom-call(bf16[512,8320]{1,0:T(8,128)(2,1)S(1)} %copy-done, bf16[1024,256]{1,0:T(8,128)(2,1)S(1)} %copy-done.1, bf16[1024,256]{1,0:T(8,128)(2,1)S(1)} %collective-permute-done.12.refs_1_, bf16[1024,256]{1,0:T(8,128)(2,1)S(1)} %collective-permute-done.13.refs_2_, ...), custom_call_target="tpu_custom_call" | custom-call | tf_op jit(solution)/shard_map/pallas_call | solution.py:148
  96.4 2.3 %fusion.11 = f32[512,512]{1,0:T(8,128)S(1)} fusion(bf16[1280,512]{1,0:T(8,128)(2,1)} %collective-permute-done.20, bf16[512,8320]{1,0:T(8,128)(2,1)S(1)} %copy-done), kind=kOutput, calls=%fused_computation.17 | convolution fusion | flops 671088640 | bytes 3670016 | tf_op jit(solution)/shard_map/dot_general | solution.py:89
  98.7 0.1 collective-permute-start.21
  98.8 1.7 collective-permute-start.22
  100.6 0.9 fusion.8
  101.4 2.9 %collective-permute-done.21.ends0 = bf16[512,256]{1,0:T(8,128)(2,1)S(1)} collective-permute-done((bf16[512,256]{1,0:T(8,128)(2,1)S(1)}, bf16[512,256]{1,0:T(8,128)(2,1)S(1)}, u32[]{:S(2)}, u32[]{:S(2)}) %collective-permute-start.21) | collective-permute-done | bytes 262176 | tf_op jit(solution)/shard_map/ppermute | solution.py:30
  104.3 1.5 collective-permute-done.22.ends1
  105.8 2.2 %fusion.9 = f32[512,512]{1,0:T(8,128)S(1)} fusion(bf16[1280,512]{1,0:T(8,128)(2,1)} %collective-permute-done.19, bf16[512,8320]{1,0:T(8,128)(2,1)S(1)} %copy-done), kind=kOutput, calls=%fused_computation.15 | convolution fusion | flops 671088640 | bytes 3670016 | tf_op jit(solution)/shard_map/dot_general | solution.py:89
  108.0 1.5 fusion.3.q_ref
  109.5 4.2 %shard_map.78 = bf16[768,768]{1,0:T(8,128)(2,1)} custom-call(bf16[512,8320]{1,0:T(8,128)(2,1)S(1)} %copy-done, s32[1,512]{1,0:T(1,128)S(1)} %add_add_fusion.slot_ref, f32[512,512]{1,0:T(8,128)S(1)} %fusion.3.q_ref, f32[512,256]{1,0:T(8,128)S(1)} %shard_map.77.kv_ref, bf16[640,512]{1,0:T(8,128)(2,1)S(1)} %collective-permute-done.23.f2a, ...), custom_call_target="tpu_custom_call" | custom-call | tf_op jit(solution)/shard_map/pallas_call | solution.py:194
  113.7 4.5 %all-to-all-start = ((bf16[32,24,768]{2,1,0:T(8,128)(2,1)}), bf16[32,24,768]{2,1,0:T(8,128)(2,1)S(1)}, u32[]{:S(2)}, u32[]{:S(2)}) async-start(bf16[32,24,768]{2,1,0:T(8,128)(2,1)} %bitcast.2), calls=%async_computation | async-start | bytes 2359296 | tf_op jit(solution)/shard_map/all_to_all | solution.py:291
  118.2 0.1 copy.11.segq_ref
  118.4 1.0 fusion.33
  119.4 0.2 pad_maximum_fusion
  119.6 0.3 fusion.ahead_ref
  120.0 20.1 %all-to-all-done = bf16[32,24,768]{2,1,0:T(8,128)(2,1)S(1)} async-done(((bf16[32,24,768]{2,1,0:T(8,128)(2,1)}), bf16[32,24,768]{2,1,0:T(8,128)(2,1)S(1)}, u32[]{:S(2)}, u32[]{:S(2)}) %all-to-all-start) | async-done | bytes 1179680 | tf_op jit(solution)/shard_map/all_to_all | solution.py:291
  140.1 4.3 %shard_map.79 = bf16[512,512]{1,0:T(8,128)(2,1)S(1)} custom-call(bf16[768,768]{1,0:T(8,128)(2,1)S(1)} %bitcast.17, bf16[768,768]{1,0:T(8,128)(2,1)S(1)} %fusion.ahead_ref, s32[512,1]{1,0:T(8,128)S(1)} %copy.11.segq_ref, s32[1,640]{1,0:T(1,128)S(1)} %broadcast_in_dim.11.segk_ref, f32[512,128]{1,0:T(8,128)S(1)} %get-tuple-element.42.cos_ref, ...), custom_call_target="tpu_custom_call" | custom-call | tf_op jit(solution)/shard_map/pallas_call | solution.py:255
  144.4 23.7 %all_to_all.21 = bf16[8,64,512]{2,1,0:T(8,128)(2,1)S(1)} all-to-all(bf16[8,64,512]{2,1,0:T(8,128)(2,1)S(1)} %bitcast.18), channel_id=1, replica_groups=mesh['dp'=32,'seq'=8] {'seq'}, dimensions={0} | all-to-all | bytes 1048576 | tf_op jit(solution)/shard_map/all_to_all | solution.py:298
  168.1 0.3 copy.12
  168.4 1.0 broadcast_in_dim.12
  (84 shorter events, 0.5 us)
Async XLA Ops:
  6.5 2.8 %copy-start.10 = (bf16[256,512]{1,0:T(8,128)(2,1)S(1)}, bf16[256,512]{1,0:T(8,128)(2,1)}, u32[]{:S(2)}) copy-start(bf16[256,512]{1,0:T(8,128)(2,1)} %param.11) | copy-start | bytes 786436
  6.5 2.8 %copy-start.20 = (bf16[256,128]{1,0:T(8,128)(2,1)S(1)}, bf16[256,128]{1,0:T(8,128)(2,1)}, u32[]{:S(2)}) copy-start(bf16[256,128]{1,0:T(8,128)(2,1)} %param.12) | copy-start | bytes 196612
  6.5 2.9 %copy-start.21 = (bf16[256,128]{1,0:T(8,128)(2,1)S(1)}, bf16[256,128]{1,0:T(8,128)(2,1)}, u32[]{:S(2)}) copy-start(bf16[256,128]{1,0:T(8,128)(2,1)} %param.13) | copy-start | bytes 196612
  6.5 62.2 %all-gather.2.cloned.1.call-start = ((), (), s32[]{:S(2)}) async-start(), calls=%async_computation.2 | async-start | bytes 9584640 | tf_op jit(solution)/shard_map/all_gather | solution.py:286
  9.4 38.1 %copy-start.6 = (bf16[256,768]{1,0:T(8,128)(2,1)}, bf16[256,768]{1,0:T(8,128)(2,1)S(1)}, u32[]{:S(2)}) copy-start(bf16[256,768]{1,0:T(8,128)(2,1)S(1)} %constant_dynamic-update-slice_fusion.refs_0_) | copy-start | bytes 1179652
  9.4 11.2 %collective-permute-start.2 = (bf16[256,768]{1,0:T(8,128)(2,1)S(1)}, bf16[256,768]{1,0:T(8,128)(2,1)S(1)}, u32[]{:S(2)}, u32[]{:S(2)}) collective-permute-start(bf16[256,768]{1,0:T(8,128)(2,1)S(1)} %constant_dynamic-update-slice_fusion.refs_0_), channel_id=1, source_target_pairs={{64,0},{72,8},{80,16},{88,24},{96,32},{104,40},{112,48},{120,56},{... | collective-permute-start | bytes 1179656 | tf_op jit(solution)/shard_map/ppermute | solution.py:35
  12.8 13.4 %collective-permute-start.3 = (bf16[256,768]{1,0:T(8,128)(2,1)S(1)}, bf16[256,768]{1,0:T(8,128)(2,1)S(1)}, u32[]{:S(2)}, u32[]{:S(2)}) collective-permute-start(bf16[256,768]{1,0:T(8,128)(2,1)S(1)} %constant_dynamic-update-slice_fusion.refs_0_), channel_id=1, source_target_pairs={{192,0},{200,8},{208,16},{216,24},{224,32},{232,40},{240,48},{248,... | collective-permute-start | bytes 1179656 | tf_op jit(solution)/shard_map/ppermute | solution.py:35
  12.8 11.2 %collective-permute-start = (bf16[256,512]{1,0:T(8,128)(2,1)S(1)}, bf16[256,512]{1,0:T(8,128)(2,1)S(1)}, u32[]{:S(2)}, u32[]{:S(2)}) collective-permute-start(bf16[256,512]{1,0:T(8,128)(2,1)S(1)} %copy-done.10), channel_id=1, source_target_pairs={{8,0},{16,8},{24,16},{32,24},{40,32},{48,40},{56,48},{0,56},{72,64... | collective-permute-start | bytes 786440 | tf_op jit(solution)/shard_map/ppermute | solution.py:30
  18.4 7.8 %collective-permute-start.1 = (bf16[256,512]{1,0:T(8,128)(2,1)S(1)}, bf16[256,512]{1,0:T(8,128)(2,1)S(1)}, u32[]{:S(2)}, u32[]{:S(2)}) collective-permute-start(bf16[256,512]{1,0:T(8,128)(2,1)S(1)} %copy-done.10), channel_id=1, source_target_pairs={{56,0},{0,8},{8,16},{16,24},{24,32},{32,40},{40,48},{48,56},{120,6... | collective-permute-start | bytes 786440 | tf_op jit(solution)/shard_map/ppermute | solution.py:30
  20.6 27.0 %copy-start.8 = (bf16[256,768]{1,0:T(8,128)(2,1)}, bf16[256,768]{1,0:T(8,128)(2,1)S(1)}, u32[]{:S(2)}) copy-start(bf16[256,768]{1,0:T(8,128)(2,1)S(1)} %collective-permute-done.2.refs_1_) | copy-start | bytes 1179652
  20.6 16.1 %collective-permute-start.5 = (bf16[256,768]{1,0:T(8,128)(2,1)S(1)}, bf16[256,768]{1,0:T(8,128)(2,1)S(1)}, u32[]{:S(2)}, u32[]{:S(2)}) collective-permute-start(bf16[256,768]{1,0:T(8,128)(2,1)S(1)} %collective-permute-done.2.refs_1_), channel_id=1, source_target_pairs={{64,0},{72,8},{80,16},{88,24},{96,32},{104,40},{112,48},{120,56},{... | collective-permute-start | bytes 1179656 | tf_op jit(solution)/shard_map/ppermute | solution.py:35
  24.0 5.7 %copy-start.18 = (bf16[256,512]{1,0:T(8,128)(2,1)}, bf16[256,512]{1,0:T(8,128)(2,1)S(1)}, u32[]{:S(2)}) copy-start(bf16[256,512]{1,0:T(8,128)(2,1)S(1)} %collective-permute-done.refs_0_) | copy-start | bytes 786436
  26.2 3.5 %copy-start.19 = (bf16[256,512]{1,0:T(8,128)(2,1)}, bf16[256,512]{1,0:T(8,128)(2,1)S(1)}, u32[]{:S(2)}) copy-start(bf16[256,512]{1,0:T(8,128)(2,1)S(1)} %collective-permute-done.1.refs_1_) | copy-start | bytes 786436
  26.2 21.4 %copy-start.7 = (bf16[256,768]{1,0:T(8,128)(2,1)}, bf16[256,768]{1,0:T(8,128)(2,1)S(1)}, u32[]{:S(2)}) copy-start(bf16[256,768]{1,0:T(8,128)(2,1)S(1)} %collective-permute-done.3.refs_3_) | copy-start | bytes 1179652
  26.2 7.3 %collective-permute-start.7 = (bf16[256,512]{1,0:T(8,128)(2,1)S(1)}, bf16[256,512]{1,0:T(8,128)(2,1)S(1)}, u32[]{:S(2)}, u32[]{:S(2)}) collective-permute-start(bf16[256,512]{1,0:T(8,128)(2,1)S(1)} %collective-permute-done.refs_0_), channel_id=1, source_target_pairs={{8,0},{16,8},{24,16},{32,24},{40,32},{48,40},{56,48},{0,56},{72,64... | collective-permute-start | bytes 786440 | tf_op jit(solution)/shard_map/ppermute | solution.py:30
  29.7 7.0 %collective-permute-start.8 = (bf16[256,512]{1,0:T(8,128)(2,1)S(1)}, bf16[256,512]{1,0:T(8,128)(2,1)S(1)}, u32[]{:S(2)}, u32[]{:S(2)}) collective-permute-start(bf16[256,512]{1,0:T(8,128)(2,1)S(1)} %collective-permute-done.1.refs_1_), channel_id=1, source_target_pairs={{56,0},{0,8},{8,16},{16,24},{24,32},{32,40},{40,48},{48,56},{120,6... | collective-permute-start | bytes 786440 | tf_op jit(solution)/shard_map/ppermute | solution.py:30
  31.6 12.8 %collective-permute-start.6 = (bf16[512,512]{1,0:T(8,128)(2,1)}, bf16[512,512]{1,0:T(8,128)(2,1)S(1)}, u32[]{:S(2)}, u32[]{:S(2)}) collective-permute-start(bf16[512,512]{1,0:T(8,128)(2,1)} %shard_map.74), channel_id=1, source_target_pairs={{192,0},{200,8},{208,16},{216,24},{224,32},{232,40},{240,48},{248,... | collective-permute-start | bytes 1572872 | tf_op jit(solution)/shard_map/ppermute | solution.py:35
  33.5 17.4 %copy-start.14 = (bf16[256,512]{1,0:T(8,128)(2,1)}, bf16[256,512]{1,0:T(8,128)(2,1)S(1)}, u32[]{:S(2)}) copy-start(bf16[256,512]{1,0:T(8,128)(2,1)S(1)} %collective-permute-done.7.refs_0_) | copy-start | bytes 786436
  36.7 14.1 %copy-start.15 = (bf16[256,512]{1,0:T(8,128)(2,1)}, bf16[256,512]{1,0:T(8,128)(2,1)S(1)}, u32[]{:S(2)}) copy-start(bf16[256,512]{1,0:T(8,128)(2,1)S(1)} %collective-permute-done.8.refs_1_) | copy-start | bytes 786436
  36.7 10.8 %copy-start.4 = (bf16[256,768]{1,0:T(8,128)(2,1)}, bf16[256,768]{1,0:T(8,128)(2,1)S(1)}, u32[]{:S(2)}) copy-start(bf16[256,768]{1,0:T(8,128)(2,1)S(1)} %collective-permute-done.5.refs_2_) | copy-start | bytes 1179652
  36.7 7.7 %collective-permute-start.9 = (bf16[256,512]{1,0:T(8,128)(2,1)S(1)}, bf16[256,512]{1,0:T(8,128)(2,1)S(1)}, u32[]{:S(2)}, u32[]{:S(2)}) collective-permute-start(bf16[256,512]{1,0:T(8,128)(2,1)S(1)} %collective-permute-done.7.refs_0_), channel_id=1, source_target_pairs={{8,0},{16,8},{24,16},{32,24},{40,32},{48,40},{56,48},{0,56},{72,64... | collective-permute-start | bytes 786440 | tf_op jit(solution)/shard_map/ppermute | solution.py:30
  37.1 7.3 %collective-permute-start.10 = (bf16[256,512]{1,0:T(8,128)(2,1)S(1)}, bf16[256,512]{1,0:T(8,128)(2,1)S(1)}, u32[]{:S(2)}, u32[]{:S(2)}) collective-permute-start(bf16[256,512]{1,0:T(8,128)(2,1)S(1)} %collective-permute-done.8.refs_1_), channel_id=1, source_target_pairs={{56,0},{0,8},{8,16},{16,24},{24,32},{32,40},{40,48},{48,56},{120,6... | collective-permute-start | bytes 786440 | tf_op jit(solution)/shard_map/ppermute | solution.py:30
  38.3 15.0 %collective-permute-start.4 = (bf16[512,512]{1,0:T(8,128)(2,1)}, bf16[512,512]{1,0:T(8,128)(2,1)S(1)}, u32[]{:S(2)}, u32[]{:S(2)}) collective-permute-start(bf16[512,512]{1,0:T(8,128)(2,1)} %shard_map.74), channel_id=1, source_target_pairs={{64,0},{72,8},{80,16},{88,24},{96,32},{104,40},{112,48},{120,56},{... | collective-permute-start | bytes 1572872 | tf_op jit(solution)/shard_map/ppermute | solution.py:35
  44.4 12.5 %copy-start.12 = (bf16[512,512]{1,0:T(8,128)(2,1)}, bf16[512,512]{1,0:T(8,128)(2,1)S(1)}, u32[]{:S(2)}) copy-start(bf16[512,512]{1,0:T(8,128)(2,1)S(1)} %collective-permute-done.6) | copy-start | bytes 1572868
  44.4 6.4 %copy-start.16 = (bf16[256,512]{1,0:T(8,128)(2,1)}, bf16[256,512]{1,0:T(8,128)(2,1)S(1)}, u32[]{:S(2)}) copy-start(bf16[256,512]{1,0:T(8,128)(2,1)S(1)} %collective-permute-done.9.refs_2_) | copy-start | bytes 786436
  44.4 0.7 copy-start.17
  45.2 5.7 %collective-permute-start.11 = (bf16[256,512]{1,0:T(8,128)(2,1)S(1)}, bf16[256,512]{1,0:T(8,128)(2,1)}, u32[]{:S(2)}, u32[]{:S(2)}) collective-permute-start(bf16[256,512]{1,0:T(8,128)(2,1)S(1)} %collective-permute-done.9.refs_2_), channel_id=1, source_target_pairs={{8,0},{16,8},{24,16},{32,24},{40,32},{48,40},{56,48},{0,56},{72,64... | collective-permute-start | bytes 786440 | tf_op jit(solution)/shard_map/ppermute | solution.py:30
  49.9 3.4 %copy-start.1 = (bf16[1024,256]{1,0:T(8,128)(2,1)S(1)}, bf16[1024,256]{1,0:T(8,128)(2,1)}, u32[]{:S(2)}) copy-start(bf16[1024,256]{1,0:T(8,128)(2,1)} %shard_map.75.refs_0_) | copy-start | bytes 1572868
  49.9 21.6 %copy-start.9 = (bf16[256,768]{1,0:T(8,128)(2,1)S(1)}, bf16[256,768]{1,0:T(8,128)(2,1)}, u32[]{:S(2)}) copy-start(bf16[256,768]{1,0:T(8,128)(2,1)} %copy-done.8) | copy-start | bytes 1179652
  49.9 11.3 %collective-permute-start.14 = (bf16[512,512]{1,0:T(8,128)(2,1)S(1)}, bf16[512,512]{1,0:T(8,128)(2,1)}, u32[]{:S(2)}, u32[]{:S(2)}) collective-permute-start(bf16[512,512]{1,0:T(8,128)(2,1)S(1)} %collective-permute-done.6), channel_id=1, source_target_pairs={{192,0},{200,8},{208,16},{216,24},{224,32},{232,40},{240,48},{248,... | collective-permute-start | bytes 1572872 | tf_op jit(solution)/shard_map/ppermute | solution.py:35
  53.3 14.0 %copy-start.13 = (bf16[512,512]{1,0:T(8,128)(2,1)}, bf16[512,512]{1,0:T(8,128)(2,1)S(1)}, u32[]{:S(2)}) copy-start(bf16[512,512]{1,0:T(8,128)(2,1)S(1)} %collective-permute-done.4) | copy-start | bytes 1572868
  53.3 10.8 %collective-permute-start.12 = (bf16[1024,256]{1,0:T(8,128)(2,1)S(1)}, bf16[1024,256]{1,0:T(8,128)(2,1)S(1)}, u32[]{:S(2)}, u32[]{:S(2)}) collective-permute-start(bf16[1024,256]{1,0:T(8,128)(2,1)S(1)} %copy-done.1), channel_id=1, source_target_pairs={{8,0},{16,8},{24,16},{32,24},{40,32},{48,40},{56,48},{0,56},{72,64... | collective-permute-start | bytes 1572872 | tf_op jit(solution)/shard_map/ppermute | solution.py:30
  56.9 10.4 %collective-permute-start.13 = (bf16[1024,256]{1,0:T(8,128)(2,1)S(1)}, bf16[1024,256]{1,0:T(8,128)(2,1)S(1)}, u32[]{:S(2)}, u32[]{:S(2)}) collective-permute-start(bf16[1024,256]{1,0:T(8,128)(2,1)S(1)} %copy-done.1), channel_id=1, source_target_pairs={{56,0},{0,8},{8,16},{16,24},{24,32},{32,40},{40,48},{48,56},{120,6... | collective-permute-start | bytes 1572872 | tf_op jit(solution)/shard_map/ppermute | solution.py:30
  57.6 19.9 %copy-start.3 = (bf16[512,512]{1,0:T(8,128)(2,1)S(1)}, bf16[512,512]{1,0:T(8,128)(2,1)}, u32[]{:S(2)}) copy-start(bf16[512,512]{1,0:T(8,128)(2,1)} %shard_map.74) | copy-start | bytes 1572868
  57.7 27.4 %collective-permute-start.19 = (bf16[1280,512]{1,0:T(8,128)(2,1)}, bf16[1280,512]{1,0:T(8,128)(2,1)}, u32[]{:S(2)}, u32[]{:S(2)}) collective-permute-start(bf16[1280,512]{1,0:T(8,128)(2,1)} %shard_map.76), channel_id=1, source_target_pairs={{64,0},{72,8},{80,16},{88,24},{96,32},{104,40},{112,48},{120,56},{... | collective-permute-start | bytes 3932168 | tf_op jit(solution)/shard_map/ppermute | solution.py:35
  57.9 32.4 %collective-permute-start.20 = (bf16[1280,512]{1,0:T(8,128)(2,1)}, bf16[1280,512]{1,0:T(8,128)(2,1)}, u32[]{:S(2)}, u32[]{:S(2)}) collective-permute-start(bf16[1280,512]{1,0:T(8,128)(2,1)} %shard_map.76), channel_id=1, source_target_pairs={{192,0},{200,8},{208,16},{216,24},{224,32},{232,40},{240,48},{248,... | collective-permute-start | bytes 3932168 | tf_op jit(solution)/shard_map/ppermute | solution.py:35
  67.3 12.8 %collective-permute-start.15 = (bf16[1024,256]{1,0:T(8,128)(2,1)S(1)}, bf16[1024,256]{1,0:T(8,128)(2,1)S(1)}, u32[]{:S(2)}, u32[]{:S(2)}) collective-permute-start(bf16[1024,256]{1,0:T(8,128)(2,1)S(1)} %collective-permute-done.12.refs_1_), channel_id=1, source_target_pairs={{8,0},{16,8},{24,16},{32,24},{40,32},{48,40},{56,48},{0,56},{72,64... | collective-permute-start | bytes 1572872 | tf_op jit(solution)/shard_map/ppermute | solution.py:30
  67.6 12.6 %collective-permute-start.16 = (bf16[1024,256]{1,0:T(8,128)(2,1)S(1)}, bf16[1024,256]{1,0:T(8,128)(2,1)S(1)}, u32[]{:S(2)}, u32[]{:S(2)}) collective-permute-start(bf16[1024,256]{1,0:T(8,128)(2,1)S(1)} %collective-permute-done.13.refs_2_), channel_id=1, source_target_pairs={{56,0},{0,8},{8,16},{16,24},{24,32},{32,40},{40,48},{48,56},{120,6... | collective-permute-start | bytes 1572872 | tf_op jit(solution)/shard_map/ppermute | solution.py:30
  68.8 4.9 %copy-start.11 = (bf16[256,512]{1,0:T(8,128)(2,1)S(1)}, bf16[256,512]{1,0:T(8,128)(2,1)}, u32[]{:S(2)}) copy-start(bf16[256,512]{1,0:T(8,128)(2,1)} %param.11) | copy-start | bytes 786436
  77.4 7.3 %copy-start.5 = (bf16[256,768]{1,0:T(8,128)(2,1)S(1)}, bf16[256,768]{1,0:T(8,128)(2,1)}, u32[]{:S(2)}) copy-start(bf16[256,768]{1,0:T(8,128)(2,1)} %copy-done.4) | copy-start | bytes 1179652
  77.5 7.2 %copy-start = (bf16[512,8320]{1,0:T(8,128)(2,1)S(1)}, bf16[512,8320]{1,0:T(8,128)(2,1)}, u32[]{:S(2)}) copy-start(bf16[512,8320]{1,0:T(8,128)(2,1)} %all-gather.2.cloned.1.call-done.tok_ref) | copy-start | bytes 25559044
  80.2 16.2 %collective-permute-start.17 = (bf16[1024,256]{1,0:T(8,128)(2,1)S(1)}, bf16[1024,256]{1,0:T(8,128)(2,1)S(1)}, u32[]{:S(2)}, u32[]{:S(2)}) collective-permute-start(bf16[1024,256]{1,0:T(8,128)(2,1)S(1)} %collective-permute-done.15.refs_3_), channel_id=1, source_target_pairs={{8,0},{16,8},{24,16},{32,24},{40,32},{48,40},{56,48},{0,56},{72,64... | collective-permute-start | bytes 1572872 | tf_op jit(solution)/shard_map/ppermute | solution.py:30
  81.7 14.7 %collective-permute-start.18 = (bf16[1024,256]{1,0:T(8,128)(2,1)S(1)}, bf16[1024,256]{1,0:T(8,128)(2,1)S(1)}, u32[]{:S(2)}, u32[]{:S(2)}) collective-permute-start(bf16[1024,256]{1,0:T(8,128)(2,1)S(1)} %collective-permute-done.16.refs_4_), channel_id=1, source_target_pairs={{56,0},{0,8},{8,16},{16,24},{24,32},{32,40},{40,48},{48,56},{120,6... | collective-permute-start | bytes 1572872 | tf_op jit(solution)/shard_map/ppermute | solution.py:30
  91.5 18.0 %collective-permute-start.23 = (bf16[640,512]{1,0:T(8,128)(2,1)S(1)}, bf16[640,512]{1,0:T(8,128)(2,1)S(1)}, u32[]{:S(2)}, u32[]{:S(2)}) collective-permute-start(bf16[640,512]{1,0:T(8,128)(2,1)S(1)} %slice.74), channel_id=1, source_target_pairs={{64,0},{72,8},{80,16},{88,24},{96,32},{104,40},{112,48},{120,56},{... | collective-permute-start | bytes 1966088 | tf_op jit(solution)/shard_map/ppermute | solution.py:35
  92.7 3.7 %copy-start.23 = (s32[1,512]{1,0:T(1,128)S(1)}, s32[1,512]{1,0:T(1,128)}, u32[]{:S(2)}) copy-start(s32[1,512]{1,0:T(1,128)} %add.83) | copy-start | bytes 6148
  92.7 16.8 %collective-permute-start.24 = (bf16[640,512]{1,0:T(8,128)(2,1)S(1)}, bf16[640,512]{1,0:T(8,128)(2,1)S(1)}, u32[]{:S(2)}, u32[]{:S(2)}) collective-permute-start(bf16[640,512]{1,0:T(8,128)(2,1)S(1)} %slice.75), channel_id=1, source_target_pairs={{192,0},{200,8},{208,16},{216,24},{224,32},{232,40},{240,48},{248,... | collective-permute-start | bytes 1966088 | tf_op jit(solution)/shard_map/ppermute | solution.py:35
  96.4 4.2 %copy-start.2 = (bf16[1280,512]{1,0:T(8,128)(2,1)S(1)}, bf16[1280,512]{1,0:T(8,128)(2,1)}, u32[]{:S(2)}) copy-start(bf16[1280,512]{1,0:T(8,128)(2,1)} %shard_map.76) | copy-start | bytes 3932164
  98.7 5.6 %collective-permute-start.21 = (bf16[512,256]{1,0:T(8,128)(2,1)S(1)}, bf16[512,256]{1,0:T(8,128)(2,1)S(1)}, u32[]{:S(2)}, u32[]{:S(2)}) collective-permute-start(bf16[512,256]{1,0:T(8,128)(2,1)S(1)} %slice.87), channel_id=1, source_target_pairs={{8,0},{16,8},{24,16},{32,24},{40,32},{48,40},{56,48},{0,56},{72,64... | collective-permute-start | bytes 786440 | tf_op jit(solution)/shard_map/ppermute | solution.py:30
  98.8 7.0 %collective-permute-start.22 = (bf16[512,256]{1,0:T(8,128)(2,1)S(1)}, bf16[512,256]{1,0:T(8,128)(2,1)S(1)}, u32[]{:S(2)}, u32[]{:S(2)}) collective-permute-start(bf16[512,256]{1,0:T(8,128)(2,1)S(1)} %slice.88), channel_id=1, source_target_pairs={{56,0},{0,8},{8,16},{16,24},{24,32},{32,40},{40,48},{48,56},{120,6... | collective-permute-start | bytes 786440 | tf_op jit(solution)/shard_map/ppermute | solution.py:30
  113.7 4.5 %copy-start.22 = (s32[1,512]{1,0:T(1,128)S(1)}, s32[1,512]{1,0:T(1,128)}, u32[]{:S(2)}) copy-start(s32[1,512]{1,0:T(1,128)} %param.9) | copy-start | bytes 6148
  113.7 26.4 %all-to-all-start = ((bf16[32,24,768]{2,1,0:T(8,128)(2,1)}), bf16[32,24,768]{2,1,0:T(8,128)(2,1)S(1)}, u32[]{:S(2)}, u32[]{:S(2)}) async-start(bf16[32,24,768]{2,1,0:T(8,128)(2,1)} %bitcast.2), calls=%async_computation | async-start | bytes 2359296 | tf_op jit(solution)/shard_map/all_to_all | solution.py:291
Sparse Core Ops, SparseCore 0:
  9.4 57.0 all-gather.1
